TPU v7x, 32 devices: a whole 2x2x4 slice. The times are simulated.
32 devices in a mesh: clips: 2 (over x), rows: 16 (over z, y, core).
Axes of the slice: x: 2, y: 2, z: 4, core: 2. Of those that a mesh axis runs over, the one named last changes fastest.
Arguments:
- state_start: bfloat16 [1024, 128, 128], P(('clips', 'rows')), parts along dimension 0, may hold values from -6 to 6
- features: bfloat16 [2, 1024, 128, 128], P(None, ('clips', 'rows')), parts along dimension 1, may hold values from -6 to 6
- row_moves: int32 [2, 2048], P(None, ('clips', 'rows')), parts along dimension 1, may hold values from -4 to 4, as said below
- col_moves: int32 [2, 2048], P(None, ('clips', 'rows')), parts along dimension 1, may hold values from -4 to 4
- merging_weight: bfloat16 [3, 3, 256, 128], replicated, may hold values from -0.125 to 0.125
- first_weight: bfloat16 [3, 3, 128, 128], replicated, may hold values from -0.1875 to 0.1875
- second_weight: bfloat16 [3, 3, 128, 128], replicated, may hold values from -0.1875 to 0.1875
Outputs:
- states: bfloat16 [2, 1024, 128, 128], P(None, ('clips', 'rows')), parts along dimension 1
There are 2 independent parts, one for each index of `clips`. A program takes and returns all parts, laid end to end along the dimension named above; an argument that names none is the same for every part. Nothing has to cross between parts.
Inputs may be any that keep to these rules, and one draw needn't show every extreme that they name: `row_moves`: every source block lies on the destination block's own device or on the device just above or below it; in each frame, among the 64 destination blocks of one device at most 32 take their source from the device above and at most 32 from the device below, and some device takes exactly 32 from the device above and some device exactly 32 from the one below.
All inputs are finite; a program needn't handle non-finite values.
Results may differ from a plain program's by a relative error of at most 0.009.
Values may be sent and summed in bfloat16 or wider, within the bound.
No kernel may reach another device: no remote copies, remote signals or barrier semaphores. Data moves between devices by JAX's collectives and lax.ppermute only.
A program may use at most 64 MiB of HBM per device.

v0:
```python
import functools

import jax
import jax.numpy as jnp
from jax import lax
from jax.experimental import pallas as pl
from jax.experimental.pallas import tpu as pltpu
from jax.sharding import PartitionSpec as P

BLK = 8
HALO = 3
VMEM = pl.BlockSpec(memory_space=pltpu.VMEM)
SMEM = pl.BlockSpec(memory_space=pltpu.SMEM)
ANY = pl.BlockSpec(memory_space=pl.ANY)
BF16 = jnp.bfloat16
F32 = jnp.float32


def shape_of(shape, dtype=BF16):
    return jax.ShapeDtypeStruct(shape, dtype)


def swap(x, axis, first):
    size = lax.axis_size(axis)
    pairs = []
    for i in range(first, size - 1, 2):
        pairs += [(i, i + 1), (i + 1, i)]
    return lax.ppermute(x, axis, pairs)


def swap_both(for_even, for_odd):
    far = swap(for_odd, "rows", 1)
    near = swap(for_even, "rows", 0)
    return near, far


def tables_kernel(band, across, slots, place_ref, row_ref, col_ref, feat_ref,
                  table_ref, near_ref, far_ref, near_edge, far_edge, sem):
    frames, blocks = row_ref.shape
    rows = feat_ref.shape[1]
    mine = place_ref[0]
    total = place_ref[1]
    odd = lax.rem(mine, 2)
    near_start = jnp.where(odd == 0, rows - HALO, 0)
    far_start = jnp.where(odd == 0, 0, rows - HALO)
    copies = [
        pltpu.make_async_copy(feat_ref.at[:, pl.ds(near_start, HALO)], near_edge, sem.at[0]),
        pltpu.make_async_copy(feat_ref.at[:, pl.ds(far_start, HALO)], far_edge, sem.at[1]),
    ]
    for copy in copies:
        copy.start()
    for frame in range(frames):
        def clear(slot, _):
            near_ref[frame, slot] = 0
            far_ref[frame, slot] = 0
            return 0

        lax.fori_loop(0, near_ref.shape[1], clear, 0)

        def visit(block, counts):
            near_count, far_count = counts
            row = lax.div(block, across)
            col = lax.rem(block, across)
            source = mine * band + row + row_ref[frame, block]
            source = jnp.clip(source, 0, total - 1) - mine * band
            column = jnp.clip(col + col_ref[frame, block], 0, across - 1)
            above = (source < 0).astype(jnp.int32)
            below = (source >= band).astype(jnp.int32)
            local = (source + (above - below) * band) * across + column
            is_near = jnp.where(odd == 0, below, above)
            is_far = jnp.where(odd == 0, above, below)
            near_ref[frame, near_count] = local
            far_ref[frame, far_count] = local
            place = jnp.where(is_near == 1, blocks + near_count, local)
            table_ref[frame, block] = jnp.where(is_far == 1, blocks + slots + far_count, place)
            return near_count + is_near, far_count + is_far

        lax.fori_loop(0, blocks, visit, (jnp.int32(0), jnp.int32(0)))
    for copy in copies:
        copy.wait()


def weights_kernel(merging_ref, first_ref, second_ref, feat_out, warp_out, first_out, second_out):
    chans = first_ref.shape[2]
    depth = 3 * chans
    for source, start, out in (
        (merging_ref, 0, feat_out),
        (merging_ref, chans, warp_out),
        (first_ref, 0, first_out),
        (second_ref, 0, second_out),
    ):
        width = source.shape[3]
        zero = jnp.zeros((chans, width), BF16)
        for a in range(4):
            for e in range(3):
                top = a * depth + e * chans
                for half in range(2):
                    tap = a - half
                    if 0 <= tap < 3:
                        value = source[tap, e, start:start + chans, :]
                    else:
                        value = zero
                    out[top:top + chans, half * width:(half + 1) * width] = value


def pack(pool_ref, near_list, far_list, frame, near_out, far_out):
    for slot in range(near_out.shape[0]):
        near_out[slot] = pool_ref[near_list[frame, slot]]
        far_out[slot] = pool_ref[far_list[frame, slot]]


def pack_kernel(frame, state_ref, near_list, far_list, pool_out, near_out, far_out):
    band, _, across = state_ref.shape[:3]
    for q in range(band):
        for r in range(BLK):
            pool_out[q * across:(q + 1) * across, r] = state_ref[q, r]
    pack(pool_out, near_list, far_list, frame, near_out, far_out)


def spread(out_ref, pair, half, value, cols):
    chans = value.shape[1]
    pairs = value.shape[0] // cols
    place = lax.broadcasted_iota(jnp.int32, (pairs, cols, chans), 1).reshape(value.shape)
    left = jnp.where(place == 0, 0.0, pltpu.roll(value, 1, 0))
    right = jnp.where(place == cols - 1, 0.0, pltpu.roll(value, value.shape[0] - 1, 0))
    for e, part in enumerate((left, value, right)):
        out_ref[pair:pair + pairs, half, :, e * chans:(e + 1) * chans] = (
            part.astype(BF16).reshape(pairs, cols, chans)
        )


def pair_dot(x_ref, w_ref, pair, pairs):
    cols, depth = x_ref.shape[2:]
    parts = [
        x_ref[pair + a // 2:pair + a // 2 + pairs, a % 2].reshape(pairs * cols, depth)
        for a in range(4)
    ]
    return jnp.dot(jnp.concatenate(parts, axis=1), w_ref[...], preferred_element_type=F32)


def chunks(total, size):
    return [(start, min(size, total - start)) for start in range(0, total, size)]


def load_rows(x_out, get_row, total, cols):
    for row in range(total):
        spread(x_out, row // 2, row % 2, get_row(row), cols)


def features_kernel(frame, place_ref, feat_ref, near_ref, far_ref, w_ref, out_ref, x_ref):
    rows, across, _, chans = feat_ref.shape[1:]
    cols = across * BLK
    even = lax.rem(place_ref[0], 2) == 0

    def get_row(row):
        row -= HALO
        if row < 0:
            value = jnp.where(even, far_ref[frame, row + HALO], near_ref[frame, row + HALO])
        elif row >= rows:
            value = jnp.where(even, near_ref[frame, row - rows], far_ref[frame, row - rows])
        else:
            value = feat_ref[frame, row]
        return value.astype(F32).reshape(cols, chans)

    load_rows(x_ref, get_row, rows + 2 * HALO, cols)
    for pair, pairs in chunks(rows // 2 + 2, 2):
        out_ref[pair:pair + pairs] = pair_dot(x_ref, w_ref, pair, pairs).reshape(
            pairs, cols, out_ref.shape[2]
        )


def assemble_kernel(frame, place_ref, table_ref, pool_ref, near_ref, far_ref,
                    warped_out, near_edge, far_edge, all_ref):
    rows, across = warped_out.shape[:2]
    blocks = pool_ref.shape[0]
    slots = near_ref.shape[0]
    all_ref[0:blocks] = pool_ref[...]
    all_ref[blocks:blocks + slots] = near_ref[...]
    all_ref[blocks + slots:blocks + 2 * slots] = far_ref[...]
    for block in range(blocks):
        q, p = divmod(block, across)
        warped_out[q * BLK:(q + 1) * BLK, p] = all_ref[table_ref[frame, block]]
    odd = lax.rem(place_ref[0], 2)
    near_start = jnp.where(odd == 0, rows - HALO, 0)
    far_start = jnp.where(odd == 0, 0, rows - HALO)
    near_edge[...] = warped_out[pl.ds(near_start, HALO)]
    far_edge[...] = warped_out[pl.ds(far_start, HALO)]


def main_kernel(frame, last, place_ref, part_ref, warped_ref, near_ref, far_ref, w1_ref, w2_ref, w3_ref,
                *refs):
    if last:
        _, out_ref, x_ref, m_ref, d_ref, state_ref, sem = refs
    else:
        near_list, far_list, out_ref, pool_out, near_out, far_out, x_ref, m_ref, d_ref, state_ref, sem = refs
    rows, across, _, chans = warped_ref.shape
    cols = across * BLK
    mine = place_ref[0]
    even = lax.rem(mine, 2) == 0
    has_above = mine > 0
    has_below = (mine + 1) * (rows // BLK) < place_ref[1]

    def get_row(row):
        row -= HALO
        if row < 0:
            value = jnp.where(even, far_ref[row + HALO], near_ref[row + HALO])
        elif row >= rows:
            value = jnp.where(even, near_ref[row - rows], far_ref[row - rows])
        else:
            value = warped_ref[row]
        return value.astype(F32).reshape(cols, chans)

    load_rows(x_ref, get_row, rows + 2 * HALO, cols)

    def keep(value, row):
        if row < 0:
            return jnp.where(has_above, value, 0.0)
        if row >= rows:
            return jnp.where(has_below, value, 0.0)
        return value

    step = 2
    for pair, pairs in chunks(rows // 2 + 2, step):
        raw = part_ref[pair:pair + pairs].reshape(pairs * cols, 2 * chans)
        raw = raw + pair_dot(x_ref, w1_ref, pair, pairs)
        value = jnp.maximum(raw, 0.1 * raw)
        for n in range(pairs):
            for half in range(2):
                one = value[n * cols:(n + 1) * cols, half * chans:(half + 1) * chans]
                spread(m_ref, pair + n, half, keep(one, 2 * (pair + n) + half - 2), cols)
    for pair, pairs in chunks(rows // 2 + 1, step):
        value = jnp.maximum(pair_dot(m_ref, w2_ref, pair, pairs), 0.0)
        for n in range(pairs):
            for half in range(2):
                one = value[n * cols:(n + 1) * cols, half * chans:(half + 1) * chans]
                spread(d_ref, pair + n, half, keep(one, 2 * (pair + n) + half - 1), cols)
    copies = []
    for pair, pairs in chunks(rows // 2, step):
        value = pair_dot(d_ref, w3_ref, pair, pairs)
        for n in range(pairs):
            for half in range(2):
                row = 2 * (pair + n) + half
                one = value[n * cols:(n + 1) * cols, half * chans:(half + 1) * chans]
                centre = m_ref[pair + n + 1, half, :, chans:2 * chans].astype(F32)
                done = (centre + one).reshape(across, BLK, chans).astype(BF16)
                state_ref[row] = done
                if not last:
                    q, r = divmod(row, BLK)
                    pool_out[q * across:(q + 1) * across, r] = done
        copy = pltpu.make_async_copy(
            state_ref.at[pl.ds(2 * pair, 2 * pairs)],
            out_ref.at[frame, pl.ds(2 * pair, 2 * pairs)],
            sem,
        )
        copy.start()
        copies.append(copy)
    if not last:
        pack(pool_out, near_list, far_list, frame + 1, near_out, far_out)
    pltpu.make_async_copy(state_ref, out_ref.at[frame], sem).wait()


def on_device(state_start, features, row_moves, col_moves, merging_weight, first_weight, second_weight):
    rows, cols, chans = state_start.shape
    frames = features.shape[0]
    band = rows // BLK
    across = cols // BLK
    blocks = band * across
    slots = blocks // 2
    list_len = slots + 8
    mine = lax.axis_index("rows")
    place = jnp.stack([mine, jnp.int32(band * lax.axis_size("rows"))]).astype(jnp.int32)
    state = state_start.reshape(band, BLK, across, BLK, chans)
    feats = features.reshape(frames, rows, across, BLK, chans)
    block_shape = (BLK, BLK, chans)
    edge_shape = (HALO, across, BLK, chans)

    table, near_list, far_list, near_feat, far_feat = pl.pallas_call(
        functools.partial(tables_kernel, band, across, slots),
        out_shape=[
            shape_of((frames, blocks), jnp.int32),
            shape_of((frames, list_len), jnp.int32),
            shape_of((frames, list_len), jnp.int32),
            shape_of((frames,) + edge_shape),
            shape_of((frames,) + edge_shape),
        ],
        in_specs=[SMEM, SMEM, SMEM, ANY],
        out_specs=[SMEM, SMEM, SMEM, VMEM, VMEM],
        scratch_shapes=[pltpu.SemaphoreType.DMA((2,))],
        name="tables",
    )(place, row_moves, col_moves, feats)
    near_list, far_list = swap_both(near_list, far_list)
    near_feat, far_feat = swap_both(near_feat, far_feat)

    pair_shape = shape_of((4 * 3 * chans, 2 * chans))
    w_feat, w_warp, w_first, w_second = pl.pallas_call(
        weights_kernel,
        out_shape=[pair_shape] * 4,
        in_specs=[VMEM] * 3,
        out_specs=[VMEM] * 4,
        name="weights",
    )(merging_weight, first_weight, second_weight)

    pool_shape = shape_of((blocks,) + block_shape)
    message = shape_of((slots,) + block_shape)
    pool, near_msg, far_msg = pl.pallas_call(
        functools.partial(pack_kernel, 0),
        out_shape=[pool_shape, message, message],
        in_specs=[VMEM, SMEM, SMEM],
        out_specs=[VMEM] * 3,
        name="pack",
    )(state, near_list, far_list)

    def wide(extra):
        return pltpu.VMEM((rows // 2 + extra, 2, cols, 3 * chans), BF16)

    def features_part(frame):
        return pl.pallas_call(
            functools.partial(features_kernel, frame),
            out_shape=shape_of((rows // 2 + 2, cols, 2 * chans), F32),
            in_specs=[SMEM] + [VMEM] * 4,
            out_specs=VMEM,
            scratch_shapes=[wide(3)],
            name="features",
        )(place, feats, near_feat, far_feat, w_feat)

    out = None
    out_shape = shape_of((frames, rows, across, BLK, chans))
    for frame in range(frames):
        last = frame == frames - 1
        part = features_part(frame)
        near_got, far_got = swap_both(near_msg, far_msg)
        warped, near_edge, far_edge = pl.pallas_call(
            functools.partial(assemble_kernel, frame),
            out_shape=[shape_of((rows, across, BLK, chans)), shape_of(edge_shape), shape_of(edge_shape)],
            in_specs=[SMEM, SMEM] + [VMEM] * 3,
            out_specs=[VMEM] * 3,
            scratch_shapes=[pltpu.VMEM((blocks + 2 * slots,) + block_shape, BF16)],
            name="assemble",
        )(place, table, pool, near_got, far_got)
        near_halo, far_halo = swap_both(near_edge, far_edge)
        scratch = [
            wide(3),
            wide(2),
            wide(1),
            pltpu.VMEM((rows, across, BLK, chans), BF16),
            pltpu.SemaphoreType.DMA,
        ]
        args = (place, part, warped, near_halo, far_halo, w_warp, w_first, w_second)
        kernel = functools.partial(main_kernel, frame, last)
        if last:
            out = pl.pallas_call(
                kernel,
                out_shape=out_shape,
                in_specs=[SMEM] + [VMEM] * 7 + [ANY],
                out_specs=ANY,
                input_output_aliases={8: 0},
                scratch_shapes=scratch,
                name="frame",
            )(*args, out)
        else:
            out, pool, near_msg, far_msg = pl.pallas_call(
                kernel,
                out_shape=[out_shape, pool_shape, message, message],
                in_specs=[SMEM] + [VMEM] * 7 + [SMEM] * 2,
                out_specs=[ANY] + [VMEM] * 3,
                scratch_shapes=scratch,
                name="frame",
            )(*args, near_list, far_list)
    return out.reshape(frames, rows, cols, chans)


def solution(mesh):
    in_specs = (
        P(("clips", "rows"), None, None),
        P(None, ("clips", "rows"), None, None),
        P(None, ("clips", "rows")),
        P(None, ("clips", "rows")),
        P(),
        P(),
        P(),
    )
    out_specs = P(None, ("clips", "rows"), None, None)
    return jax.shard_map(
        on_device, mesh=mesh, in_specs=in_specs, out_specs=out_specs, check_vma=False
    )
```

profile of v0, /device:TPU:1, one launch (start us, length us, event | category | flops | bytes accessed | tf_op | source)
XLA Modules:
  0.0 102.3 jit_solution(9011993431823526906)
XLA Ops:
  0.0 0.6 pad_add_fusion.place_ref
  0.6 5.0 %tables.1 = (s32[2,64]{1,0:T(2,128)}, s32[2,40]{1,0:T(2,128)}, s32[2,40]{1,0:T(2,128)}, bf16[2,3,16,8,128]{4,3,2,1,0:T(8,128)(2,1)}, bf16[2,3,16,8,128]{4,3,2,1,0:T(8,128)(2,1)}) custom-call(s32[2]{0:T(128)} %pad_add_fusion.place_ref, s32[2,64]{1,0:T(2,128)} %row_ref.1, s32[2,64]{1,0:T(2,128)} %col_ref.1, bf16[2,32,16,8,128]{4,3,2,1,0:T(8,128)(2,1)} %bitcast.4), custom_call_target="tpu_custom_call" | custom-call | tf_op jit(solution)/shard_map/tables/pallas_call | solution.py:277
  5.7 4.5 %collective-permute-start.3 = (s32[2,40]{1,0:T(2,128)}, s32[2,40]{1,0:T(2,128)S(1)}, u32[]{:S(2)}, u32[]{:S(2)}) collective-permute-start(s32[2,40]{1,0:T(2,128)} %get-tuple-element.32), channel_id=1, source_target_pairs={{1,2},{2,1},{3,4},{4,3},{5,6},{6,5},{7,8},{8,7},{9,10},{10,9},{11,... | collective-permute-start | bytes 968 | tf_op jit(solution)/shard_map/ppermute | solution.py:28
  10.2 1.4 %collective-permute-done.3.far_list.refs_1_ = s32[2,40]{1,0:T(2,128)S(1)} collective-permute-done((s32[2,40]{1,0:T(2,128)}, s32[2,40]{1,0:T(2,128)S(1)}, u32[]{:S(2)}, u32[]{:S(2)}) %collective-permute-start.3) | collective-permute-done | bytes 352 | tf_op jit(solution)/shard_map/ppermute | solution.py:28
  12.2 2.9 %pack.1 = (bf16[64,8,8,128]{3,2,1,0:T(8,128)(2,1)}, bf16[32,8,8,128]{3,2,1,0:T(8,128)(2,1)}, bf16[32,8,8,128]{3,2,1,0:T(8,128)(2,1)}) custom-call(bf16[4,8,16,8,128]{4,3,2,1,0:T(8,128)(2,1)} %bitcast.7, s32[2,40]{1,0:T(2,128)} %copy-done.10, s32[2,40]{1,0:T(2,128)} %copy-done.11), custom_call_target="tpu_custom_call" | custom-call | tf_op jit(solution)/shard_map/pack/pallas_call | solution.py:305
  15.1 5.0 %collective-permute-start.5 = (bf16[32,8,8,128]{3,2,1,0:T(8,128)(2,1)}, bf16[32,8,8,128]{3,2,1,0:T(8,128)(2,1)S(1)}, u32[]{:S(2)}, u32[]{:S(2)}) collective-permute-start(bf16[32,8,8,128]{3,2,1,0:T(8,128)(2,1)} %get-tuple-element.35), channel_id=1, source_target_pairs={{1,2},{2,1},{3,4},{4,3},{5,6},{6,5},{7,8},{8,7},{9,10},{10,9},{11,... | collective-permute-start | bytes 1572872 | tf_op jit(solution)/shard_map/ppermute | solution.py:28
  20.2 3.0 %collective-permute-start.1 = (bf16[2,3,16,8,128]{4,3,2,1,0:T(8,128)(2,1)}, bf16[2,3,16,8,128]{4,3,2,1,0:T(8,128)(2,1)S(1)}, u32[]{:S(2)}, u32[]{:S(2)}) collective-permute-start(bf16[2,3,16,8,128]{4,3,2,1,0:T(8,128)(2,1)} %get-tuple-element.28), channel_id=1, source_target_pairs={{1,2},{2,1},{3,4},{4,3},{5,6},{6,5},{7,8},{8,7},{9,10},{10,9},{11,... | collective-permute-start | bytes 589832 | tf_op jit(solution)/shard_map/ppermute | solution.py:28
  23.3 11.0 %collective-permute-done.5.far_ref = bf16[32,8,8,128]{3,2,1,0:T(8,128)(2,1)S(1)} collective-permute-done((bf16[32,8,8,128]{3,2,1,0:T(8,128)(2,1)}, bf16[32,8,8,128]{3,2,1,0:T(8,128)(2,1)S(1)}, u32[]{:S(2)}, u32[]{:S(2)}) %collective-permute-start.5) | collective-permute-done | bytes 524320 | tf_op jit(solution)/shard_map/ppermute | solution.py:28
  34.3 0.8 copy-done.3
  35.1 2.9 %assemble.2 = (bf16[32,16,8,128]{3,2,1,0:T(8,128)(2,1)}, bf16[3,16,8,128]{3,2,1,0:T(8,128)(2,1)}, bf16[3,16,8,128]{3,2,1,0:T(8,128)(2,1)}) custom-call(s32[2]{0:T(128)} %pad_add_fusion.place_ref, s32[2,64]{1,0:T(2,128)} %get-tuple-element.30.table_ref, bf16[64,8,8,128]{3,2,1,0:T(8,128)(2,1)} %get-tuple-element.33.pool_ref, ...), custom_call_target="tpu_custom_call" | custom-call | tf_op jit(solution)/shard_map/assemble/pallas_call | solution.py:332
  38.0 4.3 %collective-permute-start.7 = (bf16[3,16,8,128]{3,2,1,0:T(8,128)(2,1)}, bf16[3,16,8,128]{3,2,1,0:T(8,128)(2,1)S(1)}, u32[]{:S(2)}, u32[]{:S(2)}) collective-permute-start(bf16[3,16,8,128]{3,2,1,0:T(8,128)(2,1)} %get-tuple-element.38), channel_id=1, source_target_pairs={{1,2},{2,1},{3,4},{4,3},{5,6},{6,5},{7,8},{8,7},{9,10},{10,9},{11,... | collective-permute-start | bytes 294920 | tf_op jit(solution)/shard_map/ppermute | solution.py:28
  42.3 3.3 %weights.1 = (bf16[1536,256]{1,0:T(8,128)(2,1)}, bf16[1536,256]{1,0:T(8,128)(2,1)}, bf16[1536,256]{1,0:T(8,128)(2,1)}, bf16[1536,256]{1,0:T(8,128)(2,1)}) custom-call(bf16[3,3,256,128]{3,2,1,0:T(8,128)(2,1)} %merging_ref.1, bf16[3,3,128,128]{3,2,1,0:T(8,128)(2,1)} %first_ref.1, bf16[3,3,128,128]{3,2,1,0:T(8,128)(2,1)} %second_ref.1), custom_call_target="tpu_custom_call" | custom-call | tf_op jit(solution)/shard_map/weights/pallas_call | solution.py:295
  45.5 0.7 copy-done
  46.3 5.4 %features.3.part_ref = f32[18,128,256]{2,1,0:T(8,128)} custom-call(s32[2]{0:T(128)} %pad_add_fusion.place_ref, bf16[2,32,16,8,128]{4,3,2,1,0:T(8,128)(2,1)} %bitcast.5, bf16[2,3,16,8,128]{4,3,2,1,0:T(8,128)(2,1)} %copy-done, bf16[2,3,16,8,128]{4,3,2,1,0:T(8,128)(2,1)} %copy-done.1, bf16[1536,256]{1,0:T(8,128)(2,1)} %get-tuple-element.29.w_ref), custom_call_target="tpu_custom_call" | custom-call | tf_op jit(solution)/shard_map/features/pallas_call | solution.py:317
  51.7 0.6 copy-done.8
  52.4 10.6 %frame.2 = (bf16[2,32,16,8,128]{4,3,2,1,0:T(8,128)(2,1)}, bf16[64,8,8,128]{3,2,1,0:T(8,128)(2,1)}, bf16[32,8,8,128]{3,2,1,0:T(8,128)(2,1)}, bf16[32,8,8,128]{3,2,1,0:T(8,128)(2,1)}) custom-call(s32[2]{0:T(128)} %pad_add_fusion.place_ref, f32[18,128,256]{2,1,0:T(8,128)} %features.3.part_ref, bf16[32,16,8,128]{3,2,1,0:T(8,128)(2,1)} %get-tuple-element.36.warped_ref, ...), custom_call_target="tpu_custom_call" | custom-call | tf_op jit(solution)/shard_map/frame/pallas_call | solution.py:361
  63.0 3.5 %collective-permute-start.9 = (bf16[32,8,8,128]{3,2,1,0:T(8,128)(2,1)}, bf16[32,8,8,128]{3,2,1,0:T(8,128)(2,1)S(1)}, u32[]{:S(2)}, u32[]{:S(2)}) collective-permute-start(bf16[32,8,8,128]{3,2,1,0:T(8,128)(2,1)} %get-tuple-element.44), channel_id=1, source_target_pairs={{1,2},{2,1},{3,4},{4,3},{5,6},{6,5},{7,8},{8,7},{9,10},{10,9},{11,... | collective-permute-start | bytes 1572872 | tf_op jit(solution)/shard_map/ppermute | solution.py:28
  66.6 12.0 %collective-permute-done.9.far_ref = bf16[32,8,8,128]{3,2,1,0:T(8,128)(2,1)S(1)} collective-permute-done((bf16[32,8,8,128]{3,2,1,0:T(8,128)(2,1)}, bf16[32,8,8,128]{3,2,1,0:T(8,128)(2,1)S(1)}, u32[]{:S(2)}, u32[]{:S(2)}) %collective-permute-start.9) | collective-permute-done | bytes 524320 | tf_op jit(solution)/shard_map/ppermute | solution.py:28
  78.6 0.8 copy-done.5
  79.4 2.9 %assemble.3 = (bf16[32,16,8,128]{3,2,1,0:T(8,128)(2,1)}, bf16[3,16,8,128]{3,2,1,0:T(8,128)(2,1)}, bf16[3,16,8,128]{3,2,1,0:T(8,128)(2,1)}) custom-call(s32[2]{0:T(128)} %pad_add_fusion.place_ref, s32[2,64]{1,0:T(2,128)} %get-tuple-element.30.table_ref, bf16[64,8,8,128]{3,2,1,0:T(8,128)(2,1)} %get-tuple-element.42.pool_ref, ...), custom_call_target="tpu_custom_call" | custom-call | tf_op jit(solution)/shard_map/assemble/pallas_call | solution.py:332
  82.4 4.5 %collective-permute-start.11 = (bf16[3,16,8,128]{3,2,1,0:T(8,128)(2,1)}, bf16[3,16,8,128]{3,2,1,0:T(8,128)(2,1)S(1)}, u32[]{:S(2)}, u32[]{:S(2)}) collective-permute-start(bf16[3,16,8,128]{3,2,1,0:T(8,128)(2,1)} %get-tuple-element.47), channel_id=1, source_target_pairs={{1,2},{2,1},{3,4},{4,3},{5,6},{6,5},{7,8},{8,7},{9,10},{10,9},{11,... | collective-permute-start | bytes 294920 | tf_op jit(solution)/shard_map/ppermute | solution.py:28
  86.8 5.4 %features.2.part_ref = f32[18,128,256]{2,1,0:T(8,128)} custom-call(s32[2]{0:T(128)} %pad_add_fusion.place_ref, bf16[2,32,16,8,128]{4,3,2,1,0:T(8,128)(2,1)} %bitcast.6, bf16[2,3,16,8,128]{4,3,2,1,0:T(8,128)(2,1)} %copy-done, bf16[2,3,16,8,128]{4,3,2,1,0:T(8,128)(2,1)} %copy-done.1, bf16[1536,256]{1,0:T(8,128)(2,1)} %get-tuple-element.29.w_ref), custom_call_target="tpu_custom_call" | custom-call | tf_op jit(solution)/shard_map/features/pallas_call | solution.py:317
  92.2 0.6 copy-done.6
  92.9 9.2 %frame.3 = bf16[2,32,16,8,128]{4,3,2,1,0:T(8,128)(2,1)} custom-call(s32[2]{0:T(128)} %pad_add_fusion.place_ref, f32[18,128,256]{2,1,0:T(8,128)} %features.2.part_ref, bf16[32,16,8,128]{3,2,1,0:T(8,128)(2,1)} %get-tuple-element.45.warped_ref, bf16[3,16,8,128]{3,2,1,0:T(8,128)(2,1)} %copy-done.6, ...), custom_call_target="tpu_custom_call", output_to_operand_aliasing={{}: (8, {})} | custom-call | tf_op jit(solution)/shard_map/frame/pallas_call | solution.py:351
  (34 shorter events, 1.0 us)
Async XLA Ops:
  5.6 4.6 %collective-permute-start.2 = (s32[2,40]{1,0:T(2,128)}, s32[2,40]{1,0:T(2,128)S(1)}, u32[]{:S(2)}, u32[]{:S(2)}) collective-permute-start(s32[2,40]{1,0:T(2,128)} %get-tuple-element.31), channel_id=1, source_target_pairs={{0,1},{1,0},{2,3},{3,2},{4,5},{5,4},{6,7},{7,6},{8,9},{9,8},{10,11... | collective-permute-start | bytes 968 | tf_op jit(solution)/shard_map/ppermute | solution.py:28
  5.7 6.0 %collective-permute-start.3 = (s32[2,40]{1,0:T(2,128)}, s32[2,40]{1,0:T(2,128)S(1)}, u32[]{:S(2)}, u32[]{:S(2)}) collective-permute-start(s32[2,40]{1,0:T(2,128)} %get-tuple-element.32), channel_id=1, source_target_pairs={{1,2},{2,1},{3,4},{4,3},{5,6},{6,5},{7,8},{8,7},{9,10},{10,9},{11,... | collective-permute-start | bytes 968 | tf_op jit(solution)/shard_map/ppermute | solution.py:28
  10.2 1.4 %copy-start.10 = (s32[2,40]{1,0:T(2,128)}, s32[2,40]{1,0:T(2,128)S(1)}, u32[]{:S(2)}) copy-start(s32[2,40]{1,0:T(2,128)S(1)} %collective-permute-done.2.near_list.refs_0_) | copy-start | bytes 964
  11.6 0.6 copy-start.11
  15.1 8.1 %collective-permute-start.4 = (bf16[32,8,8,128]{3,2,1,0:T(8,128)(2,1)}, bf16[32,8,8,128]{3,2,1,0:T(8,128)(2,1)S(1)}, u32[]{:S(2)}, u32[]{:S(2)}) collective-permute-start(bf16[32,8,8,128]{3,2,1,0:T(8,128)(2,1)} %get-tuple-element.34), channel_id=1, source_target_pairs={{0,1},{1,0},{2,3},{3,2},{4,5},{5,4},{6,7},{7,6},{8,9},{9,8},{10,11... | collective-permute-start | bytes 1572872 | tf_op jit(solution)/shard_map/ppermute | solution.py:28
  15.1 19.2 %collective-permute-start.5 = (bf16[32,8,8,128]{3,2,1,0:T(8,128)(2,1)}, bf16[32,8,8,128]{3,2,1,0:T(8,128)(2,1)S(1)}, u32[]{:S(2)}, u32[]{:S(2)}) collective-permute-start(bf16[32,8,8,128]{3,2,1,0:T(8,128)(2,1)} %get-tuple-element.35), channel_id=1, source_target_pairs={{1,2},{2,1},{3,4},{4,3},{5,6},{6,5},{7,8},{8,7},{9,10},{10,9},{11,... | collective-permute-start | bytes 1572872 | tf_op jit(solution)/shard_map/ppermute | solution.py:28
  20.1 25.4 %collective-permute-start = (bf16[2,3,16,8,128]{4,3,2,1,0:T(8,128)(2,1)}, bf16[2,3,16,8,128]{4,3,2,1,0:T(8,128)(2,1)S(1)}, u32[]{:S(2)}, u32[]{:S(2)}) collective-permute-start(bf16[2,3,16,8,128]{4,3,2,1,0:T(8,128)(2,1)} %get-tuple-element.27), channel_id=1, source_target_pairs={{0,1},{1,0},{2,3},{3,2},{4,5},{5,4},{6,7},{7,6},{8,9},{9,8},{10,11... | collective-permute-start | bytes 589832 | tf_op jit(solution)/shard_map/ppermute | solution.py:28
  20.2 25.3 %collective-permute-start.1 = (bf16[2,3,16,8,128]{4,3,2,1,0:T(8,128)(2,1)}, bf16[2,3,16,8,128]{4,3,2,1,0:T(8,128)(2,1)S(1)}, u32[]{:S(2)}, u32[]{:S(2)}) collective-permute-start(bf16[2,3,16,8,128]{4,3,2,1,0:T(8,128)(2,1)} %get-tuple-element.28), channel_id=1, source_target_pairs={{1,2},{2,1},{3,4},{4,3},{5,6},{6,5},{7,8},{8,7},{9,10},{10,9},{11,... | collective-permute-start | bytes 589832 | tf_op jit(solution)/shard_map/ppermute | solution.py:28
  23.3 11.0 %copy-start.2 = (bf16[32,8,8,128]{3,2,1,0:T(8,128)(2,1)}, bf16[32,8,8,128]{3,2,1,0:T(8,128)(2,1)S(1)}, u32[]{:S(2)}) copy-start(bf16[32,8,8,128]{3,2,1,0:T(8,128)(2,1)S(1)} %collective-permute-done.4.near_ref) | copy-start | bytes 1572868
  34.3 0.8 copy-start.3
  38.0 13.7 %collective-permute-start.6 = (bf16[3,16,8,128]{3,2,1,0:T(8,128)(2,1)}, bf16[3,16,8,128]{3,2,1,0:T(8,128)(2,1)S(1)}, u32[]{:S(2)}, u32[]{:S(2)}) collective-permute-start(bf16[3,16,8,128]{3,2,1,0:T(8,128)(2,1)} %get-tuple-element.37), channel_id=1, source_target_pairs={{0,1},{1,0},{2,3},{3,2},{4,5},{5,4},{6,7},{7,6},{8,9},{9,8},{10,11... | collective-permute-start | bytes 294920 | tf_op jit(solution)/shard_map/ppermute | solution.py:28
  38.0 13.7 %collective-permute-start.7 = (bf16[3,16,8,128]{3,2,1,0:T(8,128)(2,1)}, bf16[3,16,8,128]{3,2,1,0:T(8,128)(2,1)S(1)}, u32[]{:S(2)}, u32[]{:S(2)}) collective-permute-start(bf16[3,16,8,128]{3,2,1,0:T(8,128)(2,1)} %get-tuple-element.38), channel_id=1, source_target_pairs={{1,2},{2,1},{3,4},{4,3},{5,6},{6,5},{7,8},{8,7},{9,10},{10,9},{11,... | collective-permute-start | bytes 294920 | tf_op jit(solution)/shard_map/ppermute | solution.py:28
  45.5 0.7 copy-start
  45.5 0.8 copy-start.1
  51.7 0.6 copy-start.8
  51.7 0.7 copy-start.9
  63.0 3.6 %collective-permute-start.8 = (bf16[32,8,8,128]{3,2,1,0:T(8,128)(2,1)}, bf16[32,8,8,128]{3,2,1,0:T(8,128)(2,1)S(1)}, u32[]{:S(2)}, u32[]{:S(2)}) collective-permute-start(bf16[32,8,8,128]{3,2,1,0:T(8,128)(2,1)} %get-tuple-element.43), channel_id=1, source_target_pairs={{0,1},{1,0},{2,3},{3,2},{4,5},{5,4},{6,7},{7,6},{8,9},{9,8},{10,11... | collective-permute-start | bytes 1572872 | tf_op jit(solution)/shard_map/ppermute | solution.py:28
  63.0 15.6 %collective-permute-start.9 = (bf16[32,8,8,128]{3,2,1,0:T(8,128)(2,1)}, bf16[32,8,8,128]{3,2,1,0:T(8,128)(2,1)S(1)}, u32[]{:S(2)}, u32[]{:S(2)}) collective-permute-start(bf16[32,8,8,128]{3,2,1,0:T(8,128)(2,1)} %get-tuple-element.44), channel_id=1, source_target_pairs={{1,2},{2,1},{3,4},{4,3},{5,6},{6,5},{7,8},{8,7},{9,10},{10,9},{11,... | collective-permute-start | bytes 1572872 | tf_op jit(solution)/shard_map/ppermute | solution.py:28
  66.6 12.0 %copy-start.4 = (bf16[32,8,8,128]{3,2,1,0:T(8,128)(2,1)}, bf16[32,8,8,128]{3,2,1,0:T(8,128)(2,1)S(1)}, u32[]{:S(2)}) copy-start(bf16[32,8,8,128]{3,2,1,0:T(8,128)(2,1)S(1)} %collective-permute-done.8.near_ref) | copy-start | bytes 1572868
  78.6 0.8 copy-start.5
  82.4 9.9 %collective-permute-start.10 = (bf16[3,16,8,128]{3,2,1,0:T(8,128)(2,1)}, bf16[3,16,8,128]{3,2,1,0:T(8,128)(2,1)S(1)}, u32[]{:S(2)}, u32[]{:S(2)}) collective-permute-start(bf16[3,16,8,128]{3,2,1,0:T(8,128)(2,1)} %get-tuple-element.46), channel_id=1, source_target_pairs={{0,1},{1,0},{2,3},{3,2},{4,5},{5,4},{6,7},{7,6},{8,9},{9,8},{10,11... | collective-permute-start | bytes 294920 | tf_op jit(solution)/shard_map/ppermute | solution.py:28
  82.4 9.9 %collective-permute-start.11 = (bf16[3,16,8,128]{3,2,1,0:T(8,128)(2,1)}, bf16[3,16,8,128]{3,2,1,0:T(8,128)(2,1)S(1)}, u32[]{:S(2)}, u32[]{:S(2)}) collective-permute-start(bf16[3,16,8,128]{3,2,1,0:T(8,128)(2,1)} %get-tuple-element.47), channel_id=1, source_target_pairs={{1,2},{2,1},{3,4},{4,3},{5,6},{6,5},{7,8},{8,7},{9,10},{10,9},{11,... | collective-permute-start | bytes 294920 | tf_op jit(solution)/shard_map/ppermute | solution.py:28
  92.2 0.6 copy-start.6
  92.2 0.7 copy-start.7
where the time goes:
time: 103 us; the launch traced here: 102 us
  Pallas kernels  47.5 us (46%)
  starting transfers between devices  25.1 us (24%)
  waiting for transfers between devices  24.5 us (24%)
  local copies, waits for them, and re-layouts  4.31 us (4%)
    ppermute x12, starting transfers between devices, swap(): return lax.ppermute(x, axis, pairs)  25.1 us
    ppermute x12, waiting for transfers between devices, swap(): return lax.ppermute(x, axis, pairs)  24.5 us
    pallas_call x2, Pallas kernels, features_part(): pl.pallas_call(functools.partial(features_kernel, frame), out_shape=shape...  10.8 us
    pallas_call x1, Pallas kernels, on_device(): pl.pallas_call(kernel, out_shape=[out_shape, pool_shape, message, message...  10.6 us
    pallas_call x1, Pallas kernels, on_device(): pl.pallas_call(kernel, out_shape=out_shape, in_specs=[SMEM] + [VMEM] * 7...  9.19 us
    pallas_call x2, Pallas kernels, on_device(): pl.pallas_call(functools.partial(assemble_kernel, frame), out_shape=[shap...  5.8 us
    pallas_call x1, Pallas kernels, on_device(): pl.pallas_call(functools.partial(tables_kernel, band, across, slots), out...  4.98 us
    unnamed x24, local copies, waits for them, and re-layouts  4.31 us
  transfers between devices with their start and end apart: 12, of which 3 were waited for; matrix products, arithmetic and copies ran while one was open for 0% of the time, Pallas kernels for 17%

commit v1 on v0

v1 whole, which is shorter than its diff:
```python
import functools

import jax
import jax.numpy as jnp
from jax import lax
from jax.experimental import pallas as pl
from jax.experimental.pallas import tpu as pltpu
from jax.sharding import PartitionSpec as P


BLK = 8
HALO = 3
STEP = 4
VMEM = pl.BlockSpec(memory_space=pltpu.VMEM)
SMEM = pl.BlockSpec(memory_space=pltpu.SMEM)
ANY = pl.BlockSpec(memory_space=pl.ANY)
BF16 = jnp.bfloat16
F32 = jnp.float32


def shape_of(shape, dtype=BF16):
    return jax.ShapeDtypeStruct(shape, dtype)


def on_chip(shape, dtype=BF16):
    return pltpu.VMEM(shape, dtype)


def room(mebibytes):
    return pltpu.CompilerParams(vmem_limit_bytes=mebibytes << 20)


def in_hbm(x):
    return pltpu.with_memory_space_constraint(x, pltpu.HBM)


def resident(x):
    return pltpu.with_memory_space_constraint(x, pltpu.VMEM)


def swap(x, axis, first):
    size = lax.axis_size(axis)
    pairs = []
    for i in range(first, size - 1, 2):
        pairs += [(i, i + 1), (i + 1, i)]
    return lax.ppermute(x, axis, pairs)


def swap_both(for_even, for_odd):
    far = swap(for_odd, "rows", 1)
    near = swap(for_even, "rows", 0)
    return near, far


def tables_kernel(band, across, slots, place_ref, row_hbm, col_hbm, feat_hbm,
                  table_ref, near_ref, far_ref, near_edge, far_edge, row_ref, col_ref, sem):
    frames, blocks = row_ref.shape
    rows = feat_hbm.shape[1]
    mine = place_ref[0]
    total = place_ref[1]
    even = lax.rem(mine, 2) == 0
    moves = [
        pltpu.make_async_copy(row_hbm, row_ref, sem.at[0]),
        pltpu.make_async_copy(col_hbm, col_ref, sem.at[1]),
    ]
    near_rows = pl.ds(jnp.where(even, rows - HALO, 0), HALO)
    far_rows = pl.ds(jnp.where(even, 0, rows - HALO), HALO)
    edges = [
        pltpu.make_async_copy(feat_hbm.at[:, near_rows], near_edge, sem.at[2]),
        pltpu.make_async_copy(feat_hbm.at[:, far_rows], far_edge, sem.at[3]),
    ]
    for copy in moves + edges:
        copy.start()
    for copy in moves:
        copy.wait()
    block = lax.broadcasted_iota(jnp.int32, (frames, blocks), 1)
    source = jnp.clip(block // across + row_ref[...], -mine * band, total - 1 - mine * band)
    column = jnp.clip(block % across + col_ref[...], 0, across - 1)
    above = source < 0
    below = source >= band
    local = source * across + column + jnp.where(above, blocks, jnp.where(below, -blocks, 0))
    earlier = lax.broadcasted_iota(jnp.int32, (blocks, blocks), 0) < lax.broadcasted_iota(
        jnp.int32, (blocks, blocks), 1
    )
    earlier = jnp.where(earlier, 1.0, 0.0).astype(BF16)

    def rank(mask):
        ones = jnp.where(mask, 1.0, 0.0).astype(BF16)
        return jnp.dot(ones, earlier, preferred_element_type=F32).astype(jnp.int32)

    rank_above = rank(above)
    rank_below = rank(below)
    near_base = blocks
    far_base = blocks + slots
    above_base = jnp.where(even, far_base, near_base)
    below_base = jnp.where(even, near_base, far_base)
    table = jnp.where(above, above_base + rank_above, local)
    table_ref[...] = jnp.where(below, below_base + rank_below, table)
    near_rank = jnp.where(even, jnp.where(below, rank_below, -1), jnp.where(above, rank_above, -1))
    far_rank = jnp.where(even, jnp.where(above, rank_above, -1), jnp.where(below, rank_below, -1))
    length = near_ref.shape[1]
    slot = lax.broadcasted_iota(jnp.int32, (length, blocks), 0)
    for frame in range(frames):
        ids = local[frame:frame + 1].astype(F32).astype(BF16)
        for ranks, out in ((near_rank, near_ref), (far_rank, far_ref)):
            chosen = jnp.where(ranks[frame:frame + 1] == slot, 1.0, 0.0).astype(BF16)
            got = lax.dot_general(ids, chosen, (((1,), (1,)), ((), ())), preferred_element_type=F32)
            out[frame:frame + 1] = got.astype(jnp.int32)
    for copy in edges:
        copy.wait()


def prepare_kernel(merging_hbm, first_hbm, second_hbm, state_hbm,
                   feat_out, warp_out, first_out, second_out, pool_out,
                   merging_ref, first_ref, second_ref, sem):
    band, _, across = state_hbm.shape[:3]
    for q in range(band):
        for r in range(BLK):
            pltpu.make_async_copy(
                state_hbm.at[q, r], pool_out.at[pl.ds(q * across, across), r], sem.at[3]
            ).start()
    loads = [
        pltpu.make_async_copy(merging_hbm, merging_ref, sem.at[0]),
        pltpu.make_async_copy(first_hbm, first_ref, sem.at[1]),
        pltpu.make_async_copy(second_hbm, second_ref, sem.at[2]),
    ]
    for load in loads:
        load.start()
    chans = first_ref.shape[2]
    depth = 3 * chans
    for source, start, out, load in (
        (merging_ref, 0, feat_out, loads[0]),
        (merging_ref, chans, warp_out, None),
        (first_ref, 0, first_out, loads[1]),
        (second_ref, 0, second_out, loads[2]),
    ):
        if load is not None:
            load.wait()
        width = source.shape[3]
        zero = jnp.zeros((chans, width), BF16)
        for a in range(4):
            for e in range(3):
                top = a * depth + e * chans
                for half in range(2):
                    tap = a - half
                    if 0 <= tap < 3:
                        value = source[tap, e, start:start + chans, :]
                    else:
                        value = zero
                    out[top:top + chans, half * width:(half + 1) * width] = value
    pltpu.make_async_copy(pool_out, pool_out, sem.at[3]).wait()


def pack(pool_ref, near_list, far_list, frame, near_out, far_out):
    for slot in range(near_out.shape[0]):
        near_out[slot] = pool_ref[near_list[frame, slot]]
        far_out[slot] = pool_ref[far_list[frame, slot]]


def pack_kernel(frame, pool_ref, near_list, far_list, near_out, far_out):
    pack(pool_ref, near_list, far_list, frame, near_out, far_out)


def spread(out_ref, pair, half, value, cols):
    chans = value.shape[1]
    pairs = value.shape[0] // cols
    place = lax.broadcasted_iota(jnp.int32, (pairs, cols, chans), 1).reshape(value.shape)
    left = jnp.where(place == 0, 0.0, pltpu.roll(value, 1, 0))
    right = jnp.where(place == cols - 1, 0.0, pltpu.roll(value, value.shape[0] - 1, 0))
    for e, part in enumerate((left, value, right)):
        out_ref[pair:pair + pairs, half, :, e * chans:(e + 1) * chans] = (
            part.astype(BF16).reshape(pairs, cols, chans)
        )


def pair_dot(x_ref, w_ref, pair, pairs):
    cols, depth = x_ref.shape[2:]
    parts = [
        x_ref[pair + a // 2:pair + a // 2 + pairs, a % 2].reshape(pairs * cols, depth)
        for a in range(4)
    ]
    return jnp.dot(jnp.concatenate(parts, axis=1), w_ref[...], preferred_element_type=F32)


def chunks(first, end, size):
    total = end - first
    count = -(-total // size)
    bounds = [first + total * n // count for n in range(count + 1)]
    return [(a, b - a) for a, b in zip(bounds, bounds[1:])]


def features_kernel(frame, place_ref, feat_hbm, near_ref, far_ref, w_ref, out_ref, feat_ref, x_ref, sem):
    rows, across, _, chans = feat_ref.shape
    cols = across * BLK
    even = lax.rem(place_ref[0], 2) == 0
    size = rows // sem.shape[0]
    loads = []
    for n in range(sem.shape[0]):
        part = pl.ds(n * size, size)
        loads.append(pltpu.make_async_copy(feat_hbm.at[frame, part], feat_ref.at[part], sem.at[n]))
        loads[-1].start()
    for row in range(-HALO, rows + HALO):
        if row < 0:
            value = jnp.where(even, far_ref[frame, row + HALO], near_ref[frame, row + HALO])
        elif row >= rows:
            value = jnp.where(even, near_ref[frame, row - rows], far_ref[frame, row - rows])
        else:
            if row % size == 0:
                loads[row // size].wait()
            value = feat_ref[row]
        value = value.astype(F32).reshape(cols, chans)
        spread(x_ref, (row + HALO) // 2, (row + HALO) % 2, value, cols)
    for pair, pairs in chunks(0, rows // 2 + 2, STEP):
        out_ref[pair:pair + pairs] = pair_dot(x_ref, w_ref, pair, pairs).reshape(
            pairs, cols, out_ref.shape[2]
        )


def assemble_kernel(frame, place_ref, table_ref, pool_ref, near_ref, far_ref, _,
                    warped_out, near_edge, far_edge, all_ref):
    rows, across = warped_out.shape[:2]
    blocks = pool_ref.shape[0]
    slots = near_ref.shape[0]
    all_ref[0:blocks] = pool_ref[...]
    all_ref[blocks:blocks + slots] = near_ref[...]
    all_ref[blocks + slots:blocks + 2 * slots] = far_ref[...]
    for block in range(blocks):
        q, p = divmod(block, across)
        warped_out[q * BLK:(q + 1) * BLK, p] = all_ref[table_ref[frame, block]]
    odd = lax.rem(place_ref[0], 2)
    near_start = jnp.where(odd == 0, rows - HALO, 0)
    far_start = jnp.where(odd == 0, 0, rows - HALO)
    near_edge[...] = warped_out[pl.ds(near_start, HALO)]
    far_edge[...] = warped_out[pl.ds(far_start, HALO)]


def split_rows(value, pairs, cols, chans):
    for n in range(pairs):
        for half in range(2):
            yield n, half, value[n * cols:(n + 1) * cols, half * chans:(half + 1) * chans]


def finish(state_ref, pool_ref, centre, value, row, across, chans):
    done = (centre.astype(F32) + value).reshape(across, BLK, chans).astype(BF16)
    state_ref[row] = done
    if pool_ref is not None:
        q, r = divmod(row, BLK)
        pool_ref[q * across:(q + 1) * across, r] = done


def inner_kernel(frame, last, part_ref, warped_ref, w1_ref, w2_ref, w3_ref, *refs):
    if frame:
        refs = refs[1:]
    out_ref = refs[0]
    pool_ref = None if last else refs[1]
    m_edge, d_edge, x_ref, m_ref, d_ref, state_ref, sem = refs[-7:]
    rows, across, _, chans = warped_ref.shape
    cols = across * BLK
    half_rows = rows // 2
    for row in range(rows):
        value = warped_ref[row].astype(F32).reshape(cols, chans)
        spread(x_ref, (row + HALO) // 2, (row + HALO) % 2, value, cols)
    for pair, pairs in chunks(2, half_rows, STEP):
        raw = part_ref[pair:pair + pairs].reshape(pairs * cols, 2 * chans)
        raw = raw + pair_dot(x_ref, w1_ref, pair, pairs)
        value = jnp.maximum(raw, 0.1 * raw)
        for n, half, one in split_rows(value, pairs, cols, chans):
            spread(m_ref, pair + n, half, one, cols)
    m_edge[0] = m_ref[2]
    m_edge[1] = m_ref[half_rows - 1]
    for pair, pairs in chunks(2, half_rows - 1, STEP):
        value = jnp.maximum(pair_dot(m_ref, w2_ref, pair, pairs), 0.0)
        for n, half, one in split_rows(value, pairs, cols, chans):
            spread(d_ref, pair + n, half, one, cols)
    d_edge[0] = d_ref[2]
    d_edge[1] = d_ref[half_rows - 2]
    for pair, pairs in chunks(2, half_rows - 2, STEP):
        value = pair_dot(d_ref, w3_ref, pair, pairs)
        for n, half, one in split_rows(value, pairs, cols, chans):
            centre = m_ref[pair + n + 1, half, :, chans:2 * chans]
            finish(state_ref, pool_ref, centre, one, 2 * (pair + n) + half, across, chans)
        pltpu.make_async_copy(
            state_ref.at[pl.ds(2 * pair, 2 * pairs)],
            out_ref.at[frame, pl.ds(2 * pair, 2 * pairs)],
            sem,
        ).start()
    inner = pl.ds(4, rows - 8)
    pltpu.make_async_copy(state_ref.at[inner], out_ref.at[frame, inner], sem).wait()


def border_kernel(frame, last, place_ref, part_ref, warped_ref, near_ref, far_ref, w1_ref, w2_ref, w3_ref,
                  m_edge, d_edge, *refs):
    if last:
        _, out_ref, x_ref, m_ref, d_ref, state_ref, sem = refs
        pool_ref = None
    else:
        _, _, near_list, far_list, out_ref, pool_ref, near_out, far_out = refs[:8]
        x_ref, m_ref, d_ref, state_ref, sem = refs[8:]
    rows, across, _, chans = warped_ref.shape
    cols = across * BLK
    mine = place_ref[0]
    even = lax.rem(mine, 2) == 0
    has_above = mine > 0
    has_below = (mine + 1) * (rows // BLK) < place_ref[1]
    depth = 3 * chans

    def edge_dot(ref, side, w_ref):
        parts = [ref[side, a // 2:a // 2 + 2, a % 2].reshape(2 * cols, depth) for a in range(4)]
        return jnp.dot(jnp.concatenate(parts, axis=1), w_ref[...], preferred_element_type=F32)

    def flat(value):
        return value.astype(F32).reshape(cols, chans)

    for n in range(HALO):
        above = jnp.where(even, far_ref[n], near_ref[n])
        below = jnp.where(even, near_ref[n], far_ref[n])
        spread(x_ref.at[0], n // 2, n % 2, flat(above), cols)
        spread(x_ref.at[0], (n + 3) // 2, (n + 3) % 2, flat(warped_ref[n]), cols)
        spread(x_ref.at[1], n // 2, n % 2, flat(warped_ref[rows - HALO + n]), cols)
        spread(x_ref.at[1], (n + 3) // 2, (n + 3) % 2, flat(below), cols)
    half_rows = rows // 2

    def masked(value, row):
        if row < 0:
            return jnp.where(has_above, value, 0.0)
        return jnp.where(has_below, value, 0.0) if row >= rows else value

    m_ref[0, 2] = m_edge[0]
    m_ref[1, 0] = m_edge[1]
    d_ref[0, 2] = d_edge[0]
    d_ref[1, 0] = d_edge[1]
    for side in range(2):
        first = side * half_rows
        raw = part_ref[first:first + 2].reshape(2 * cols, 2 * chans) + edge_dot(x_ref, side, w1_ref)
        value = jnp.maximum(raw, 0.1 * raw)
        for n, half, one in split_rows(value, 2, cols, chans):
            one = masked(one, 2 * (first + n) + half - 2)
            spread(m_ref.at[side], n + side, half, one, cols)
    for side in range(2):
        first = side * (half_rows - 1)
        value = jnp.maximum(edge_dot(m_ref, side, w2_ref), 0.0)
        for n, half, one in split_rows(value, 2, cols, chans):
            one = masked(one, 2 * (first + n) + half - 1)
            spread(d_ref.at[side], n + side, half, one, cols)
    for side in range(2):
        first = side * (half_rows - 2)
        value = edge_dot(d_ref, side, w3_ref)
        for n, half, one in split_rows(value, 2, cols, chans):
            centre = m_ref[side, n + 1 - side, half, :, chans:2 * chans]
            finish(state_ref, pool_ref, centre, one, 2 * (first + n) + half, across, chans)
    copies = []
    for n, start in enumerate((0, rows - 4)):
        part = pl.ds(start, 4)
        copies.append(pltpu.make_async_copy(state_ref.at[part], out_ref.at[frame, part], sem.at[n]))
        copies[-1].start()
    if not last:
        pack(pool_ref, near_list, far_list, frame + 1, near_out, far_out)
    for copy in copies:
        copy.wait()


def on_device(state_start, features, row_moves, col_moves, merging_weight, first_weight, second_weight):
    rows, cols, chans = state_start.shape
    frames = features.shape[0]
    band = rows // BLK
    across = cols // BLK
    blocks = band * across
    slots = blocks // 2
    list_len = slots + 8
    mine = lax.axis_index("rows")
    place = jnp.stack([mine, jnp.int32(band * lax.axis_size("rows"))]).astype(jnp.int32)
    state = state_start.reshape(band, BLK, across, BLK, chans)
    feats = features.reshape(frames, rows, across, BLK, chans)
    block_shape = (BLK, BLK, chans)
    edge_shape = (HALO, across, BLK, chans)

    table, near_list, far_list, near_feat, far_feat = pl.pallas_call(
        functools.partial(tables_kernel, band, across, slots),
        out_shape=[
            on_chip((frames, blocks), jnp.int32),
            on_chip((frames, list_len), jnp.int32),
            on_chip((frames, list_len), jnp.int32),
            on_chip((frames,) + edge_shape),
            on_chip((frames,) + edge_shape),
        ],
        in_specs=[SMEM, ANY, ANY, ANY],
        out_specs=[VMEM] * 5,
        scratch_shapes=[
            pltpu.VMEM((frames, blocks), jnp.int32),
            pltpu.VMEM((frames, blocks), jnp.int32),
            pltpu.SemaphoreType.DMA((4,)),
        ],
        compiler_params=room(4),
        name="tables",
    )(place, *map(in_hbm, (row_moves, col_moves, feats)))
    near_list, far_list = swap_both(near_list, far_list)
    near_feat, far_feat = swap_both(near_feat, far_feat)

    pair_shape = on_chip((4 * 3 * chans, 2 * chans))
    pool_shape = on_chip((blocks,) + block_shape)
    message = on_chip((slots,) + block_shape)
    w_feat, w_warp, w_first, w_second, pool = pl.pallas_call(
        prepare_kernel,
        out_shape=[pair_shape] * 4 + [pool_shape],
        in_specs=[ANY] * 4,
        out_specs=[VMEM] * 5,
        scratch_shapes=[
            pltpu.VMEM(merging_weight.shape, BF16),
            pltpu.VMEM(first_weight.shape, BF16),
            pltpu.VMEM(second_weight.shape, BF16),
            pltpu.SemaphoreType.DMA((4,)),
        ],
        compiler_params=room(4),
        name="prepare",
    )(*map(in_hbm, (merging_weight, first_weight, second_weight, state)))

    near_msg, far_msg = pl.pallas_call(
        functools.partial(pack_kernel, 0),
        out_shape=[message, message],
        in_specs=[VMEM, SMEM, SMEM],
        out_specs=[VMEM] * 2,
        compiler_params=room(4),
        name="pack",
    )(resident(pool), near_list, far_list)

    def wide(extra):
        return pltpu.VMEM((rows // 2 + extra, 2, cols, 3 * chans), BF16)

    def features_part(frame):
        return pl.pallas_call(
            functools.partial(features_kernel, frame),
            out_shape=on_chip((rows // 2 + 2, cols, 2 * chans), F32),
            in_specs=[SMEM, ANY] + [VMEM] * 3,
            out_specs=VMEM,
            scratch_shapes=[
                pltpu.VMEM((rows, across, BLK, chans), BF16),
                wide(3),
                pltpu.SemaphoreType.DMA((4,)),
            ],
            compiler_params=room(16),
            name="features",
        )(place, in_hbm(feats), resident(near_feat), resident(far_feat), resident(w_feat))

    out = None
    out_shape = shape_of((frames, rows, across, BLK, chans))
    edge_pairs = on_chip((2, 2, cols, 3 * chans))
    for frame in range(frames):
        last = frame == frames - 1
        near_got, far_got = swap_both(near_msg, far_msg)
        part = features_part(frame)
        warped, near_edge, far_edge = pl.pallas_call(
            functools.partial(assemble_kernel, frame),
            out_shape=[on_chip((rows, across, BLK, chans)), on_chip(edge_shape), on_chip(edge_shape)],
            in_specs=[SMEM, SMEM] + [VMEM] * 3 + [ANY],
            out_specs=[VMEM] * 3,
            scratch_shapes=[pltpu.VMEM((blocks + 2 * slots,) + block_shape, BF16)],
            compiler_params=room(8),
            name="assemble",
        )(place, table, resident(pool), resident(near_got), resident(far_got), part)
        near_halo, far_halo = swap_both(near_edge, far_edge)
        args = tuple(map(resident, (part, warped, w_warp, w_first, w_second)))
        results = pl.pallas_call(
            functools.partial(inner_kernel, frame, last),
            out_shape=[out_shape] + [pool_shape] * (not last) + [edge_pairs] * 2,
            in_specs=[VMEM] * 5 + [ANY] * (frame > 0),
            out_specs=[ANY] + [VMEM] * (2 + (not last)),
            input_output_aliases={5: 0} if frame else {},
            scratch_shapes=[
                wide(3),
                wide(2),
                wide(1),
                pltpu.VMEM((rows, across, BLK, chans), BF16),
                pltpu.SemaphoreType.DMA,
            ],
            compiler_params=room(24),
            name="inner",
        )(*args, *([out] if frame else []))
        out = results[0]
        m_edge, d_edge = results[-2:]
        args = (place,) + tuple(map(resident, (
            part, warped, near_halo, far_halo, w_warp, w_first, w_second, m_edge, d_edge
        )))
        scratch = [pltpu.VMEM((2, 3, 2, cols, 3 * chans), BF16) for _ in range(3)] + [
            pltpu.VMEM((rows, across, BLK, chans), BF16),
            pltpu.SemaphoreType.DMA((2,)),
        ]
        kernel = functools.partial(border_kernel, frame, last)
        if last:
            out = pl.pallas_call(
                kernel,
                out_shape=out_shape,
                in_specs=[SMEM] + [VMEM] * 9 + [ANY],
                out_specs=ANY,
                input_output_aliases={10: 0},
                scratch_shapes=scratch,
                compiler_params=room(12),
                name="border",
            )(*args, out)
        else:
            out, pool, near_msg, far_msg = pl.pallas_call(
                kernel,
                out_shape=[out_shape, pool_shape, message, message],
                in_specs=[SMEM] + [VMEM] * 9 + [ANY, VMEM] + [SMEM] * 2,
                out_specs=[ANY] + [VMEM] * 3,
                input_output_aliases={10: 0, 11: 1},
                scratch_shapes=scratch,
                compiler_params=room(12),
                name="border",
            )(*args, out, resident(results[1]), near_list, far_list)
    return out.reshape(frames, rows, cols, chans)


def solution(mesh):
    in_specs = (
        P(("clips", "rows"), None, None),
        P(None, ("clips", "rows"), None, None),
        P(None, ("clips", "rows")),
        P(None, ("clips", "rows")),
        P(),
        P(),
        P(),
    )
    out_specs = P(None, ("clips", "rows"), None, None)
    return jax.shard_map(
        on_device, mesh=mesh, in_specs=in_specs, out_specs=out_specs, check_vma=False
    )
```

time: 103 us -> 77.3 us (0.75)
  Pallas kernels: 47.5 us -> 31.4 us
  local copies, waits for them, and re-layouts: 4.31 us -> 0 us
  waiting for transfers between devices: 24.5 us -> 20.4 us
    pallas_call x1, Pallas kernels: 10.6 us -> 3.13 us  [on_device(): pl.pallas_call(kernel, out_shape=[out_shape, pool_shape, message, message...]
    pallas_call x7 -> x9, Pallas kernels: 31.9 us -> 26.6 us  [the longest x2 11.2 us: on_device(): pl.pallas_call(functools.partial(inner_kernel, frame, last), out_shape=[o...]
    unnamed x24 -> x0, local copies, waits for them, and re-layouts: 4.31 us -> none
    ppermute x12, waiting for transfers between devices: 24.5 us -> 20.4 us  [swap(): return lax.ppermute(x, axis, pairs)]
    pallas_call x1, Pallas kernels: 4.98 us -> 1.63 us  [on_device(): pl.pallas_call(functools.partial(tables_kernel, band, across, slots), out...]
  transfers between devices with their start and end apart: 12 -> 12, of which waited for: 3 -> 2; matrix products, arithmetic and copies ran while one was open for 0% -> 0% of each run, Pallas kernels for 17% -> 27%
where the time goes in v1:
time: 77.3 us; the launch traced here: 77 us
  Pallas kernels  31.4 us (41%)
  starting transfers between devices  24.8 us (32%)
  waiting for transfers between devices  20.4 us (26%)
    ppermute x12, starting transfers between devices, swap(): return lax.ppermute(x, axis, pairs)  24.8 us
    ppermute x12, waiting for transfers between devices, swap(): return lax.ppermute(x, axis, pairs)  20.4 us
    pallas_call x2, Pallas kernels, on_device(): pl.pallas_call(functools.partial(inner_kernel, frame, last), out_shape=[o...  11.2 us
    pallas_call x2, Pallas kernels, features_part(): pl.pallas_call(functools.partial(features_kernel, frame), out_shape=on_ch...  7.92 us
    pallas_call x1, Pallas kernels, on_device(): pl.pallas_call(kernel, out_shape=[out_shape, pool_shape, message, message...  3.13 us
    pallas_call x1, Pallas kernels, on_device(): pl.pallas_call(kernel, out_shape=out_shape, in_specs=[SMEM] + [VMEM] * 9...  3.1 us
    pallas_call x1, Pallas kernels, on_device(): pl.pallas_call(prepare_kernel, out_shape=[pair_shape] * 4 + [pool_shape],...  1.96 us
    pallas_call x2, Pallas kernels, on_device(): pl.pallas_call(functools.partial(assemble_kernel, frame), out_shape=[on_c...  1.82 us
  transfers between devices with their start and end apart: 12, of which 2 were waited for; matrix products, arithmetic and copies ran while one was open for 0% of the time, Pallas kernels for 27%

profile of v1, /device:TPU:1, one launch (start us, length us, event | category | flops | bytes accessed | tf_op | source)
XLA Modules:
  0.0 77.0 jit_solution(5744748116072524852)
XLA Ops:
  0.0 0.1 pad_add_fusion.place_ref
  0.1 1.6 %tables.1 = (s32[2,64]{1,0:T(2,128)S(1)}, s32[2,40]{1,0:T(2,128)S(1)}, s32[2,40]{1,0:T(2,128)S(1)}, bf16[2,3,16,8,128]{4,3,2,1,0:T(8,128)(2,1)S(1)}, bf16[2,3,16,8,128]{4,3,2,1,0:T(8,128)(2,1)S(1)}) custom-call(s32[2]{0:T(128)S(1)} %pad_add_fusion.place_ref, s32[2,64]{1,0:T(2,128)} %row_hbm.1, s32[2,64]{1,0:T(2,128)} %col_hbm.1, ...), custom_call_target="tpu_custom_call" | custom-call | tf_op jit(solution)/shard_map/tables/pallas_call | solution.py:377
  1.7 0.1 collective-permute-start.2
  1.8 4.5 %collective-permute-start.3 = (s32[2,40]{1,0:T(2,128)S(1)}, s32[2,40]{1,0:T(2,128)S(1)}, u32[]{:S(2)}, u32[]{:S(2)}) collective-permute-start(s32[2,40]{1,0:T(2,128)S(1)} %get-tuple-element.40), channel_id=1, source_target_pairs={{1,2},{2,1},{3,4},{4,3},{5,6},{6,5},{7,8},{8,7},{9,10},{10,9},{11,... | collective-permute-start | bytes 968 | tf_op jit(solution)/shard_map/ppermute | solution.py:46
  6.3 2.0 %prepare.1 = (bf16[1536,256]{1,0:T(8,128)(2,1)S(1)}, bf16[1536,256]{1,0:T(8,128)(2,1)S(1)}, bf16[1536,256]{1,0:T(8,128)(2,1)S(1)}, bf16[1536,256]{1,0:T(8,128)(2,1)S(1)}, bf16[64,8,8,128]{3,2,1,0:T(8,128)(2,1)S(1)}) custom-call(bf16[3,3,256,128]{3,2,1,0:T(8,128)(2,1)} %merging_hbm.1, bf16[3,3,128,128]{3,2,1,0:T(8,128)(2,1)} %first_hbm.1, ...), custom_call_target="tpu_custom_call" | custom-call | tf_op jit(solution)/shard_map/prepare/pallas_call | solution.py:402
  8.3 0.6 pack.1
  9.0 0.1 collective-permute-start.4
  9.0 4.3 %collective-permute-start.5 = (bf16[32,8,8,128]{3,2,1,0:T(8,128)(2,1)S(1)}, bf16[32,8,8,128]{3,2,1,0:T(8,128)(2,1)S(1)}, u32[]{:S(2)}, u32[]{:S(2)}) collective-permute-start(bf16[32,8,8,128]{3,2,1,0:T(8,128)(2,1)S(1)} %get-tuple-element.42), channel_id=1, source_target_pairs={{1,2},{2,1},{3,4},{4,3},{5,6},{6,5},{7,8},{8,7},{9,10},{10,9},{11,... | collective-permute-start | bytes 1572872 | tf_op jit(solution)/shard_map/ppermute | solution.py:46
  13.3 0.1 collective-permute-start
  13.4 3.1 %collective-permute-start.1 = (bf16[2,3,16,8,128]{4,3,2,1,0:T(8,128)(2,1)S(1)}, bf16[2,3,16,8,128]{4,3,2,1,0:T(8,128)(2,1)S(1)}, u32[]{:S(2)}, u32[]{:S(2)}) collective-permute-start(bf16[2,3,16,8,128]{4,3,2,1,0:T(8,128)(2,1)S(1)} %get-tuple-element.35), channel_id=1, source_target_pairs={{1,2},{2,1},{3,4},{4,3},{5,6},{6,5},{7,8},{8,7},{9,10},{10,9},{11,... | collective-permute-start | bytes 589832 | tf_op jit(solution)/shard_map/ppermute | solution.py:46
  16.4 12.8 %collective-permute-done.1.far_ref = bf16[2,3,16,8,128]{4,3,2,1,0:T(8,128)(2,1)S(1)} collective-permute-done((bf16[2,3,16,8,128]{4,3,2,1,0:T(8,128)(2,1)S(1)}, bf16[2,3,16,8,128]{4,3,2,1,0:T(8,128)(2,1)S(1)}, u32[]{:S(2)}, u32[]{:S(2)}) %collective-permute-start.1) | collective-permute-done | bytes 196640 | tf_op jit(solution)/shard_map/ppermute | solution.py:46
  29.2 4.0 %features.3._.part_ref = f32[18,128,256]{2,1,0:T(8,128)S(1)} custom-call(s32[2]{0:T(128)S(1)} %pad_add_fusion.place_ref, bf16[2,32,16,8,128]{4,3,2,1,0:T(8,128)(2,1)} %bitcast.5, bf16[2,3,16,8,128]{4,3,2,1,0:T(8,128)(2,1)S(1)} %collective-permute-done.near_ref, bf16[2,3,16,8,128]{4,3,2,1,0:T(8,128)(2,1)S(1)} %collective-permute-done.1.far_ref, ...), custom_call_target="tpu_custom_call" | custom-call | tf_op jit(solution)/shard_map/features/pallas_call | solution.py:430
  33.2 0.9 %assemble.2 = (bf16[32,16,8,128]{3,2,1,0:T(8,128)(2,1)S(1)}, bf16[3,16,8,128]{3,2,1,0:T(8,128)(2,1)S(1)}, bf16[3,16,8,128]{3,2,1,0:T(8,128)(2,1)S(1)}) custom-call(s32[2]{0:T(128)S(1)} %pad_add_fusion.place_ref, s32[2,64]{1,0:T(2,128)S(1)} %get-tuple-element.37.table_ref, bf16[64,8,8,128]{3,2,1,0:T(8,128)(2,1)S(1)} %get-tuple-element.38.pool_ref, ...), custom_call_target="tpu_custom_call" | custom-call | tf_op jit(solution)/shard_map/assemble/pallas_call | solution.py:451
  34.2 4.4 %collective-permute-start.7 = (bf16[3,16,8,128]{3,2,1,0:T(8,128)(2,1)S(1)}, bf16[3,16,8,128]{3,2,1,0:T(8,128)(2,1)S(1)}, u32[]{:S(2)}, u32[]{:S(2)}) collective-permute-start(bf16[3,16,8,128]{3,2,1,0:T(8,128)(2,1)S(1)} %get-tuple-element.45), channel_id=1, source_target_pairs={{1,2},{2,1},{3,4},{4,3},{5,6},{6,5},{7,8},{8,7},{9,10},{10,9},{11,... | collective-permute-start | bytes 294920 | tf_op jit(solution)/shard_map/ppermute | solution.py:46
  38.6 5.6 %inner.2 = (bf16[2,32,16,8,128]{4,3,2,1,0:T(8,128)(2,1)}, bf16[64,8,8,128]{3,2,1,0:T(8,128)(2,1)S(1)}, bf16[2,2,128,384]{3,2,1,0:T(8,128)(2,1)S(1)}, bf16[2,2,128,384]{3,2,1,0:T(8,128)(2,1)S(1)}) custom-call(f32[18,128,256]{2,1,0:T(8,128)S(1)} %features.3._.part_ref, bf16[32,16,8,128]{3,2,1,0:T(8,128)(2,1)S(1)} %get-tuple-element.43.warped_ref, ...), custom_call_target="tpu_custom_call" | custom-call | tf_op jit(solution)/shard_map/inner/pallas_call | solution.py:462
  44.3 3.1 %border.2 = (bf16[2,32,16,8,128]{4,3,2,1,0:T(8,128)(2,1)}, bf16[64,8,8,128]{3,2,1,0:T(8,128)(2,1)S(1)}, bf16[32,8,8,128]{3,2,1,0:T(8,128)(2,1)S(1)}, bf16[32,8,8,128]{3,2,1,0:T(8,128)(2,1)S(1)}) custom-call(s32[2]{0:T(128)S(1)} %pad_add_fusion.place_ref, f32[18,128,256]{2,1,0:T(8,128)S(1)} %features.3._.part_ref, ...), custom_call_target="tpu_custom_call", output_to_operand_aliasing={{0}: (10, {}), {1}: (11, {})} | custom-call | tf_op jit(solution)/shard_map/border/pallas_call | solution.py:500
  47.4 0.1 collective-permute-start.8
  47.5 3.7 %collective-permute-start.9 = (bf16[32,8,8,128]{3,2,1,0:T(8,128)(2,1)S(1)}, bf16[32,8,8,128]{3,2,1,0:T(8,128)(2,1)S(1)}, u32[]{:S(2)}, u32[]{:S(2)}) collective-permute-start(bf16[32,8,8,128]{3,2,1,0:T(8,128)(2,1)S(1)} %get-tuple-element.55), channel_id=1, source_target_pairs={{1,2},{2,1},{3,4},{4,3},{5,6},{6,5},{7,8},{8,7},{9,10},{10,9},{11,... | collective-permute-start | bytes 1572872 | tf_op jit(solution)/shard_map/ppermute | solution.py:46
  51.2 4.0 %features.2._.part_ref = f32[18,128,256]{2,1,0:T(8,128)S(1)} custom-call(s32[2]{0:T(128)S(1)} %pad_add_fusion.place_ref, bf16[2,32,16,8,128]{4,3,2,1,0:T(8,128)(2,1)} %bitcast.6, bf16[2,3,16,8,128]{4,3,2,1,0:T(8,128)(2,1)S(1)} %collective-permute-done.near_ref, bf16[2,3,16,8,128]{4,3,2,1,0:T(8,128)(2,1)S(1)} %collective-permute-done.1.far_ref, ...), custom_call_target="tpu_custom_call" | custom-call | tf_op jit(solution)/shard_map/features/pallas_call | solution.py:430
  55.2 7.6 %collective-permute-done.9.far_ref = bf16[32,8,8,128]{3,2,1,0:T(8,128)(2,1)S(1)} collective-permute-done((bf16[32,8,8,128]{3,2,1,0:T(8,128)(2,1)S(1)}, bf16[32,8,8,128]{3,2,1,0:T(8,128)(2,1)S(1)}, u32[]{:S(2)}, u32[]{:S(2)}) %collective-permute-start.9) | collective-permute-done | bytes 524320 | tf_op jit(solution)/shard_map/ppermute | solution.py:46
  62.7 0.9 %assemble.3 = (bf16[32,16,8,128]{3,2,1,0:T(8,128)(2,1)S(1)}, bf16[3,16,8,128]{3,2,1,0:T(8,128)(2,1)S(1)}, bf16[3,16,8,128]{3,2,1,0:T(8,128)(2,1)S(1)}) custom-call(s32[2]{0:T(128)S(1)} %pad_add_fusion.place_ref, s32[2,64]{1,0:T(2,128)S(1)} %get-tuple-element.37.table_ref, bf16[64,8,8,128]{3,2,1,0:T(8,128)(2,1)S(1)} %get-tuple-element.53.pool_ref, ...), custom_call_target="tpu_custom_call" | custom-call | tf_op jit(solution)/shard_map/assemble/pallas_call | solution.py:451
  63.7 4.4 %collective-permute-start.11 = (bf16[3,16,8,128]{3,2,1,0:T(8,128)(2,1)S(1)}, bf16[3,16,8,128]{3,2,1,0:T(8,128)(2,1)S(1)}, u32[]{:S(2)}, u32[]{:S(2)}) collective-permute-start(bf16[3,16,8,128]{3,2,1,0:T(8,128)(2,1)S(1)} %get-tuple-element.58), channel_id=1, source_target_pairs={{1,2},{2,1},{3,4},{4,3},{5,6},{6,5},{7,8},{8,7},{9,10},{10,9},{11,... | collective-permute-start | bytes 294920 | tf_op jit(solution)/shard_map/ppermute | solution.py:46
  68.1 5.6 %inner.3 = (bf16[2,32,16,8,128]{4,3,2,1,0:T(8,128)(2,1)}, bf16[2,2,128,384]{3,2,1,0:T(8,128)(2,1)S(1)}, bf16[2,2,128,384]{3,2,1,0:T(8,128)(2,1)S(1)}) custom-call(f32[18,128,256]{2,1,0:T(8,128)S(1)} %features.2._.part_ref, bf16[32,16,8,128]{3,2,1,0:T(8,128)(2,1)S(1)} %get-tuple-element.56.warped_ref, ...), custom_call_target="tpu_custom_call", output_to_operand_aliasing={{0}: (5, {})} | custom-call | tf_op jit(solution)/shard_map/inner/pallas_call | solution.py:462
  73.7 3.1 %border.3 = bf16[2,32,16,8,128]{4,3,2,1,0:T(8,128)(2,1)} custom-call(s32[2]{0:T(128)S(1)} %pad_add_fusion.place_ref, f32[18,128,256]{2,1,0:T(8,128)S(1)} %features.2._.part_ref, bf16[32,16,8,128]{3,2,1,0:T(8,128)(2,1)S(1)} %get-tuple-element.56.warped_ref, ...), custom_call_target="tpu_custom_call", output_to_operand_aliasing={{}: (10, {})} | custom-call | tf_op jit(solution)/shard_map/border/pallas_call | solution.py:489
  (12 shorter events, 0.2 us)
Async XLA Ops:
  1.7 6.6 %collective-permute-start.2 = (s32[2,40]{1,0:T(2,128)S(1)}, s32[2,40]{1,0:T(2,128)S(1)}, u32[]{:S(2)}, u32[]{:S(2)}) collective-permute-start(s32[2,40]{1,0:T(2,128)S(1)} %get-tuple-element.39), channel_id=1, source_target_pairs={{0,1},{1,0},{2,3},{3,2},{4,5},{5,4},{6,7},{7,6},{8,9},{9,8},{10,11... | collective-permute-start | bytes 968 | tf_op jit(solution)/shard_map/ppermute | solution.py:46
  1.8 6.5 %collective-permute-start.3 = (s32[2,40]{1,0:T(2,128)S(1)}, s32[2,40]{1,0:T(2,128)S(1)}, u32[]{:S(2)}, u32[]{:S(2)}) collective-permute-start(s32[2,40]{1,0:T(2,128)S(1)} %get-tuple-element.40), channel_id=1, source_target_pairs={{1,2},{2,1},{3,4},{4,3},{5,6},{6,5},{7,8},{8,7},{9,10},{10,9},{11,... | collective-permute-start | bytes 968 | tf_op jit(solution)/shard_map/ppermute | solution.py:46
  9.0 24.2 %collective-permute-start.4 = (bf16[32,8,8,128]{3,2,1,0:T(8,128)(2,1)S(1)}, bf16[32,8,8,128]{3,2,1,0:T(8,128)(2,1)S(1)}, u32[]{:S(2)}, u32[]{:S(2)}) collective-permute-start(bf16[32,8,8,128]{3,2,1,0:T(8,128)(2,1)S(1)} %get-tuple-element.41), channel_id=1, source_target_pairs={{0,1},{1,0},{2,3},{3,2},{4,5},{5,4},{6,7},{7,6},{8,9},{9,8},{10,11... | collective-permute-start | bytes 1572872 | tf_op jit(solution)/shard_map/ppermute | solution.py:46
  9.0 24.2 %collective-permute-start.5 = (bf16[32,8,8,128]{3,2,1,0:T(8,128)(2,1)S(1)}, bf16[32,8,8,128]{3,2,1,0:T(8,128)(2,1)S(1)}, u32[]{:S(2)}, u32[]{:S(2)}) collective-permute-start(bf16[32,8,8,128]{3,2,1,0:T(8,128)(2,1)S(1)} %get-tuple-element.42), channel_id=1, source_target_pairs={{1,2},{2,1},{3,4},{4,3},{5,6},{6,5},{7,8},{8,7},{9,10},{10,9},{11,... | collective-permute-start | bytes 1572872 | tf_op jit(solution)/shard_map/ppermute | solution.py:46
  13.3 3.1 %collective-permute-start = (bf16[2,3,16,8,128]{4,3,2,1,0:T(8,128)(2,1)S(1)}, bf16[2,3,16,8,128]{4,3,2,1,0:T(8,128)(2,1)S(1)}, u32[]{:S(2)}, u32[]{:S(2)}) collective-permute-start(bf16[2,3,16,8,128]{4,3,2,1,0:T(8,128)(2,1)S(1)} %get-tuple-element.34), channel_id=1, source_target_pairs={{0,1},{1,0},{2,3},{3,2},{4,5},{5,4},{6,7},{7,6},{8,9},{9,8},{10,11... | collective-permute-start | bytes 589832 | tf_op jit(solution)/shard_map/ppermute | solution.py:46
  13.4 15.9 %collective-permute-start.1 = (bf16[2,3,16,8,128]{4,3,2,1,0:T(8,128)(2,1)S(1)}, bf16[2,3,16,8,128]{4,3,2,1,0:T(8,128)(2,1)S(1)}, u32[]{:S(2)}, u32[]{:S(2)}) collective-permute-start(bf16[2,3,16,8,128]{4,3,2,1,0:T(8,128)(2,1)S(1)} %get-tuple-element.35), channel_id=1, source_target_pairs={{1,2},{2,1},{3,4},{4,3},{5,6},{6,5},{7,8},{8,7},{9,10},{10,9},{11,... | collective-permute-start | bytes 589832 | tf_op jit(solution)/shard_map/ppermute | solution.py:46
  34.1 10.1 %collective-permute-start.6 = (bf16[3,16,8,128]{3,2,1,0:T(8,128)(2,1)S(1)}, bf16[3,16,8,128]{3,2,1,0:T(8,128)(2,1)S(1)}, u32[]{:S(2)}, u32[]{:S(2)}) collective-permute-start(bf16[3,16,8,128]{3,2,1,0:T(8,128)(2,1)S(1)} %get-tuple-element.44), channel_id=1, source_target_pairs={{0,1},{1,0},{2,3},{3,2},{4,5},{5,4},{6,7},{7,6},{8,9},{9,8},{10,11... | collective-permute-start | bytes 294920 | tf_op jit(solution)/shard_map/ppermute | solution.py:46
  34.2 10.0 %collective-permute-start.7 = (bf16[3,16,8,128]{3,2,1,0:T(8,128)(2,1)S(1)}, bf16[3,16,8,128]{3,2,1,0:T(8,128)(2,1)S(1)}, u32[]{:S(2)}, u32[]{:S(2)}) collective-permute-start(bf16[3,16,8,128]{3,2,1,0:T(8,128)(2,1)S(1)} %get-tuple-element.45), channel_id=1, source_target_pairs={{1,2},{2,1},{3,4},{4,3},{5,6},{6,5},{7,8},{8,7},{9,10},{10,9},{11,... | collective-permute-start | bytes 294920 | tf_op jit(solution)/shard_map/ppermute | solution.py:46
  47.4 7.8 %collective-permute-start.8 = (bf16[32,8,8,128]{3,2,1,0:T(8,128)(2,1)S(1)}, bf16[32,8,8,128]{3,2,1,0:T(8,128)(2,1)S(1)}, u32[]{:S(2)}, u32[]{:S(2)}) collective-permute-start(bf16[32,8,8,128]{3,2,1,0:T(8,128)(2,1)S(1)} %get-tuple-element.54), channel_id=1, source_target_pairs={{0,1},{1,0},{2,3},{3,2},{4,5},{5,4},{6,7},{7,6},{8,9},{9,8},{10,11... | collective-permute-start | bytes 1572872 | tf_op jit(solution)/shard_map/ppermute | solution.py:46
  47.5 15.2 %collective-permute-start.9 = (bf16[32,8,8,128]{3,2,1,0:T(8,128)(2,1)S(1)}, bf16[32,8,8,128]{3,2,1,0:T(8,128)(2,1)S(1)}, u32[]{:S(2)}, u32[]{:S(2)}) collective-permute-start(bf16[32,8,8,128]{3,2,1,0:T(8,128)(2,1)S(1)} %get-tuple-element.55), channel_id=1, source_target_pairs={{1,2},{2,1},{3,4},{4,3},{5,6},{6,5},{7,8},{8,7},{9,10},{10,9},{11,... | collective-permute-start | bytes 1572872 | tf_op jit(solution)/shard_map/ppermute | solution.py:46
  63.6 10.1 %collective-permute-start.10 = (bf16[3,16,8,128]{3,2,1,0:T(8,128)(2,1)S(1)}, bf16[3,16,8,128]{3,2,1,0:T(8,128)(2,1)S(1)}, u32[]{:S(2)}, u32[]{:S(2)}) collective-permute-start(bf16[3,16,8,128]{3,2,1,0:T(8,128)(2,1)S(1)} %get-tuple-element.57), channel_id=1, source_target_pairs={{0,1},{1,0},{2,3},{3,2},{4,5},{5,4},{6,7},{7,6},{8,9},{9,8},{10,11... | collective-permute-start | bytes 294920 | tf_op jit(solution)/shard_map/ppermute | solution.py:46
  63.7 10.0 %collective-permute-start.11 = (bf16[3,16,8,128]{3,2,1,0:T(8,128)(2,1)S(1)}, bf16[3,16,8,128]{3,2,1,0:T(8,128)(2,1)S(1)}, u32[]{:S(2)}, u32[]{:S(2)}) collective-permute-start(bf16[3,16,8,128]{3,2,1,0:T(8,128)(2,1)S(1)} %get-tuple-element.58), channel_id=1, source_target_pairs={{1,2},{2,1},{3,4},{4,3},{5,6},{6,5},{7,8},{8,7},{9,10},{10,9},{11,... | collective-permute-start | bytes 294920 | tf_op jit(solution)/shard_map/ppermute | solution.py:46

commit v2 on v1

--- a/solution.py
+++ b/solution.py
@@ -38,18 +38,33 @@
     return pltpu.with_memory_space_constraint(x, pltpu.VMEM)
 
 
-def swap(x, axis, first):
-    size = lax.axis_size(axis)
-    pairs = []
-    for i in range(first, size - 1, 2):
-        pairs += [(i, i + 1), (i + 1, i)]
-    return lax.ppermute(x, axis, pairs)
+def neighbours(first):
+    clips, size = lax.axis_size("clips"), lax.axis_size("rows")
+    inside = [(i, i + 1) for i in range(first, size - 1, 2)]
+    pairs = [(c * size + i, c * size + j) for c in range(clips) for i, j in inside]
+    left = [i for i in range(size) if not any(i in pair for pair in inside)]
+    pairs += [(c * size + i, (c + 1) * size + i) for c in range(0, clips - 1, 2) for i in left]
+    return pairs + [(j, i) for i, j in pairs]
+
+
+def swap(x, first):
+    return lax.ppermute(x, ("clips", "rows"), neighbours(first))
 
 
 def swap_both(for_even, for_odd):
-    far = swap(for_odd, "rows", 1)
-    near = swap(for_even, "rows", 0)
+    far = swap(for_odd, 1)
+    near = swap(for_even, 0)
     return near, far
+
+
+def halo_row(near_row, far_row, even, exists, upper):
+    row = jnp.where(even, far_row, near_row) if upper else jnp.where(even, near_row, far_row)
+    return jnp.where(exists, row, jnp.zeros_like(row))
+
+
+def borders(place_ref, band):
+    mine = place_ref[0]
+    return lax.rem(mine, 2) == 0, mine > 0, (mine + 1) * band < place_ref[1]
 
 
 def tables_kernel(band, across, slots, place_ref, row_hbm, col_hbm, feat_hbm,
@@ -192,7 +207,7 @@
 def features_kernel(frame, place_ref, feat_hbm, near_ref, far_ref, w_ref, out_ref, feat_ref, x_ref, sem):
     rows, across, _, chans = feat_ref.shape
     cols = across * BLK
-    even = lax.rem(place_ref[0], 2) == 0
+    even, has_above, has_below = borders(place_ref, rows // BLK)
     size = rows // sem.shape[0]
     loads = []
     for n in range(sem.shape[0]):
@@ -201,9 +216,11 @@
         loads[-1].start()
     for row in range(-HALO, rows + HALO):
         if row < 0:
-            value = jnp.where(even, far_ref[frame, row + HALO], near_ref[frame, row + HALO])
+            n = row + HALO
+            value = halo_row(near_ref[frame, n], far_ref[frame, n], even, has_above, True)
         elif row >= rows:
-            value = jnp.where(even, near_ref[frame, row - rows], far_ref[frame, row - rows])
+            n = row - rows
+            value = halo_row(near_ref[frame, n], far_ref[frame, n], even, has_below, False)
         else:
             if row % size == 0:
                 loads[row // size].wait()
@@ -298,10 +315,7 @@
         x_ref, m_ref, d_ref, state_ref, sem = refs[8:]
     rows, across, _, chans = warped_ref.shape
     cols = across * BLK
-    mine = place_ref[0]
-    even = lax.rem(mine, 2) == 0
-    has_above = mine > 0
-    has_below = (mine + 1) * (rows // BLK) < place_ref[1]
+    even, has_above, has_below = borders(place_ref, rows // BLK)
     depth = 3 * chans
 
     def edge_dot(ref, side, w_ref):
@@ -312,8 +326,8 @@
         return value.astype(F32).reshape(cols, chans)
 
     for n in range(HALO):
-        above = jnp.where(even, far_ref[n], near_ref[n])
-        below = jnp.where(even, near_ref[n], far_ref[n])
+        above = halo_row(near_ref[n], far_ref[n], even, has_above, True)
+        below = halo_row(near_ref[n], far_ref[n], even, has_below, False)
         spread(x_ref.at[0], n // 2, n % 2, flat(above), cols)
         spread(x_ref.at[0], (n + 3) // 2, (n + 3) % 2, flat(warped_ref[n]), cols)
         spread(x_ref.at[1], n // 2, n % 2, flat(warped_ref[rows - HALO + n]), cols)

time: 77.3 us -> 68.1 us (0.88)
  starting transfers between devices: 24.8 us -> 13.4 us
  waiting for transfers between devices: 20.4 us -> 22.5 us
    ppermute x12, starting transfers between devices: 24.8 us -> 13.4 us  [swap(): return lax.ppermute(x, ('clips', 'rows'), neighbours(first))]
    ppermute x12, waiting for transfers between devices: 20.4 us -> 22.5 us  [swap(): return lax.ppermute(x, ('clips', 'rows'), neighbours(first))]
  transfers between devices with their start and end apart: 12 -> 12, of which waited for: 2 -> 3; matrix products, arithmetic and copies ran while one was open for 0% -> 0% of each run, Pallas kernels for 27% -> 31%
where the time goes in v2:
time: 68.1 us; the launch traced here: 67.9 us
  Pallas kernels  31.6 us (46%)
  waiting for transfers between devices  22.5 us (33%)
  starting transfers between devices  13.4 us (20%)
    ppermute x12, waiting for transfers between devices, swap(): return lax.ppermute(x, ('clips', 'rows'), neighbours(first))  22.5 us
    ppermute x12, starting transfers between devices, swap(): return lax.ppermute(x, ('clips', 'rows'), neighbours(first))  13.4 us
    pallas_call x2, Pallas kernels, on_device(): pl.pallas_call(functools.partial(inner_kernel, frame, last), out_shape=[o...  11.2 us
    pallas_call x2, Pallas kernels, features_part(): pl.pallas_call(functools.partial(features_kernel, frame), out_shape=on_ch...  7.91 us
    pallas_call x1, Pallas kernels, on_device(): pl.pallas_call(kernel, out_shape=[out_shape, pool_shape, message, message...  3.15 us
    pallas_call x1, Pallas kernels, on_device(): pl.pallas_call(kernel, out_shape=out_shape, in_specs=[SMEM] + [VMEM] * 9...  3.12 us
    pallas_call x2, Pallas kernels, on_device(): pl.pallas_call(functools.partial(assemble_kernel, frame), out_shape=[on_c...  2 us
    pallas_call x1, Pallas kernels, on_device(): pl.pallas_call(prepare_kernel, out_shape=[pair_shape] * 4 + [pool_shape],...  1.95 us
  transfers between devices with their start and end apart: 12, of which 3 were waited for; matrix products, arithmetic and copies ran while one was open for 0% of the time, Pallas kernels for 31%

profile of v2, /device:TPU:1, one launch (start us, length us, event | category | flops | bytes accessed | tf_op | source)
XLA Modules:
  0.0 67.9 jit_solution(10509660852288328621)
XLA Ops:
  0.0 0.1 pad_add_fusion.place_ref
  0.1 1.6 %tables.1 = (s32[2,64]{1,0:T(2,128)S(1)}, s32[2,40]{1,0:T(2,128)S(1)}, s32[2,40]{1,0:T(2,128)S(1)}, bf16[2,3,16,8,128]{4,3,2,1,0:T(8,128)(2,1)S(1)}, bf16[2,3,16,8,128]{4,3,2,1,0:T(8,128)(2,1)S(1)}) custom-call(s32[2]{0:T(128)S(1)} %pad_add_fusion.place_ref, s32[2,64]{1,0:T(2,128)} %row_hbm.1, s32[2,64]{1,0:T(2,128)} %col_hbm.1, ...), custom_call_target="tpu_custom_call" | custom-call | tf_op jit(solution)/shard_map/tables/pallas_call | solution.py:391
  1.7 0.1 collective-permute-start.2
  1.8 2.7 %collective-permute-start.3 = (s32[2,40]{1,0:T(2,128)S(1)}, s32[2,40]{1,0:T(2,128)S(1)}, u32[]{:S(2)}, u32[]{:S(2)}) collective-permute-start(s32[2,40]{1,0:T(2,128)S(1)} %get-tuple-element.40), channel_id=1, source_target_pairs={{1,2},{3,4},{5,6},{7,8},{9,10},{11,12},{13,14},{17,18},{19,20},{21... | collective-permute-start | bytes 968 | tf_op jit(solution)/shard_map/ppermute | solution.py:51
  4.5 1.9 %prepare.1 = (bf16[1536,256]{1,0:T(8,128)(2,1)S(1)}, bf16[1536,256]{1,0:T(8,128)(2,1)S(1)}, bf16[1536,256]{1,0:T(8,128)(2,1)S(1)}, bf16[1536,256]{1,0:T(8,128)(2,1)S(1)}, bf16[64,8,8,128]{3,2,1,0:T(8,128)(2,1)S(1)}) custom-call(bf16[3,3,256,128]{3,2,1,0:T(8,128)(2,1)} %merging_hbm.1, bf16[3,3,128,128]{3,2,1,0:T(8,128)(2,1)} %first_hbm.1, ...), custom_call_target="tpu_custom_call" | custom-call | tf_op jit(solution)/shard_map/prepare/pallas_call | solution.py:416
  6.5 0.6 pack.1
  7.1 0.4 collective-permute-start.4
  7.5 2.0 %collective-permute-start.5 = (bf16[32,8,8,128]{3,2,1,0:T(8,128)(2,1)S(1)}, bf16[32,8,8,128]{3,2,1,0:T(8,128)(2,1)S(1)}, u32[]{:S(2)}, u32[]{:S(2)}) collective-permute-start(bf16[32,8,8,128]{3,2,1,0:T(8,128)(2,1)S(1)} %get-tuple-element.42), channel_id=1, source_target_pairs={{1,2},{3,4},{5,6},{7,8},{9,10},{11,12},{13,14},{17,18},{19,20},{21... | collective-permute-start | bytes 1572872 | tf_op jit(solution)/shard_map/ppermute | solution.py:51
  9.5 1.3 %collective-permute-start.1 = (bf16[2,3,16,8,128]{4,3,2,1,0:T(8,128)(2,1)S(1)}, bf16[2,3,16,8,128]{4,3,2,1,0:T(8,128)(2,1)S(1)}, u32[]{:S(2)}, u32[]{:S(2)}) collective-permute-start(bf16[2,3,16,8,128]{4,3,2,1,0:T(8,128)(2,1)S(1)} %get-tuple-element.35), channel_id=1, source_target_pairs={{1,2},{3,4},{5,6},{7,8},{9,10},{11,12},{13,14},{17,18},{19,20},{21... | collective-permute-start | bytes 589832 | tf_op jit(solution)/shard_map/ppermute | solution.py:51
  10.8 0.2 collective-permute-done.near_ref
  11.0 14.5 %collective-permute-done.1.far_ref = bf16[2,3,16,8,128]{4,3,2,1,0:T(8,128)(2,1)S(1)} collective-permute-done((bf16[2,3,16,8,128]{4,3,2,1,0:T(8,128)(2,1)S(1)}, bf16[2,3,16,8,128]{4,3,2,1,0:T(8,128)(2,1)S(1)}, u32[]{:S(2)}, u32[]{:S(2)}) %collective-permute-start.1) | collective-permute-done | bytes 196640 | tf_op jit(solution)/shard_map/ppermute | solution.py:51
  25.5 4.0 %features.3._.part_ref = f32[18,128,256]{2,1,0:T(8,128)S(1)} custom-call(s32[2]{0:T(128)S(1)} %pad_add_fusion.place_ref, bf16[2,32,16,8,128]{4,3,2,1,0:T(8,128)(2,1)} %bitcast.5, bf16[2,3,16,8,128]{4,3,2,1,0:T(8,128)(2,1)S(1)} %collective-permute-done.near_ref, bf16[2,3,16,8,128]{4,3,2,1,0:T(8,128)(2,1)S(1)} %collective-permute-done.1.far_ref, ...), custom_call_target="tpu_custom_call" | custom-call | tf_op jit(solution)/shard_map/features/pallas_call | solution.py:444
  29.5 0.9 %assemble.2 = (bf16[32,16,8,128]{3,2,1,0:T(8,128)(2,1)S(1)}, bf16[3,16,8,128]{3,2,1,0:T(8,128)(2,1)S(1)}, bf16[3,16,8,128]{3,2,1,0:T(8,128)(2,1)S(1)}) custom-call(s32[2]{0:T(128)S(1)} %pad_add_fusion.place_ref, s32[2,64]{1,0:T(2,128)S(1)} %get-tuple-element.37.table_ref, bf16[64,8,8,128]{3,2,1,0:T(8,128)(2,1)S(1)} %get-tuple-element.38.pool_ref, ...), custom_call_target="tpu_custom_call" | custom-call | tf_op jit(solution)/shard_map/assemble/pallas_call | solution.py:465
  30.4 2.5 %collective-permute-start.7 = (bf16[3,16,8,128]{3,2,1,0:T(8,128)(2,1)S(1)}, bf16[3,16,8,128]{3,2,1,0:T(8,128)(2,1)S(1)}, u32[]{:S(2)}, u32[]{:S(2)}) collective-permute-start(bf16[3,16,8,128]{3,2,1,0:T(8,128)(2,1)S(1)} %get-tuple-element.45), channel_id=1, source_target_pairs={{1,2},{3,4},{5,6},{7,8},{9,10},{11,12},{13,14},{17,18},{19,20},{21... | collective-permute-start | bytes 294920 | tf_op jit(solution)/shard_map/ppermute | solution.py:51
  33.0 5.6 %inner.2 = (bf16[2,32,16,8,128]{4,3,2,1,0:T(8,128)(2,1)}, bf16[64,8,8,128]{3,2,1,0:T(8,128)(2,1)S(1)}, bf16[2,2,128,384]{3,2,1,0:T(8,128)(2,1)S(1)}, bf16[2,2,128,384]{3,2,1,0:T(8,128)(2,1)S(1)}) custom-call(f32[18,128,256]{2,1,0:T(8,128)S(1)} %features.3._.part_ref, bf16[32,16,8,128]{3,2,1,0:T(8,128)(2,1)S(1)} %get-tuple-element.43.warped_ref, ...), custom_call_target="tpu_custom_call" | custom-call | tf_op jit(solution)/shard_map/inner/pallas_call | solution.py:476
  38.6 3.1 %border.2 = (bf16[2,32,16,8,128]{4,3,2,1,0:T(8,128)(2,1)}, bf16[64,8,8,128]{3,2,1,0:T(8,128)(2,1)S(1)}, bf16[32,8,8,128]{3,2,1,0:T(8,128)(2,1)S(1)}, bf16[32,8,8,128]{3,2,1,0:T(8,128)(2,1)S(1)}) custom-call(s32[2]{0:T(128)S(1)} %pad_add_fusion.place_ref, f32[18,128,256]{2,1,0:T(8,128)S(1)} %features.3._.part_ref, ...), custom_call_target="tpu_custom_call", output_to_operand_aliasing={{0}: (10, {}), {1}: (11, {})} | custom-call | tf_op jit(solution)/shard_map/border/pallas_call | solution.py:514
  41.9 1.6 %collective-permute-start.9 = (bf16[32,8,8,128]{3,2,1,0:T(8,128)(2,1)S(1)}, bf16[32,8,8,128]{3,2,1,0:T(8,128)(2,1)S(1)}, u32[]{:S(2)}, u32[]{:S(2)}) collective-permute-start(bf16[32,8,8,128]{3,2,1,0:T(8,128)(2,1)S(1)} %get-tuple-element.55), channel_id=1, source_target_pairs={{1,2},{3,4},{5,6},{7,8},{9,10},{11,12},{13,14},{17,18},{19,20},{21... | collective-permute-start | bytes 1572872 | tf_op jit(solution)/shard_map/ppermute | solution.py:51
  43.5 4.0 %features.2._.part_ref = f32[18,128,256]{2,1,0:T(8,128)S(1)} custom-call(s32[2]{0:T(128)S(1)} %pad_add_fusion.place_ref, bf16[2,32,16,8,128]{4,3,2,1,0:T(8,128)(2,1)} %bitcast.6, bf16[2,3,16,8,128]{4,3,2,1,0:T(8,128)(2,1)S(1)} %collective-permute-done.near_ref, bf16[2,3,16,8,128]{4,3,2,1,0:T(8,128)(2,1)S(1)} %collective-permute-done.1.far_ref, ...), custom_call_target="tpu_custom_call" | custom-call | tf_op jit(solution)/shard_map/features/pallas_call | solution.py:444
  47.5 7.8 %collective-permute-done.9.far_ref = bf16[32,8,8,128]{3,2,1,0:T(8,128)(2,1)S(1)} collective-permute-done((bf16[32,8,8,128]{3,2,1,0:T(8,128)(2,1)S(1)}, bf16[32,8,8,128]{3,2,1,0:T(8,128)(2,1)S(1)}, u32[]{:S(2)}, u32[]{:S(2)}) %collective-permute-start.9) | collective-permute-done | bytes 524320 | tf_op jit(solution)/shard_map/ppermute | solution.py:51
  55.2 1.1 %assemble.3 = (bf16[32,16,8,128]{3,2,1,0:T(8,128)(2,1)S(1)}, bf16[3,16,8,128]{3,2,1,0:T(8,128)(2,1)S(1)}, bf16[3,16,8,128]{3,2,1,0:T(8,128)(2,1)S(1)}) custom-call(s32[2]{0:T(128)S(1)} %pad_add_fusion.place_ref, s32[2,64]{1,0:T(2,128)S(1)} %get-tuple-element.37.table_ref, bf16[64,8,8,128]{3,2,1,0:T(8,128)(2,1)S(1)} %get-tuple-element.53.pool_ref, ...), custom_call_target="tpu_custom_call" | custom-call | tf_op jit(solution)/shard_map/assemble/pallas_call | solution.py:465
  56.3 0.1 collective-permute-start.10
  56.4 2.5 %collective-permute-start.11 = (bf16[3,16,8,128]{3,2,1,0:T(8,128)(2,1)S(1)}, bf16[3,16,8,128]{3,2,1,0:T(8,128)(2,1)S(1)}, u32[]{:S(2)}, u32[]{:S(2)}) collective-permute-start(bf16[3,16,8,128]{3,2,1,0:T(8,128)(2,1)S(1)} %get-tuple-element.58), channel_id=1, source_target_pairs={{1,2},{3,4},{5,6},{7,8},{9,10},{11,12},{13,14},{17,18},{19,20},{21... | collective-permute-start | bytes 294920 | tf_op jit(solution)/shard_map/ppermute | solution.py:51
  59.0 5.6 %inner.3 = (bf16[2,32,16,8,128]{4,3,2,1,0:T(8,128)(2,1)}, bf16[2,2,128,384]{3,2,1,0:T(8,128)(2,1)S(1)}, bf16[2,2,128,384]{3,2,1,0:T(8,128)(2,1)S(1)}) custom-call(f32[18,128,256]{2,1,0:T(8,128)S(1)} %features.2._.part_ref, bf16[32,16,8,128]{3,2,1,0:T(8,128)(2,1)S(1)} %get-tuple-element.56.warped_ref, ...), custom_call_target="tpu_custom_call", output_to_operand_aliasing={{0}: (5, {})} | custom-call | tf_op jit(solution)/shard_map/inner/pallas_call | solution.py:476
  64.6 3.1 %border.3 = bf16[2,32,16,8,128]{4,3,2,1,0:T(8,128)(2,1)} custom-call(s32[2]{0:T(128)S(1)} %pad_add_fusion.place_ref, f32[18,128,256]{2,1,0:T(8,128)S(1)} %features.2._.part_ref, bf16[32,16,8,128]{3,2,1,0:T(8,128)(2,1)S(1)} %get-tuple-element.56.warped_ref, ...), custom_call_target="tpu_custom_call", output_to_operand_aliasing={{}: (10, {})} | custom-call | tf_op jit(solution)/shard_map/border/pallas_call | solution.py:503
  (12 shorter events, 0.2 us)
Async XLA Ops:
  1.7 4.7 %collective-permute-start.2 = (s32[2,40]{1,0:T(2,128)S(1)}, s32[2,40]{1,0:T(2,128)S(1)}, u32[]{:S(2)}, u32[]{:S(2)}) collective-permute-start(s32[2,40]{1,0:T(2,128)S(1)} %get-tuple-element.39), channel_id=1, source_target_pairs={{0,1},{2,3},{4,5},{6,7},{8,9},{10,11},{12,13},{14,15},{16,17},{18,... | collective-permute-start | bytes 968 | tf_op jit(solution)/shard_map/ppermute | solution.py:51
  1.8 4.6 %collective-permute-start.3 = (s32[2,40]{1,0:T(2,128)S(1)}, s32[2,40]{1,0:T(2,128)S(1)}, u32[]{:S(2)}, u32[]{:S(2)}) collective-permute-start(s32[2,40]{1,0:T(2,128)S(1)} %get-tuple-element.40), channel_id=1, source_target_pairs={{1,2},{3,4},{5,6},{7,8},{9,10},{11,12},{13,14},{17,18},{19,20},{21... | collective-permute-start | bytes 968 | tf_op jit(solution)/shard_map/ppermute | solution.py:51
  7.1 22.3 %collective-permute-start.4 = (bf16[32,8,8,128]{3,2,1,0:T(8,128)(2,1)S(1)}, bf16[32,8,8,128]{3,2,1,0:T(8,128)(2,1)S(1)}, u32[]{:S(2)}, u32[]{:S(2)}) collective-permute-start(bf16[32,8,8,128]{3,2,1,0:T(8,128)(2,1)S(1)} %get-tuple-element.41), channel_id=1, source_target_pairs={{0,1},{2,3},{4,5},{6,7},{8,9},{10,11},{12,13},{14,15},{16,17},{18,... | collective-permute-start | bytes 1572872 | tf_op jit(solution)/shard_map/ppermute | solution.py:51
  7.5 21.9 %collective-permute-start.5 = (bf16[32,8,8,128]{3,2,1,0:T(8,128)(2,1)S(1)}, bf16[32,8,8,128]{3,2,1,0:T(8,128)(2,1)S(1)}, u32[]{:S(2)}, u32[]{:S(2)}) collective-permute-start(bf16[32,8,8,128]{3,2,1,0:T(8,128)(2,1)S(1)} %get-tuple-element.42), channel_id=1, source_target_pairs={{1,2},{3,4},{5,6},{7,8},{9,10},{11,12},{13,14},{17,18},{19,20},{21... | collective-permute-start | bytes 1572872 | tf_op jit(solution)/shard_map/ppermute | solution.py:51
  9.5 1.4 %collective-permute-start = (bf16[2,3,16,8,128]{4,3,2,1,0:T(8,128)(2,1)S(1)}, bf16[2,3,16,8,128]{4,3,2,1,0:T(8,128)(2,1)S(1)}, u32[]{:S(2)}, u32[]{:S(2)}) collective-permute-start(bf16[2,3,16,8,128]{4,3,2,1,0:T(8,128)(2,1)S(1)} %get-tuple-element.34), channel_id=1, source_target_pairs={{0,1},{2,3},{4,5},{6,7},{8,9},{10,11},{12,13},{14,15},{16,17},{18,... | collective-permute-start | bytes 589832 | tf_op jit(solution)/shard_map/ppermute | solution.py:51
  9.5 16.0 %collective-permute-start.1 = (bf16[2,3,16,8,128]{4,3,2,1,0:T(8,128)(2,1)S(1)}, bf16[2,3,16,8,128]{4,3,2,1,0:T(8,128)(2,1)S(1)}, u32[]{:S(2)}, u32[]{:S(2)}) collective-permute-start(bf16[2,3,16,8,128]{4,3,2,1,0:T(8,128)(2,1)S(1)} %get-tuple-element.35), channel_id=1, source_target_pairs={{1,2},{3,4},{5,6},{7,8},{9,10},{11,12},{13,14},{17,18},{19,20},{21... | collective-permute-start | bytes 589832 | tf_op jit(solution)/shard_map/ppermute | solution.py:51
  30.4 8.3 %collective-permute-start.6 = (bf16[3,16,8,128]{3,2,1,0:T(8,128)(2,1)S(1)}, bf16[3,16,8,128]{3,2,1,0:T(8,128)(2,1)S(1)}, u32[]{:S(2)}, u32[]{:S(2)}) collective-permute-start(bf16[3,16,8,128]{3,2,1,0:T(8,128)(2,1)S(1)} %get-tuple-element.44), channel_id=1, source_target_pairs={{0,1},{2,3},{4,5},{6,7},{8,9},{10,11},{12,13},{14,15},{16,17},{18,... | collective-permute-start | bytes 294920 | tf_op jit(solution)/shard_map/ppermute | solution.py:51
  30.4 8.2 %collective-permute-start.7 = (bf16[3,16,8,128]{3,2,1,0:T(8,128)(2,1)S(1)}, bf16[3,16,8,128]{3,2,1,0:T(8,128)(2,1)S(1)}, u32[]{:S(2)}, u32[]{:S(2)}) collective-permute-start(bf16[3,16,8,128]{3,2,1,0:T(8,128)(2,1)S(1)} %get-tuple-element.45), channel_id=1, source_target_pairs={{1,2},{3,4},{5,6},{7,8},{9,10},{11,12},{13,14},{17,18},{19,20},{21... | collective-permute-start | bytes 294920 | tf_op jit(solution)/shard_map/ppermute | solution.py:51
  41.8 5.7 %collective-permute-start.8 = (bf16[32,8,8,128]{3,2,1,0:T(8,128)(2,1)S(1)}, bf16[32,8,8,128]{3,2,1,0:T(8,128)(2,1)S(1)}, u32[]{:S(2)}, u32[]{:S(2)}) collective-permute-start(bf16[32,8,8,128]{3,2,1,0:T(8,128)(2,1)S(1)} %get-tuple-element.54), channel_id=1, source_target_pairs={{0,1},{2,3},{4,5},{6,7},{8,9},{10,11},{12,13},{14,15},{16,17},{18,... | collective-permute-start | bytes 1572872 | tf_op jit(solution)/shard_map/ppermute | solution.py:51
  41.9 13.4 %collective-permute-start.9 = (bf16[32,8,8,128]{3,2,1,0:T(8,128)(2,1)S(1)}, bf16[32,8,8,128]{3,2,1,0:T(8,128)(2,1)S(1)}, u32[]{:S(2)}, u32[]{:S(2)}) collective-permute-start(bf16[32,8,8,128]{3,2,1,0:T(8,128)(2,1)S(1)} %get-tuple-element.55), channel_id=1, source_target_pairs={{1,2},{3,4},{5,6},{7,8},{9,10},{11,12},{13,14},{17,18},{19,20},{21... | collective-permute-start | bytes 1572872 | tf_op jit(solution)/shard_map/ppermute | solution.py:51
  56.3 8.2 %collective-permute-start.10 = (bf16[3,16,8,128]{3,2,1,0:T(8,128)(2,1)S(1)}, bf16[3,16,8,128]{3,2,1,0:T(8,128)(2,1)S(1)}, u32[]{:S(2)}, u32[]{:S(2)}) collective-permute-start(bf16[3,16,8,128]{3,2,1,0:T(8,128)(2,1)S(1)} %get-tuple-element.57), channel_id=1, source_target_pairs={{0,1},{2,3},{4,5},{6,7},{8,9},{10,11},{12,13},{14,15},{16,17},{18,... | collective-permute-start | bytes 294920 | tf_op jit(solution)/shard_map/ppermute | solution.py:51
  56.4 8.2 %collective-permute-start.11 = (bf16[3,16,8,128]{3,2,1,0:T(8,128)(2,1)S(1)}, bf16[3,16,8,128]{3,2,1,0:T(8,128)(2,1)S(1)}, u32[]{:S(2)}, u32[]{:S(2)}) collective-permute-start(bf16[3,16,8,128]{3,2,1,0:T(8,128)(2,1)S(1)} %get-tuple-element.58), channel_id=1, source_target_pairs={{1,2},{3,4},{5,6},{7,8},{9,10},{11,12},{13,14},{17,18},{19,20},{21... | collective-permute-start | bytes 294920 | tf_op jit(solution)/shard_map/ppermute | solution.py:51

commit v3 on v2

--- a/solution.py
+++ b/solution.py
@@ -62,17 +62,17 @@
     return jnp.where(exists, row, jnp.zeros_like(row))
 
 
-def borders(place_ref, band):
-    mine = place_ref[0]
-    return lax.rem(mine, 2) == 0, mine > 0, (mine + 1) * band < place_ref[1]
-
-
-def tables_kernel(band, across, slots, place_ref, row_hbm, col_hbm, feat_hbm,
-                  table_ref, near_ref, far_ref, near_edge, far_edge, row_ref, col_ref, sem):
+def borders():
+    mine = lax.axis_index("rows")
+    return lax.rem(mine, 2) == 0, mine > 0, mine < lax.axis_size("rows") - 1
+
+
+def tables_kernel(band, across, slots, row_hbm, col_hbm, feat_hbm, state_hbm,
+                  table_ref, near_ref, far_ref, near_edge, far_edge, pool_ref, row_ref, col_ref, sem):
     frames, blocks = row_ref.shape
     rows = feat_hbm.shape[1]
-    mine = place_ref[0]
-    total = place_ref[1]
+    mine = lax.axis_index("rows")
+    total = band * lax.axis_size("rows")
     even = lax.rem(mine, 2) == 0
     moves = [
         pltpu.make_async_copy(row_hbm, row_ref, sem.at[0]),
@@ -81,11 +81,16 @@
     near_rows = pl.ds(jnp.where(even, rows - HALO, 0), HALO)
     far_rows = pl.ds(jnp.where(even, 0, rows - HALO), HALO)
     edges = [
-        pltpu.make_async_copy(feat_hbm.at[:, near_rows], near_edge, sem.at[2]),
-        pltpu.make_async_copy(feat_hbm.at[:, far_rows], far_edge, sem.at[3]),
+        pltpu.make_async_copy(feat_hbm.at[0, near_rows], near_edge, sem.at[2]),
+        pltpu.make_async_copy(feat_hbm.at[0, far_rows], far_edge, sem.at[3]),
     ]
     for copy in moves + edges:
         copy.start()
+    for q in range(band):
+        for r in range(BLK):
+            pltpu.make_async_copy(
+                state_hbm.at[q, r], pool_ref.at[pl.ds(q * across, across), r], sem.at[4]
+            ).start()
     for copy in moves:
         copy.wait()
     block = lax.broadcasted_iota(jnp.int32, (frames, blocks), 1)
@@ -123,17 +128,11 @@
             out[frame:frame + 1] = got.astype(jnp.int32)
     for copy in edges:
         copy.wait()
-
-
-def prepare_kernel(merging_hbm, first_hbm, second_hbm, state_hbm,
-                   feat_out, warp_out, first_out, second_out, pool_out,
-                   merging_ref, first_ref, second_ref, sem):
-    band, _, across = state_hbm.shape[:3]
-    for q in range(band):
-        for r in range(BLK):
-            pltpu.make_async_copy(
-                state_hbm.at[q, r], pool_out.at[pl.ds(q * across, across), r], sem.at[3]
-            ).start()
+    pltpu.make_async_copy(pool_ref, pool_ref, sem.at[4]).wait()
+
+
+def weights_kernel(merging_hbm, first_hbm, second_hbm, _,
+                   feat_out, warp_out, first_out, second_out, merging_ref, first_ref, second_ref, sem):
     loads = [
         pltpu.make_async_copy(merging_hbm, merging_ref, sem.at[0]),
         pltpu.make_async_copy(first_hbm, first_ref, sem.at[1]),
@@ -163,7 +162,6 @@
                     else:
                         value = zero
                     out[top:top + chans, half * width:(half + 1) * width] = value
-    pltpu.make_async_copy(pool_out, pool_out, sem.at[3]).wait()
 
 
 def pack(pool_ref, near_list, far_list, frame, near_out, far_out):
@@ -176,16 +174,25 @@
     pack(pool_ref, near_list, far_list, frame, near_out, far_out)
 
 
-def spread(out_ref, pair, half, value, cols):
-    chans = value.shape[1]
-    pairs = value.shape[0] // cols
-    place = lax.broadcasted_iota(jnp.int32, (pairs, cols, chans), 1).reshape(value.shape)
-    left = jnp.where(place == 0, 0.0, pltpu.roll(value, 1, 0))
-    right = jnp.where(place == cols - 1, 0.0, pltpu.roll(value, value.shape[0] - 1, 0))
-    for e, part in enumerate((left, value, right)):
-        out_ref[pair:pair + pairs, half, :, e * chans:(e + 1) * chans] = (
-            part.astype(BF16).reshape(pairs, cols, chans)
-        )
+def shifter(pad_ref):
+    slots, length, chans = pad_ref.shape
+    cols = length - 2 * BLK
+    edge = jnp.zeros((BLK, chans), F32)
+    for slot in range(slots):
+        pad_ref[slot, 0:BLK] = edge
+        pad_ref[slot, BLK + cols:length] = edge
+    turn = [0]
+
+    def spread(out_ref, pair, half, value):
+        slot = turn[0] % slots
+        turn[0] += 1
+        pad_ref[slot, BLK:BLK + cols] = value
+        left = pad_ref[slot, BLK - 1:BLK - 1 + cols]
+        right = pad_ref[slot, BLK + 1:BLK + 1 + cols]
+        for e, part in enumerate((left, value, right)):
+            out_ref[pair, half, :, e * chans:(e + 1) * chans] = part.astype(BF16)
+
+    return spread
 
 
 def pair_dot(x_ref, w_ref, pair, pairs):
@@ -204,51 +211,62 @@
     return [(a, b - a) for a, b in zip(bounds, bounds[1:])]
 
 
-def features_kernel(frame, place_ref, feat_hbm, near_ref, far_ref, w_ref, out_ref, feat_ref, x_ref, sem):
+def features_kernel(frame, feat_hbm, near_ref, far_ref, w_ref, out_ref, *refs):
+    feat_ref, x_ref, pad_ref, sem, edge_sem = refs[-5:]
     rows, across, _, chans = feat_ref.shape
     cols = across * BLK
-    even, has_above, has_below = borders(place_ref, rows // BLK)
+    even, has_above, has_below = borders()
     size = rows // sem.shape[0]
+    spread = shifter(pad_ref)
     loads = []
     for n in range(sem.shape[0]):
         part = pl.ds(n * size, size)
         loads.append(pltpu.make_async_copy(feat_hbm.at[frame, part], feat_ref.at[part], sem.at[n]))
         loads[-1].start()
+    starts = (jnp.where(even, rows - HALO, 0), jnp.where(even, 0, rows - HALO))
+    for n, edge in enumerate(refs[:-5]):
+        part = pl.ds(starts[n], HALO)
+        loads.append(pltpu.make_async_copy(feat_hbm.at[frame + 1, part], edge, edge_sem.at[n]))
+        loads[-1].start()
     for row in range(-HALO, rows + HALO):
         if row < 0:
-            n = row + HALO
-            value = halo_row(near_ref[frame, n], far_ref[frame, n], even, has_above, True)
+            n = row + near_ref.shape[0]
+            value = halo_row(near_ref[n], far_ref[n], even, has_above, True)
         elif row >= rows:
-            n = row - rows
-            value = halo_row(near_ref[frame, n], far_ref[frame, n], even, has_below, False)
+            n = row - rows + near_ref.shape[0] - HALO
+            value = halo_row(near_ref[n], far_ref[n], even, has_below, False)
         else:
             if row % size == 0:
                 loads[row // size].wait()
             value = feat_ref[row]
         value = value.astype(F32).reshape(cols, chans)
-        spread(x_ref, (row + HALO) // 2, (row + HALO) % 2, value, cols)
+        spread(x_ref, (row + HALO) // 2, (row + HALO) % 2, value)
     for pair, pairs in chunks(0, rows // 2 + 2, STEP):
         out_ref[pair:pair + pairs] = pair_dot(x_ref, w_ref, pair, pairs).reshape(
             pairs, cols, out_ref.shape[2]
         )
-
-
-def assemble_kernel(frame, place_ref, table_ref, pool_ref, near_ref, far_ref, _,
-                    warped_out, near_edge, far_edge, all_ref):
+    for load in loads[sem.shape[0]:]:
+        load.wait()
+
+
+def assemble_kernel(frame, table_ref, pool_ref, near_ref, far_ref, _, *refs):
+    warped_out, near_edge, far_edge, all_ref = refs[-4:]
     rows, across = warped_out.shape[:2]
     blocks = pool_ref.shape[0]
     slots = near_ref.shape[0]
+    odd = lax.rem(lax.axis_index("rows"), 2)
+    near_rows = pl.ds(jnp.where(odd == 0, rows - HALO, 0), HALO)
+    far_rows = pl.ds(jnp.where(odd == 0, 0, rows - HALO), HALO)
+    for edge, feat_edge in zip((near_edge, far_edge), refs[:-4]):
+        edge[HALO:2 * HALO] = feat_edge[...]
     all_ref[0:blocks] = pool_ref[...]
     all_ref[blocks:blocks + slots] = near_ref[...]
     all_ref[blocks + slots:blocks + 2 * slots] = far_ref[...]
     for block in range(blocks):
         q, p = divmod(block, across)
         warped_out[q * BLK:(q + 1) * BLK, p] = all_ref[table_ref[frame, block]]
-    odd = lax.rem(place_ref[0], 2)
-    near_start = jnp.where(odd == 0, rows - HALO, 0)
-    far_start = jnp.where(odd == 0, 0, rows - HALO)
-    near_edge[...] = warped_out[pl.ds(near_start, HALO)]
-    far_edge[...] = warped_out[pl.ds(far_start, HALO)]
+    near_edge[0:HALO] = warped_out[near_rows]
+    far_edge[0:HALO] = warped_out[far_rows]
 
 
 def split_rows(value, pairs, cols, chans):
@@ -270,25 +288,26 @@
         refs = refs[1:]
     out_ref = refs[0]
     pool_ref = None if last else refs[1]
-    m_edge, d_edge, x_ref, m_ref, d_ref, state_ref, sem = refs[-7:]
+    m_edge, d_edge, x_ref, m_ref, d_ref, pad_ref, state_ref, sem = refs[-8:]
+    spread = shifter(pad_ref)
     rows, across, _, chans = warped_ref.shape
     cols = across * BLK
     half_rows = rows // 2
     for row in range(rows):
         value = warped_ref[row].astype(F32).reshape(cols, chans)
-        spread(x_ref, (row + HALO) // 2, (row + HALO) % 2, value, cols)
+        spread(x_ref, (row + HALO) // 2, (row + HALO) % 2, value)
     for pair, pairs in chunks(2, half_rows, STEP):
         raw = part_ref[pair:pair + pairs].reshape(pairs * cols, 2 * chans)
         raw = raw + pair_dot(x_ref, w1_ref, pair, pairs)
         value = jnp.maximum(raw, 0.1 * raw)
         for n, half, one in split_rows(value, pairs, cols, chans):
-            spread(m_ref, pair + n, half, one, cols)
+            spread(m_ref, pair + n, half, one)
     m_edge[0] = m_ref[2]
     m_edge[1] = m_ref[half_rows - 1]
     for pair, pairs in chunks(2, half_rows - 1, STEP):
         value = jnp.maximum(pair_dot(m_ref, w2_ref, pair, pairs), 0.0)
         for n, half, one in split_rows(value, pairs, cols, chans):
-            spread(d_ref, pair + n, half, one, cols)
+            spread(d_ref, pair + n, half, one)
     d_edge[0] = d_ref[2]
     d_edge[1] = d_ref[half_rows - 2]
     for pair, pairs in chunks(2, half_rows - 2, STEP):
@@ -305,17 +324,18 @@
     pltpu.make_async_copy(state_ref.at[inner], out_ref.at[frame, inner], sem).wait()
 
 
-def border_kernel(frame, last, place_ref, part_ref, warped_ref, near_ref, far_ref, w1_ref, w2_ref, w3_ref,
+def border_kernel(frame, last, part_ref, warped_ref, near_ref, far_ref, w1_ref, w2_ref, w3_ref,
                   m_edge, d_edge, *refs):
     if last:
-        _, out_ref, x_ref, m_ref, d_ref, state_ref, sem = refs
+        _, out_ref, x_ref, m_ref, d_ref, pad_ref, state_ref, sem = refs
         pool_ref = None
     else:
         _, _, near_list, far_list, out_ref, pool_ref, near_out, far_out = refs[:8]
-        x_ref, m_ref, d_ref, state_ref, sem = refs[8:]
+        x_ref, m_ref, d_ref, pad_ref, state_ref, sem = refs[8:]
+    spread = shifter(pad_ref)
     rows, across, _, chans = warped_ref.shape
     cols = across * BLK
-    even, has_above, has_below = borders(place_ref, rows // BLK)
+    even, has_above, has_below = borders()
     depth = 3 * chans
 
     def edge_dot(ref, side, w_ref):
@@ -328,10 +348,10 @@
     for n in range(HALO):
         above = halo_row(near_ref[n], far_ref[n], even, has_above, True)
         below = halo_row(near_ref[n], far_ref[n], even, has_below, False)
-        spread(x_ref.at[0], n // 2, n % 2, flat(above), cols)
-        spread(x_ref.at[0], (n + 3) // 2, (n + 3) % 2, flat(warped_ref[n]), cols)
-        spread(x_ref.at[1], n // 2, n % 2, flat(warped_ref[rows - HALO + n]), cols)
-        spread(x_ref.at[1], (n + 3) // 2, (n + 3) % 2, flat(below), cols)
+        spread(x_ref.at[0], n // 2, n % 2, flat(above))
+        spread(x_ref.at[0], (n + 3) // 2, (n + 3) % 2, flat(warped_ref[n]))
+        spread(x_ref.at[1], n // 2, n % 2, flat(warped_ref[rows - HALO + n]))
+        spread(x_ref.at[1], (n + 3) // 2, (n + 3) % 2, flat(below))
     half_rows = rows // 2
 
     def masked(value, row):
@@ -349,13 +369,13 @@
         value = jnp.maximum(raw, 0.1 * raw)
         for n, half, one in split_rows(value, 2, cols, chans):
             one = masked(one, 2 * (first + n) + half - 2)
-            spread(m_ref.at[side], n + side, half, one, cols)
+            spread(m_ref.at[side], n + side, half, one)
     for side in range(2):
         first = side * (half_rows - 1)
         value = jnp.maximum(edge_dot(m_ref, side, w2_ref), 0.0)
         for n, half, one in split_rows(value, 2, cols, chans):
             one = masked(one, 2 * (first + n) + half - 1)
-            spread(d_ref.at[side], n + side, half, one, cols)
+            spread(d_ref.at[side], n + side, half, one)
     for side in range(2):
         first = side * (half_rows - 2)
         value = edge_dot(d_ref, side, w3_ref)
@@ -381,52 +401,35 @@
     blocks = band * across
     slots = blocks // 2
     list_len = slots + 8
-    mine = lax.axis_index("rows")
-    place = jnp.stack([mine, jnp.int32(band * lax.axis_size("rows"))]).astype(jnp.int32)
     state = state_start.reshape(band, BLK, across, BLK, chans)
     feats = features.reshape(frames, rows, across, BLK, chans)
     block_shape = (BLK, BLK, chans)
     edge_shape = (HALO, across, BLK, chans)
-
-    table, near_list, far_list, near_feat, far_feat = pl.pallas_call(
+    pool_shape = on_chip((blocks,) + block_shape)
+    message = on_chip((slots,) + block_shape)
+
+    table, near_list, far_list, near_feat, far_feat, pool = pl.pallas_call(
         functools.partial(tables_kernel, band, across, slots),
         out_shape=[
             on_chip((frames, blocks), jnp.int32),
             on_chip((frames, list_len), jnp.int32),
             on_chip((frames, list_len), jnp.int32),
-            on_chip((frames,) + edge_shape),
-            on_chip((frames,) + edge_shape),
+            on_chip(edge_shape),
+            on_chip(edge_shape),
+            pool_shape,
         ],
-        in_specs=[SMEM, ANY, ANY, ANY],
-        out_specs=[VMEM] * 5,
+        in_specs=[ANY] * 4,
+        out_specs=[VMEM] * 6,
         scratch_shapes=[
             pltpu.VMEM((frames, blocks), jnp.int32),
             pltpu.VMEM((frames, blocks), jnp.int32),
-            pltpu.SemaphoreType.DMA((4,)),
+            pltpu.SemaphoreType.DMA((5,)),
         ],
         compiler_params=room(4),
         name="tables",
-    )(place, *map(in_hbm, (row_moves, col_moves, feats)))
+    )(*map(in_hbm, (row_moves, col_moves, feats, state)))
     near_list, far_list = swap_both(near_list, far_list)
     near_feat, far_feat = swap_both(near_feat, far_feat)
-
-    pair_shape = on_chip((4 * 3 * chans, 2 * chans))
-    pool_shape = on_chip((blocks,) + block_shape)
-    message = on_chip((slots,) + block_shape)
-    w_feat, w_warp, w_first, w_second, pool = pl.pallas_call(
-        prepare_kernel,
-        out_shape=[pair_shape] * 4 + [pool_shape],
-        in_specs=[ANY] * 4,
-        out_specs=[VMEM] * 5,
-        scratch_shapes=[
-            pltpu.VMEM(merging_weight.shape, BF16),
-            pltpu.VMEM(first_weight.shape, BF16),
-            pltpu.VMEM(second_weight.shape, BF16),
-            pltpu.SemaphoreType.DMA((4,)),
-        ],
-        compiler_params=room(4),
-        name="prepare",
-    )(*map(in_hbm, (merging_weight, first_weight, second_weight, state)))
 
     near_msg, far_msg = pl.pallas_call(
         functools.partial(pack_kernel, 0),
@@ -437,23 +440,44 @@
         name="pack",
     )(resident(pool), near_list, far_list)
 
+    pair_shape = on_chip((4 * 3 * chans, 2 * chans))
+    w_feat, w_warp, w_first, w_second = pl.pallas_call(
+        weights_kernel,
+        out_shape=[pair_shape] * 4,
+        in_specs=[ANY] * 4,
+        out_specs=[VMEM] * 4,
+        scratch_shapes=[
+            pltpu.VMEM(merging_weight.shape, BF16),
+            pltpu.VMEM(first_weight.shape, BF16),
+            pltpu.VMEM(second_weight.shape, BF16),
+            pltpu.SemaphoreType.DMA((3,)),
+        ],
+        compiler_params=room(4),
+        name="weights",
+    )(*map(in_hbm, (merging_weight, first_weight, second_weight)), near_msg)
+
+    pad_rows = pltpu.VMEM((8, cols + 2 * BLK, chans), F32)
+
     def wide(extra):
         return pltpu.VMEM((rows // 2 + extra, 2, cols, 3 * chans), BF16)
 
-    def features_part(frame):
+    def features_part(frame, near_feat, far_feat):
+        passed = 0 if frame == frames - 1 else 2
         return pl.pallas_call(
             functools.partial(features_kernel, frame),
-            out_shape=on_chip((rows // 2 + 2, cols, 2 * chans), F32),
-            in_specs=[SMEM, ANY] + [VMEM] * 3,
-            out_specs=VMEM,
+            out_shape=[on_chip((rows // 2 + 2, cols, 2 * chans), F32)] + [on_chip(edge_shape)] * passed,
+            in_specs=[ANY] + [VMEM] * 3,
+            out_specs=[VMEM] * (1 + passed),
             scratch_shapes=[
                 pltpu.VMEM((rows, across, BLK, chans), BF16),
                 wide(3),
+                pad_rows,
                 pltpu.SemaphoreType.DMA((4,)),
+                pltpu.SemaphoreType.DMA((2,)),
             ],
             compiler_params=room(16),
             name="features",
-        )(place, in_hbm(feats), resident(near_feat), resident(far_feat), resident(w_feat))
+        )(in_hbm(feats), resident(near_feat), resident(far_feat), resident(w_feat))
 
     out = None
     out_shape = shape_of((frames, rows, across, BLK, chans))
@@ -461,17 +485,19 @@
     for frame in range(frames):
         last = frame == frames - 1
         near_got, far_got = swap_both(near_msg, far_msg)
-        part = features_part(frame)
+        part, *next_edges = features_part(frame, near_feat, far_feat)
+        sent_edge = on_chip(((1 if last else 2) * HALO,) + edge_shape[1:])
         warped, near_edge, far_edge = pl.pallas_call(
             functools.partial(assemble_kernel, frame),
-            out_shape=[on_chip((rows, across, BLK, chans)), on_chip(edge_shape), on_chip(edge_shape)],
-            in_specs=[SMEM, SMEM] + [VMEM] * 3 + [ANY],
+            out_shape=[on_chip((rows, across, BLK, chans)), sent_edge, sent_edge],
+            in_specs=[SMEM] + [VMEM] * 3 + [ANY] + [VMEM] * len(next_edges),
             out_specs=[VMEM] * 3,
             scratch_shapes=[pltpu.VMEM((blocks + 2 * slots,) + block_shape, BF16)],
             compiler_params=room(8),
             name="assemble",
-        )(place, table, resident(pool), resident(near_got), resident(far_got), part)
+        )(table, resident(pool), resident(near_got), resident(far_got), part, *map(resident, next_edges))
         near_halo, far_halo = swap_both(near_edge, far_edge)
+        near_feat, far_feat = near_halo, far_halo
         args = tuple(map(resident, (part, warped, w_warp, w_first, w_second)))
         results = pl.pallas_call(
             functools.partial(inner_kernel, frame, last),
@@ -483,6 +509,7 @@
                 wide(3),
                 wide(2),
                 wide(1),
+            pad_rows,
                 pltpu.VMEM((rows, across, BLK, chans), BF16),
                 pltpu.SemaphoreType.DMA,
             ],
@@ -491,10 +518,11 @@
         )(*args, *([out] if frame else []))
         out = results[0]
         m_edge, d_edge = results[-2:]
-        args = (place,) + tuple(map(resident, (
+        args = tuple(map(resident, (
             part, warped, near_halo, far_halo, w_warp, w_first, w_second, m_edge, d_edge
         )))
         scratch = [pltpu.VMEM((2, 3, 2, cols, 3 * chans), BF16) for _ in range(3)] + [
+            pad_rows,
             pltpu.VMEM((rows, across, BLK, chans), BF16),
             pltpu.SemaphoreType.DMA((2,)),
         ]
@@ -503,9 +531,9 @@
             out = pl.pallas_call(
                 kernel,
                 out_shape=out_shape,
-                in_specs=[SMEM] + [VMEM] * 9 + [ANY],
+                in_specs=[VMEM] * 9 + [ANY],
                 out_specs=ANY,
-                input_output_aliases={10: 0},
+                input_output_aliases={9: 0},
                 scratch_shapes=scratch,
                 compiler_params=room(12),
                 name="border",
@@ -514,9 +542,9 @@
             out, pool, near_msg, far_msg = pl.pallas_call(
                 kernel,
                 out_shape=[out_shape, pool_shape, message, message],
-                in_specs=[SMEM] + [VMEM] * 9 + [ANY, VMEM] + [SMEM] * 2,
+                in_specs=[VMEM] * 9 + [ANY, VMEM] + [SMEM] * 2,
                 out_specs=[ANY] + [VMEM] * 3,
-                input_output_aliases={10: 0, 11: 1},
+                input_output_aliases={9: 0, 10: 1},
                 scratch_shapes=scratch,
                 compiler_params=room(12),
                 name="border",

time: 68.1 us -> 64.4 us (0.946)
  Pallas kernels: 31.6 us -> 29.1 us
  waiting for transfers between devices: 22.5 us -> 20.7 us
    pallas_call x4, Pallas kernels: 13 us -> 11.2 us  [the longest x2 7.21 us: features_part(): pl.pallas_call(functools.partial(features_kernel, frame), out_shape=[on_c...]
    ppermute x12, waiting for transfers between devices: 22.5 us -> 20.7 us  [swap(): return lax.ppermute(x, ('clips', 'rows'), neighbours(first))]
where the time goes in v3:
time: 64.4 us; the launch traced here: 64.2 us
  Pallas kernels  29.1 us (45%)
  waiting for transfers between devices  20.7 us (32%)
  starting transfers between devices  13.8 us (21%)
    ppermute x12, waiting for transfers between devices, swap(): return lax.ppermute(x, ('clips', 'rows'), neighbours(first))  20.7 us
    ppermute x12, starting transfers between devices, swap(): return lax.ppermute(x, ('clips', 'rows'), neighbours(first))  13.8 us
    pallas_call x2, Pallas kernels, on_device(): pl.pallas_call(functools.partial(inner_kernel, frame, last), out_shape=[o...  11.2 us
    pallas_call x2, Pallas kernels, features_part(): pl.pallas_call(functools.partial(features_kernel, frame), out_shape=[on_c...  7.21 us
    pallas_call x1, Pallas kernels, on_device(): pl.pallas_call(kernel, out_shape=[out_shape, pool_shape, message, message...  3.02 us
    pallas_call x1, Pallas kernels, on_device(): pl.pallas_call(kernel, out_shape=out_shape, in_specs=[VMEM] * 9 + [ANY],...  2.46 us
    pallas_call x2, Pallas kernels, on_device(): pl.pallas_call(functools.partial(assemble_kernel, frame), out_shape=[on_c...  1.82 us
    pallas_call x1, Pallas kernels, on_device(): pl.pallas_call(weights_kernel, out_shape=[pair_shape] * 4, in_specs=[ANY]...  1.5 us
  transfers between devices with their start and end apart: 12, of which 3 were waited for; matrix products, arithmetic and copies ran while one was open for 0% of the time, Pallas kernels for 31%

profile of v3, /device:TPU:1, one launch (start us, length us, event | category | flops | bytes accessed | tf_op | source)
XLA Modules:
  0.0 64.2 jit_solution(11054648514160845351)
XLA Ops:
  0.0 1.3 %tables.1 = (s32[2,64]{1,0:T(2,128)S(1)}, s32[2,40]{1,0:T(2,128)S(1)}, s32[2,40]{1,0:T(2,128)S(1)}, bf16[3,16,8,128]{3,2,1,0:T(8,128)(2,1)S(1)}, bf16[3,16,8,128...) custom-call(s32[2,64]{1,0:T(2,128)} %row_hbm.1, s32[2,64]{1,0:T(2,128)} %col_hbm.1, ...), custom_call_target="tpu_custom_call" | custom-call | tf_op jit(solution)/shard_map/tables/pallas_call | solution.py:411
  1.3 0.1 collective-permute-start
  1.4 2.7 %collective-permute-start.1 = (s32[2,40]{1,0:T(2,128)S(1)}, s32[2,40]{1,0:T(2,128)S(1)}, u32[]{:S(2)}, u32[]{:S(2)}) collective-permute-start(s32[2,40]{1,0:T(2,128)S(1)} %get-tuple-element.40), channel_id=1, source_target_pairs={{1,2},{3,4},{5,6},{7,8},{9,10},{11,12},{13,14},{17,18},{19,20},{21... | collective-permute-start | bytes 968 | tf_op jit(solution)/shard_map/ppermute | solution.py:51
  4.1 1.5 %collective-permute-done.1.far_list.refs_3_ = s32[2,40]{1,0:T(2,128)S(1)} collective-permute-done((s32[2,40]{1,0:T(2,128)S(1)}, s32[2,40]{1,0:T(2,128)S(1)}, u32[]{:S(2)}, u32[]{:S(2)}) %collective-permute-start.1) | collective-permute-done | bytes 352 | tf_op jit(solution)/shard_map/ppermute | solution.py:51
  5.6 0.6 pack.1
  6.2 0.5 collective-permute-start.2
  6.7 2.4 %collective-permute-start.3 = (bf16[32,8,8,128]{3,2,1,0:T(8,128)(2,1)S(1)}, bf16[32,8,8,128]{3,2,1,0:T(8,128)(2,1)S(1)}, u32[]{:S(2)}, u32[]{:S(2)}) collective-permute-start(bf16[32,8,8,128]{3,2,1,0:T(8,128)(2,1)S(1)} %get-tuple-element.42), channel_id=1, source_target_pairs={{1,2},{3,4},{5,6},{7,8},{9,10},{11,12},{13,14},{17,18},{19,20},{21... | collective-permute-start | bytes 1572872 | tf_op jit(solution)/shard_map/ppermute | solution.py:51
  9.1 1.3 %collective-permute-start.5 = (bf16[3,16,8,128]{3,2,1,0:T(8,128)(2,1)S(1)}, bf16[3,16,8,128]{3,2,1,0:T(8,128)(2,1)S(1)}, u32[]{:S(2)}, u32[]{:S(2)}) collective-permute-start(bf16[3,16,8,128]{3,2,1,0:T(8,128)(2,1)S(1)} %get-tuple-element.44), channel_id=1, source_target_pairs={{1,2},{3,4},{5,6},{7,8},{9,10},{11,12},{13,14},{17,18},{19,20},{21... | collective-permute-start | bytes 294920 | tf_op jit(solution)/shard_map/ppermute | solution.py:51
  10.4 1.5 %weights.1 = (bf16[1536,256]{1,0:T(8,128)(2,1)S(1)}, bf16[1536,256]{1,0:T(8,128)(2,1)S(1)}, bf16[1536,256]{1,0:T(8,128)(2,1)S(1)}, bf16[1536,256]{1,0:T(8,128)(2,1)S(1)}) custom-call(bf16[3,3,256,128]{3,2,1,0:T(8,128)(2,1)} %merging_hbm.1, bf16[3,3,128,128]{3,2,1,0:T(8,128)(2,1)} %first_hbm.1, bf16[3,3,128,128]{3,2,1,0:T(8,128)(2,1)} %second_hbm.1, ...), custom_call_target="tpu_custom_call" | custom-call | tf_op jit(solution)/shard_map/weights/pallas_call | solution.py:444
  11.9 11.1 %collective-permute-done.5.far_ref = bf16[3,16,8,128]{3,2,1,0:T(8,128)(2,1)S(1)} collective-permute-done((bf16[3,16,8,128]{3,2,1,0:T(8,128)(2,1)S(1)}, bf16[3,16,8,128]{3,2,1,0:T(8,128)(2,1)S(1)}, u32[]{:S(2)}, u32[]{:S(2)}) %collective-permute-start.5) | collective-permute-done | bytes 98336 | tf_op jit(solution)/shard_map/ppermute | solution.py:51
  22.9 3.6 %features.2 = (f32[18,128,256]{2,1,0:T(8,128)S(1)}, bf16[3,16,8,128]{3,2,1,0:T(8,128)(2,1)S(1)}, bf16[3,16,8,128]{3,2,1,0:T(8,128)(2,1)S(1)}) custom-call(bf16[2,32,16,8,128]{4,3,2,1,0:T(8,128)(2,1)} %bitcast.4, bf16[3,16,8,128]{3,2,1,0:T(8,128)(2,1)S(1)} %collective-permute-done.4.near_ref, bf16[3,16,8,128]{3,2,1,0:T(8,128)(2,1)S(1)} %collective-permute-done.5.far_ref, ...), custom_call_target="tpu_custom_call" | custom-call | tf_op jit(solution)/shard_map/features/pallas_call | solution.py:466
  26.6 0.9 %assemble.2 = (bf16[32,16,8,128]{3,2,1,0:T(8,128)(2,1)S(1)}, bf16[6,16,8,128]{3,2,1,0:T(8,128)(2,1)S(1)}, bf16[6,16,8,128]{3,2,1,0:T(8,128)(2,1)S(1)}) custom-call(s32[2,64]{1,0:T(2,128)S(1)} %get-tuple-element.37.table_ref, bf16[64,8,8,128]{3,2,1,0:T(8,128)(2,1)S(1)} %get-tuple-element.38.pool_ref, ...), custom_call_target="tpu_custom_call" | custom-call | tf_op jit(solution)/shard_map/assemble/pallas_call | solution.py:490
  27.5 0.1 collective-permute-start.6
  27.6 2.5 %collective-permute-start.7 = (bf16[6,16,8,128]{3,2,1,0:T(8,128)(2,1)S(1)}, bf16[6,16,8,128]{3,2,1,0:T(8,128)(2,1)S(1)}, u32[]{:S(2)}, u32[]{:S(2)}) collective-permute-start(bf16[6,16,8,128]{3,2,1,0:T(8,128)(2,1)S(1)} %get-tuple-element.50), channel_id=1, source_target_pairs={{1,2},{3,4},{5,6},{7,8},{9,10},{11,12},{13,14},{17,18},{19,20},{21... | collective-permute-start | bytes 589832 | tf_op jit(solution)/shard_map/ppermute | solution.py:51
  30.1 5.6 %inner.2 = (bf16[2,32,16,8,128]{4,3,2,1,0:T(8,128)(2,1)}, bf16[64,8,8,128]{3,2,1,0:T(8,128)(2,1)S(1)}, bf16[2,2,128,384]{3,2,1,0:T(8,128)(2,1)S(1)}, bf16[2,2,128,384]{3,2,1,0:T(8,128)(2,1)S(1)}) custom-call(f32[18,128,256]{2,1,0:T(8,128)S(1)} %get-tuple-element.46._.part_ref, bf16[32,16,8,128]{3,2,1,0:T(8,128)(2,1)S(1)} %get-tuple-element.51.warped_ref, ...), custom_call_target="tpu_custom_call" | custom-call | tf_op jit(solution)/shard_map/inner/pallas_call | solution.py:502
  35.8 3.0 %border.2 = (bf16[2,32,16,8,128]{4,3,2,1,0:T(8,128)(2,1)}, bf16[64,8,8,128]{3,2,1,0:T(8,128)(2,1)S(1)}, bf16[32,8,8,128]{3,2,1,0:T(8,128)(2,1)S(1)}, bf16[32,8,8,128]{3,2,1,0:T(8,128)(2,1)S(1)}) custom-call(f32[18,128,256]{2,1,0:T(8,128)S(1)} %get-tuple-element.46._.part_ref, ...), custom_call_target="tpu_custom_call", output_to_operand_aliasing={{0}: (9, {}), {1}: (10, {})} | custom-call | tf_op jit(solution)/shard_map/border/pallas_call | solution.py:542
  38.8 0.1 collective-permute-start.8
  38.9 1.6 %collective-permute-start.9 = (bf16[32,8,8,128]{3,2,1,0:T(8,128)(2,1)S(1)}, bf16[32,8,8,128]{3,2,1,0:T(8,128)(2,1)S(1)}, u32[]{:S(2)}, u32[]{:S(2)}) collective-permute-start(bf16[32,8,8,128]{3,2,1,0:T(8,128)(2,1)S(1)} %get-tuple-element.61), channel_id=1, source_target_pairs={{1,2},{3,4},{5,6},{7,8},{9,10},{11,12},{13,14},{17,18},{19,20},{21... | collective-permute-start | bytes 1572872 | tf_op jit(solution)/shard_map/ppermute | solution.py:51
  40.5 3.6 %features.3._.part_ref = f32[18,128,256]{2,1,0:T(8,128)S(1)} custom-call(bf16[2,32,16,8,128]{4,3,2,1,0:T(8,128)(2,1)} %bitcast.5, bf16[6,16,8,128]{3,2,1,0:T(8,128)(2,1)S(1)} %collective-permute-done.6.near_ref, bf16[6,16,8,128]{3,2,1,0:T(8,128)(2,1)S(1)} %collective-permute-done.7.far_ref, bf16[1536,256]{1,0:T(8,128)(2,1)S(1)} %get-tuple-element.45.w_ref), custom_call_target="tpu_custom_call" | custom-call | tf_op jit(solution)/shard_map/features/pallas_call | solution.py:466
  44.1 8.1 %collective-permute-done.9.far_ref = bf16[32,8,8,128]{3,2,1,0:T(8,128)(2,1)S(1)} collective-permute-done((bf16[32,8,8,128]{3,2,1,0:T(8,128)(2,1)S(1)}, bf16[32,8,8,128]{3,2,1,0:T(8,128)(2,1)S(1)}, u32[]{:S(2)}, u32[]{:S(2)}) %collective-permute-start.9) | collective-permute-done | bytes 524320 | tf_op jit(solution)/shard_map/ppermute | solution.py:51
  52.2 0.9 %assemble.3 = (bf16[32,16,8,128]{3,2,1,0:T(8,128)(2,1)S(1)}, bf16[3,16,8,128]{3,2,1,0:T(8,128)(2,1)S(1)}, bf16[3,16,8,128]{3,2,1,0:T(8,128)(2,1)S(1)}) custom-call(s32[2,64]{1,0:T(2,128)S(1)} %get-tuple-element.37.table_ref, bf16[64,8,8,128]{3,2,1,0:T(8,128)(2,1)S(1)} %get-tuple-element.59.pool_ref, ...), custom_call_target="tpu_custom_call" | custom-call | tf_op jit(solution)/shard_map/assemble/pallas_call | solution.py:490
  53.4 2.5 %collective-permute-start.11 = (bf16[3,16,8,128]{3,2,1,0:T(8,128)(2,1)S(1)}, bf16[3,16,8,128]{3,2,1,0:T(8,128)(2,1)S(1)}, u32[]{:S(2)}, u32[]{:S(2)}) collective-permute-start(bf16[3,16,8,128]{3,2,1,0:T(8,128)(2,1)S(1)} %get-tuple-element.64), channel_id=1, source_target_pairs={{1,2},{3,4},{5,6},{7,8},{9,10},{11,12},{13,14},{17,18},{19,20},{21... | collective-permute-start | bytes 294920 | tf_op jit(solution)/shard_map/ppermute | solution.py:51
  56.0 5.6 %inner.3 = (bf16[2,32,16,8,128]{4,3,2,1,0:T(8,128)(2,1)}, bf16[2,2,128,384]{3,2,1,0:T(8,128)(2,1)S(1)}, bf16[2,2,128,384]{3,2,1,0:T(8,128)(2,1)S(1)}) custom-call(f32[18,128,256]{2,1,0:T(8,128)S(1)} %features.3._.part_ref, bf16[32,16,8,128]{3,2,1,0:T(8,128)(2,1)S(1)} %get-tuple-element.62.warped_ref, ...), custom_call_target="tpu_custom_call", output_to_operand_aliasing={{0}: (5, {})} | custom-call | tf_op jit(solution)/shard_map/inner/pallas_call | solution.py:502
  61.6 2.5 %border.3 = bf16[2,32,16,8,128]{4,3,2,1,0:T(8,128)(2,1)} custom-call(f32[18,128,256]{2,1,0:T(8,128)S(1)} %features.3._.part_ref, bf16[32,16,8,128]{3,2,1,0:T(8,128)(2,1)S(1)} %get-tuple-element.62.warped_ref, bf16[3,16,8,128]{3,2,1,0:T(8,128)(2,1)S(1)} %collective-permute-done.10.near_ref, ...), custom_call_target="tpu_custom_call", output_to_operand_aliasing={{}: (9, {})} | custom-call | tf_op jit(solution)/shard_map/border/pallas_call | solution.py:531
  (11 shorter events, 0.1 us)
Async XLA Ops:
  1.3 2.8 %collective-permute-start = (s32[2,40]{1,0:T(2,128)S(1)}, s32[2,40]{1,0:T(2,128)S(1)}, u32[]{:S(2)}, u32[]{:S(2)}) collective-permute-start(s32[2,40]{1,0:T(2,128)S(1)} %get-tuple-element.39), channel_id=1, source_target_pairs={{0,1},{2,3},{4,5},{6,7},{8,9},{10,11},{12,13},{14,15},{16,17},{18,... | collective-permute-start | bytes 968 | tf_op jit(solution)/shard_map/ppermute | solution.py:51
  1.4 4.2 %collective-permute-start.1 = (s32[2,40]{1,0:T(2,128)S(1)}, s32[2,40]{1,0:T(2,128)S(1)}, u32[]{:S(2)}, u32[]{:S(2)}) collective-permute-start(s32[2,40]{1,0:T(2,128)S(1)} %get-tuple-element.40), channel_id=1, source_target_pairs={{1,2},{3,4},{5,6},{7,8},{9,10},{11,12},{13,14},{17,18},{19,20},{21... | collective-permute-start | bytes 968 | tf_op jit(solution)/shard_map/ppermute | solution.py:51
  6.2 20.3 %collective-permute-start.2 = (bf16[32,8,8,128]{3,2,1,0:T(8,128)(2,1)S(1)}, bf16[32,8,8,128]{3,2,1,0:T(8,128)(2,1)S(1)}, u32[]{:S(2)}, u32[]{:S(2)}) collective-permute-start(bf16[32,8,8,128]{3,2,1,0:T(8,128)(2,1)S(1)} %get-tuple-element.41._), channel_id=1, source_target_pairs={{0,1},{2,3},{4,5},{6,7},{8,9},{10,11},{12,13},{14,15},{16,17},{18,... | collective-permute-start | bytes 1572872 | tf_op jit(solution)/shard_map/ppermute | solution.py:51
  6.7 19.9 %collective-permute-start.3 = (bf16[32,8,8,128]{3,2,1,0:T(8,128)(2,1)S(1)}, bf16[32,8,8,128]{3,2,1,0:T(8,128)(2,1)S(1)}, u32[]{:S(2)}, u32[]{:S(2)}) collective-permute-start(bf16[32,8,8,128]{3,2,1,0:T(8,128)(2,1)S(1)} %get-tuple-element.42), channel_id=1, source_target_pairs={{1,2},{3,4},{5,6},{7,8},{9,10},{11,12},{13,14},{17,18},{19,20},{21... | collective-permute-start | bytes 1572872 | tf_op jit(solution)/shard_map/ppermute | solution.py:51
  9.1 2.8 %collective-permute-start.4 = (bf16[3,16,8,128]{3,2,1,0:T(8,128)(2,1)S(1)}, bf16[3,16,8,128]{3,2,1,0:T(8,128)(2,1)S(1)}, u32[]{:S(2)}, u32[]{:S(2)}) collective-permute-start(bf16[3,16,8,128]{3,2,1,0:T(8,128)(2,1)S(1)} %get-tuple-element.43), channel_id=1, source_target_pairs={{0,1},{2,3},{4,5},{6,7},{8,9},{10,11},{12,13},{14,15},{16,17},{18,... | collective-permute-start | bytes 294920 | tf_op jit(solution)/shard_map/ppermute | solution.py:51
  9.1 13.8 %collective-permute-start.5 = (bf16[3,16,8,128]{3,2,1,0:T(8,128)(2,1)S(1)}, bf16[3,16,8,128]{3,2,1,0:T(8,128)(2,1)S(1)}, u32[]{:S(2)}, u32[]{:S(2)}) collective-permute-start(bf16[3,16,8,128]{3,2,1,0:T(8,128)(2,1)S(1)} %get-tuple-element.44), channel_id=1, source_target_pairs={{1,2},{3,4},{5,6},{7,8},{9,10},{11,12},{13,14},{17,18},{19,20},{21... | collective-permute-start | bytes 294920 | tf_op jit(solution)/shard_map/ppermute | solution.py:51
  27.5 8.2 %collective-permute-start.6 = (bf16[6,16,8,128]{3,2,1,0:T(8,128)(2,1)S(1)}, bf16[6,16,8,128]{3,2,1,0:T(8,128)(2,1)S(1)}, u32[]{:S(2)}, u32[]{:S(2)}) collective-permute-start(bf16[6,16,8,128]{3,2,1,0:T(8,128)(2,1)S(1)} %get-tuple-element.49), channel_id=1, source_target_pairs={{0,1},{2,3},{4,5},{6,7},{8,9},{10,11},{12,13},{14,15},{16,17},{18,... | collective-permute-start | bytes 589832 | tf_op jit(solution)/shard_map/ppermute | solution.py:51
  27.6 8.2 %collective-permute-start.7 = (bf16[6,16,8,128]{3,2,1,0:T(8,128)(2,1)S(1)}, bf16[6,16,8,128]{3,2,1,0:T(8,128)(2,1)S(1)}, u32[]{:S(2)}, u32[]{:S(2)}) collective-permute-start(bf16[6,16,8,128]{3,2,1,0:T(8,128)(2,1)S(1)} %get-tuple-element.50), channel_id=1, source_target_pairs={{1,2},{3,4},{5,6},{7,8},{9,10},{11,12},{13,14},{17,18},{19,20},{21... | collective-permute-start | bytes 589832 | tf_op jit(solution)/shard_map/ppermute | solution.py:51
  38.8 5.3 %collective-permute-start.8 = (bf16[32,8,8,128]{3,2,1,0:T(8,128)(2,1)S(1)}, bf16[32,8,8,128]{3,2,1,0:T(8,128)(2,1)S(1)}, u32[]{:S(2)}, u32[]{:S(2)}) collective-permute-start(bf16[32,8,8,128]{3,2,1,0:T(8,128)(2,1)S(1)} %get-tuple-element.60), channel_id=1, source_target_pairs={{0,1},{2,3},{4,5},{6,7},{8,9},{10,11},{12,13},{14,15},{16,17},{18,... | collective-permute-start | bytes 1572872 | tf_op jit(solution)/shard_map/ppermute | solution.py:51
  38.9 13.4 %collective-permute-start.9 = (bf16[32,8,8,128]{3,2,1,0:T(8,128)(2,1)S(1)}, bf16[32,8,8,128]{3,2,1,0:T(8,128)(2,1)S(1)}, u32[]{:S(2)}, u32[]{:S(2)}) collective-permute-start(bf16[32,8,8,128]{3,2,1,0:T(8,128)(2,1)S(1)} %get-tuple-element.61), channel_id=1, source_target_pairs={{1,2},{3,4},{5,6},{7,8},{9,10},{11,12},{13,14},{17,18},{19,20},{21... | collective-permute-start | bytes 1572872 | tf_op jit(solution)/shard_map/ppermute | solution.py:51
  53.3 8.2 %collective-permute-start.10 = (bf16[3,16,8,128]{3,2,1,0:T(8,128)(2,1)S(1)}, bf16[3,16,8,128]{3,2,1,0:T(8,128)(2,1)S(1)}, u32[]{:S(2)}, u32[]{:S(2)}) collective-permute-start(bf16[3,16,8,128]{3,2,1,0:T(8,128)(2,1)S(1)} %get-tuple-element.63), channel_id=1, source_target_pairs={{0,1},{2,3},{4,5},{6,7},{8,9},{10,11},{12,13},{14,15},{16,17},{18,... | collective-permute-start | bytes 294920 | tf_op jit(solution)/shard_map/ppermute | solution.py:51
  53.4 8.2 %collective-permute-start.11 = (bf16[3,16,8,128]{3,2,1,0:T(8,128)(2,1)S(1)}, bf16[3,16,8,128]{3,2,1,0:T(8,128)(2,1)S(1)}, u32[]{:S(2)}, u32[]{:S(2)}) collective-permute-start(bf16[3,16,8,128]{3,2,1,0:T(8,128)(2,1)S(1)} %get-tuple-element.64), channel_id=1, source_target_pairs={{1,2},{3,4},{5,6},{7,8},{9,10},{11,12},{13,14},{17,18},{19,20},{21... | collective-permute-start | bytes 294920 | tf_op jit(solution)/shard_map/ppermute | solution.py:51

commit v4 on v3

--- a/solution.py
+++ b/solution.py
@@ -249,19 +249,22 @@
         load.wait()
 
 
-def assemble_kernel(frame, table_ref, pool_ref, near_ref, far_ref, _, *refs):
-    warped_out, near_edge, far_edge, all_ref = refs[-4:]
+def assemble_kernel(frame, table_vmem, pool_ref, near_ref, far_ref, _, *refs):
+    warped_out, near_edge, far_edge, all_ref, table_ref, table_sem = refs[-6:]
+    table_copy = pltpu.make_async_copy(table_vmem, table_ref, table_sem)
+    table_copy.start()
     rows, across = warped_out.shape[:2]
     blocks = pool_ref.shape[0]
     slots = near_ref.shape[0]
     odd = lax.rem(lax.axis_index("rows"), 2)
     near_rows = pl.ds(jnp.where(odd == 0, rows - HALO, 0), HALO)
     far_rows = pl.ds(jnp.where(odd == 0, 0, rows - HALO), HALO)
-    for edge, feat_edge in zip((near_edge, far_edge), refs[:-4]):
+    for edge, feat_edge in zip((near_edge, far_edge), refs[:-6]):
         edge[HALO:2 * HALO] = feat_edge[...]
     all_ref[0:blocks] = pool_ref[...]
     all_ref[blocks:blocks + slots] = near_ref[...]
     all_ref[blocks + slots:blocks + 2 * slots] = far_ref[...]
+    table_copy.wait()
     for block in range(blocks):
         q, p = divmod(block, across)
         warped_out[q * BLK:(q + 1) * BLK, p] = all_ref[table_ref[frame, block]]
@@ -330,8 +333,14 @@
         _, out_ref, x_ref, m_ref, d_ref, pad_ref, state_ref, sem = refs
         pool_ref = None
     else:
-        _, _, near_list, far_list, out_ref, pool_ref, near_out, far_out = refs[:8]
-        x_ref, m_ref, d_ref, pad_ref, state_ref, sem = refs[8:]
+        _, _, near_vmem, far_vmem, out_ref, pool_ref, near_out, far_out = refs[:8]
+        x_ref, m_ref, d_ref, pad_ref, state_ref, sem, near_list, far_list = refs[8:]
+        lists = [
+            pltpu.make_async_copy(near_vmem, near_list, sem.at[2]),
+            pltpu.make_async_copy(far_vmem, far_list, sem.at[3]),
+        ]
+        for copy in lists:
+            copy.start()
     spread = shifter(pad_ref)
     rows, across, _, chans = warped_ref.shape
     cols = across * BLK
@@ -376,18 +385,19 @@
         for n, half, one in split_rows(value, 2, cols, chans):
             one = masked(one, 2 * (first + n) + half - 1)
             spread(d_ref.at[side], n + side, half, one)
+    copies = []
     for side in range(2):
         first = side * (half_rows - 2)
         value = edge_dot(d_ref, side, w3_ref)
         for n, half, one in split_rows(value, 2, cols, chans):
             centre = m_ref[side, n + 1 - side, half, :, chans:2 * chans]
             finish(state_ref, pool_ref, centre, one, 2 * (first + n) + half, across, chans)
-    copies = []
-    for n, start in enumerate((0, rows - 4)):
-        part = pl.ds(start, 4)
-        copies.append(pltpu.make_async_copy(state_ref.at[part], out_ref.at[frame, part], sem.at[n]))
+        part = pl.ds(side * (rows - 4), 4)
+        copies.append(pltpu.make_async_copy(state_ref.at[part], out_ref.at[frame, part], sem.at[side]))
         copies[-1].start()
     if not last:
+        for copy in lists:
+            copy.wait()
         pack(pool_ref, near_list, far_list, frame + 1, near_out, far_out)
     for copy in copies:
         copy.wait()
@@ -456,7 +466,7 @@
         name="weights",
     )(*map(in_hbm, (merging_weight, first_weight, second_weight)), near_msg)
 
-    pad_rows = pltpu.VMEM((8, cols + 2 * BLK, chans), F32)
+    pad_rows = pltpu.VMEM((24, cols + 2 * BLK, chans), F32)
 
     def wide(extra):
         return pltpu.VMEM((rows // 2 + extra, 2, cols, 3 * chans), BF16)
@@ -490,12 +500,16 @@
         warped, near_edge, far_edge = pl.pallas_call(
             functools.partial(assemble_kernel, frame),
             out_shape=[on_chip((rows, across, BLK, chans)), sent_edge, sent_edge],
-            in_specs=[SMEM] + [VMEM] * 3 + [ANY] + [VMEM] * len(next_edges),
+            in_specs=[VMEM] * 4 + [ANY] + [VMEM] * len(next_edges),
             out_specs=[VMEM] * 3,
-            scratch_shapes=[pltpu.VMEM((blocks + 2 * slots,) + block_shape, BF16)],
+            scratch_shapes=[
+                pltpu.VMEM((blocks + 2 * slots,) + block_shape, BF16),
+                pltpu.SMEM((frames, blocks), jnp.int32),
+                pltpu.SemaphoreType.DMA,
+            ],
             compiler_params=room(8),
             name="assemble",
-        )(table, resident(pool), resident(near_got), resident(far_got), part, *map(resident, next_edges))
+        )(resident(table), resident(pool), resident(near_got), resident(far_got), part, *map(resident, next_edges))
         near_halo, far_halo = swap_both(near_edge, far_edge)
         near_feat, far_feat = near_halo, far_halo
         args = tuple(map(resident, (part, warped, w_warp, w_first, w_second)))
@@ -524,8 +538,8 @@
         scratch = [pltpu.VMEM((2, 3, 2, cols, 3 * chans), BF16) for _ in range(3)] + [
             pad_rows,
             pltpu.VMEM((rows, across, BLK, chans), BF16),
-            pltpu.SemaphoreType.DMA((2,)),
-        ]
+            pltpu.SemaphoreType.DMA((4,)),
+        ] + [pltpu.SMEM((frames, list_len), jnp.int32)] * (0 if last else 2)
         kernel = functools.partial(border_kernel, frame, last)
         if last:
             out = pl.pallas_call(
@@ -542,13 +556,13 @@
             out, pool, near_msg, far_msg = pl.pallas_call(
                 kernel,
                 out_shape=[out_shape, pool_shape, message, message],
-                in_specs=[VMEM] * 9 + [ANY, VMEM] + [SMEM] * 2,
+                in_specs=[VMEM] * 9 + [ANY] + [VMEM] * 3,
                 out_specs=[ANY] + [VMEM] * 3,
                 input_output_aliases={9: 0, 10: 1},
                 scratch_shapes=scratch,
                 compiler_params=room(12),
                 name="border",
-            )(*args, out, resident(results[1]), near_list, far_list)
+            )(*args, out, resident(results[1]), resident(near_list), resident(far_list))
     return out.reshape(frames, rows, cols, chans)
 
 

time: 64.4 us -> 63.6 us (0.988)
  Pallas kernels: 29.1 us -> 28.1 us
where the time goes in v4:
time: 63.6 us; the launch traced here: 63.3 us
  Pallas kernels  28.1 us (44%)
  waiting for transfers between devices  20.7 us (33%)
  starting transfers between devices  14.2 us (22%)
    ppermute x12, waiting for transfers between devices, swap(): return lax.ppermute(x, ('clips', 'rows'), neighbours(first))  20.7 us
    ppermute x12, starting transfers between devices, swap(): return lax.ppermute(x, ('clips', 'rows'), neighbours(first))  14.2 us
    pallas_call x2, Pallas kernels, on_device(): pl.pallas_call(functools.partial(inner_kernel, frame, last), out_shape=[o...  10.9 us
    pallas_call x2, Pallas kernels, features_part(): pl.pallas_call(functools.partial(features_kernel, frame), out_shape=[on_c...  7.21 us
    pallas_call x1, Pallas kernels, on_device(): pl.pallas_call(kernel, out_shape=[out_shape, pool_shape, message, message...  2.5 us
    pallas_call x1, Pallas kernels, on_device(): pl.pallas_call(kernel, out_shape=out_shape, in_specs=[VMEM] * 9 + [ANY],...  2.5 us
    pallas_call x2, Pallas kernels, on_device(): pl.pallas_call(functools.partial(assemble_kernel, frame), out_shape=[on_c...  1.59 us
    pallas_call x1, Pallas kernels, on_device(): pl.pallas_call(weights_kernel, out_shape=[pair_shape] * 4, in_specs=[ANY]...  1.5 us
  transfers between devices with their start and end apart: 12, of which 3 were waited for; matrix products, arithmetic and copies ran while one was open for 0% of the time, Pallas kernels for 31%

profile of v4, /device:TPU:1, one launch (start us, length us, event | category | flops | bytes accessed | tf_op | source)
XLA Modules:
  0.0 63.3 jit_solution(8315955402420749014)
XLA Ops:
  0.0 1.3 %tables.1 = (s32[2,64]{1,0:T(2,128)S(1)}, s32[2,40]{1,0:T(2,128)S(1)}, s32[2,40]{1,0:T(2,128)S(1)}, bf16[3,16,8,128]{3,2,1,0:T(8,128)(2,1)S(1)}, bf16[3,16,8,128...) custom-call(s32[2,64]{1,0:T(2,128)} %row_hbm.1, s32[2,64]{1,0:T(2,128)} %col_hbm.1, ...), custom_call_target="tpu_custom_call" | custom-call | tf_op jit(solution)/shard_map/tables/pallas_call | solution.py:421
  1.3 0.1 collective-permute-start
  1.4 2.7 %collective-permute-start.1 = (s32[2,40]{1,0:T(2,128)S(1)}, s32[2,40]{1,0:T(2,128)S(1)}, u32[]{:S(2)}, u32[]{:S(2)}) collective-permute-start(s32[2,40]{1,0:T(2,128)S(1)} %get-tuple-element.40), channel_id=1, source_target_pairs={{1,2},{3,4},{5,6},{7,8},{9,10},{11,12},{13,14},{17,18},{19,20},{21... | collective-permute-start | bytes 968 | tf_op jit(solution)/shard_map/ppermute | solution.py:51
  4.1 1.5 %collective-permute-done.1.far_list.refs_3_ = s32[2,40]{1,0:T(2,128)S(1)} collective-permute-done((s32[2,40]{1,0:T(2,128)S(1)}, s32[2,40]{1,0:T(2,128)S(1)}, u32[]{:S(2)}, u32[]{:S(2)}) %collective-permute-start.1) | collective-permute-done | bytes 352 | tf_op jit(solution)/shard_map/ppermute | solution.py:51
  5.6 0.6 pack.1
  6.2 0.5 collective-permute-start.2
  6.7 2.4 %collective-permute-start.3 = (bf16[32,8,8,128]{3,2,1,0:T(8,128)(2,1)S(1)}, bf16[32,8,8,128]{3,2,1,0:T(8,128)(2,1)S(1)}, u32[]{:S(2)}, u32[]{:S(2)}) collective-permute-start(bf16[32,8,8,128]{3,2,1,0:T(8,128)(2,1)S(1)} %get-tuple-element.42), channel_id=1, source_target_pairs={{1,2},{3,4},{5,6},{7,8},{9,10},{11,12},{13,14},{17,18},{19,20},{21... | collective-permute-start | bytes 1572872 | tf_op jit(solution)/shard_map/ppermute | solution.py:51
  9.1 1.3 %collective-permute-start.5 = (bf16[3,16,8,128]{3,2,1,0:T(8,128)(2,1)S(1)}, bf16[3,16,8,128]{3,2,1,0:T(8,128)(2,1)S(1)}, u32[]{:S(2)}, u32[]{:S(2)}) collective-permute-start(bf16[3,16,8,128]{3,2,1,0:T(8,128)(2,1)S(1)} %get-tuple-element.44), channel_id=1, source_target_pairs={{1,2},{3,4},{5,6},{7,8},{9,10},{11,12},{13,14},{17,18},{19,20},{21... | collective-permute-start | bytes 294920 | tf_op jit(solution)/shard_map/ppermute | solution.py:51
  10.4 1.5 %weights.1 = (bf16[1536,256]{1,0:T(8,128)(2,1)S(1)}, bf16[1536,256]{1,0:T(8,128)(2,1)S(1)}, bf16[1536,256]{1,0:T(8,128)(2,1)S(1)}, bf16[1536,256]{1,0:T(8,128)(2,1)S(1)}) custom-call(bf16[3,3,256,128]{3,2,1,0:T(8,128)(2,1)} %merging_hbm.1, bf16[3,3,128,128]{3,2,1,0:T(8,128)(2,1)} %first_hbm.1, bf16[3,3,128,128]{3,2,1,0:T(8,128)(2,1)} %second_hbm.1, ...), custom_call_target="tpu_custom_call" | custom-call | tf_op jit(solution)/shard_map/weights/pallas_call | solution.py:454
  11.9 11.1 %collective-permute-done.5.far_ref = bf16[3,16,8,128]{3,2,1,0:T(8,128)(2,1)S(1)} collective-permute-done((bf16[3,16,8,128]{3,2,1,0:T(8,128)(2,1)S(1)}, bf16[3,16,8,128]{3,2,1,0:T(8,128)(2,1)S(1)}, u32[]{:S(2)}, u32[]{:S(2)}) %collective-permute-start.5) | collective-permute-done | bytes 98336 | tf_op jit(solution)/shard_map/ppermute | solution.py:51
  22.9 3.6 %features.2 = (f32[18,128,256]{2,1,0:T(8,128)S(1)}, bf16[3,16,8,128]{3,2,1,0:T(8,128)(2,1)S(1)}, bf16[3,16,8,128]{3,2,1,0:T(8,128)(2,1)S(1)}) custom-call(bf16[2,32,16,8,128]{4,3,2,1,0:T(8,128)(2,1)} %bitcast.4, bf16[3,16,8,128]{3,2,1,0:T(8,128)(2,1)S(1)} %collective-permute-done.4.near_ref, bf16[3,16,8,128]{3,2,1,0:T(8,128)(2,1)S(1)} %collective-permute-done.5.far_ref, ...), custom_call_target="tpu_custom_call" | custom-call | tf_op jit(solution)/shard_map/features/pallas_call | solution.py:476
  26.6 0.8 %assemble.2 = (bf16[32,16,8,128]{3,2,1,0:T(8,128)(2,1)S(1)}, bf16[6,16,8,128]{3,2,1,0:T(8,128)(2,1)S(1)}, bf16[6,16,8,128]{3,2,1,0:T(8,128)(2,1)S(1)}) custom-call(s32[2,64]{1,0:T(2,128)S(1)} %get-tuple-element.37.table_vmem, bf16[64,8,8,128]{3,2,1,0:T(8,128)(2,1)S(1)} %get-tuple-element.38.pool_ref, ...), custom_call_target="tpu_custom_call" | custom-call | tf_op jit(solution)/shard_map/assemble/pallas_call | solution.py:500
  27.4 0.1 collective-permute-start.6
  27.5 2.5 %collective-permute-start.7 = (bf16[6,16,8,128]{3,2,1,0:T(8,128)(2,1)S(1)}, bf16[6,16,8,128]{3,2,1,0:T(8,128)(2,1)S(1)}, u32[]{:S(2)}, u32[]{:S(2)}) collective-permute-start(bf16[6,16,8,128]{3,2,1,0:T(8,128)(2,1)S(1)} %get-tuple-element.50), channel_id=1, source_target_pairs={{1,2},{3,4},{5,6},{7,8},{9,10},{11,12},{13,14},{17,18},{19,20},{21... | collective-permute-start | bytes 589832 | tf_op jit(solution)/shard_map/ppermute | solution.py:51
  30.0 5.5 %inner.2 = (bf16[2,32,16,8,128]{4,3,2,1,0:T(8,128)(2,1)}, bf16[64,8,8,128]{3,2,1,0:T(8,128)(2,1)S(1)}, bf16[2,2,128,384]{3,2,1,0:T(8,128)(2,1)S(1)}, bf16[2,2,128,384]{3,2,1,0:T(8,128)(2,1)S(1)}) custom-call(f32[18,128,256]{2,1,0:T(8,128)S(1)} %get-tuple-element.46._.part_ref, bf16[32,16,8,128]{3,2,1,0:T(8,128)(2,1)S(1)} %get-tuple-element.51.warped_ref, ...), custom_call_target="tpu_custom_call" | custom-call | tf_op jit(solution)/shard_map/inner/pallas_call | solution.py:516
  35.5 2.5 %border.2 = (bf16[2,32,16,8,128]{4,3,2,1,0:T(8,128)(2,1)}, bf16[64,8,8,128]{3,2,1,0:T(8,128)(2,1)S(1)}, bf16[32,8,8,128]{3,2,1,0:T(8,128)(2,1)S(1)}, bf16[32,8,8,128]{3,2,1,0:T(8,128)(2,1)S(1)}) custom-call(f32[18,128,256]{2,1,0:T(8,128)S(1)} %get-tuple-element.46._.part_ref, ...), custom_call_target="tpu_custom_call", output_to_operand_aliasing={{0}: (9, {}), {1}: (10, {})} | custom-call | tf_op jit(solution)/shard_map/border/pallas_call | solution.py:556
  38.0 0.1 collective-permute-start.8
  38.1 1.8 %collective-permute-start.9 = (bf16[32,8,8,128]{3,2,1,0:T(8,128)(2,1)S(1)}, bf16[32,8,8,128]{3,2,1,0:T(8,128)(2,1)S(1)}, u32[]{:S(2)}, u32[]{:S(2)}) collective-permute-start(bf16[32,8,8,128]{3,2,1,0:T(8,128)(2,1)S(1)} %get-tuple-element.61), channel_id=1, source_target_pairs={{1,2},{3,4},{5,6},{7,8},{9,10},{11,12},{13,14},{17,18},{19,20},{21... | collective-permute-start | bytes 1572872 | tf_op jit(solution)/shard_map/ppermute | solution.py:51
  39.9 3.6 %features.3._.part_ref = f32[18,128,256]{2,1,0:T(8,128)S(1)} custom-call(bf16[2,32,16,8,128]{4,3,2,1,0:T(8,128)(2,1)} %bitcast.5, bf16[6,16,8,128]{3,2,1,0:T(8,128)(2,1)S(1)} %collective-permute-done.6.near_ref, bf16[6,16,8,128]{3,2,1,0:T(8,128)(2,1)S(1)} %collective-permute-done.7.far_ref, bf16[1536,256]{1,0:T(8,128)(2,1)S(1)} %get-tuple-element.45.w_ref), custom_call_target="tpu_custom_call" | custom-call | tf_op jit(solution)/shard_map/features/pallas_call | solution.py:476
  43.5 8.1 %collective-permute-done.9.far_ref = bf16[32,8,8,128]{3,2,1,0:T(8,128)(2,1)S(1)} collective-permute-done((bf16[32,8,8,128]{3,2,1,0:T(8,128)(2,1)S(1)}, bf16[32,8,8,128]{3,2,1,0:T(8,128)(2,1)S(1)}, u32[]{:S(2)}, u32[]{:S(2)}) %collective-permute-start.9) | collective-permute-done | bytes 524320 | tf_op jit(solution)/shard_map/ppermute | solution.py:51
  51.6 0.8 %assemble.3 = (bf16[32,16,8,128]{3,2,1,0:T(8,128)(2,1)S(1)}, bf16[3,16,8,128]{3,2,1,0:T(8,128)(2,1)S(1)}, bf16[3,16,8,128]{3,2,1,0:T(8,128)(2,1)S(1)}) custom-call(s32[2,64]{1,0:T(2,128)S(1)} %get-tuple-element.37.table_vmem, bf16[64,8,8,128]{3,2,1,0:T(8,128)(2,1)S(1)} %get-tuple-element.59.pool_ref, ...), custom_call_target="tpu_custom_call" | custom-call | tf_op jit(solution)/shard_map/assemble/pallas_call | solution.py:500
  52.5 2.7 %collective-permute-start.11 = (bf16[3,16,8,128]{3,2,1,0:T(8,128)(2,1)S(1)}, bf16[3,16,8,128]{3,2,1,0:T(8,128)(2,1)S(1)}, u32[]{:S(2)}, u32[]{:S(2)}) collective-permute-start(bf16[3,16,8,128]{3,2,1,0:T(8,128)(2,1)S(1)} %get-tuple-element.64), channel_id=1, source_target_pairs={{1,2},{3,4},{5,6},{7,8},{9,10},{11,12},{13,14},{17,18},{19,20},{21... | collective-permute-start | bytes 294920 | tf_op jit(solution)/shard_map/ppermute | solution.py:51
  55.2 5.4 %inner.3 = (bf16[2,32,16,8,128]{4,3,2,1,0:T(8,128)(2,1)}, bf16[2,2,128,384]{3,2,1,0:T(8,128)(2,1)S(1)}, bf16[2,2,128,384]{3,2,1,0:T(8,128)(2,1)S(1)}) custom-call(f32[18,128,256]{2,1,0:T(8,128)S(1)} %features.3._.part_ref, bf16[32,16,8,128]{3,2,1,0:T(8,128)(2,1)S(1)} %get-tuple-element.62.warped_ref, ...), custom_call_target="tpu_custom_call", output_to_operand_aliasing={{0}: (5, {})} | custom-call | tf_op jit(solution)/shard_map/inner/pallas_call | solution.py:516
  60.7 2.5 %border.3 = bf16[2,32,16,8,128]{4,3,2,1,0:T(8,128)(2,1)} custom-call(f32[18,128,256]{2,1,0:T(8,128)S(1)} %features.3._.part_ref, bf16[32,16,8,128]{3,2,1,0:T(8,128)(2,1)S(1)} %get-tuple-element.62.warped_ref, bf16[3,16,8,128]{3,2,1,0:T(8,128)(2,1)S(1)} %collective-permute-done.10.near_ref, ...), custom_call_target="tpu_custom_call", output_to_operand_aliasing={{}: (9, {})} | custom-call | tf_op jit(solution)/shard_map/border/pallas_call | solution.py:545
  (11 shorter events, 0.1 us)
Async XLA Ops:
  1.3 2.8 %collective-permute-start = (s32[2,40]{1,0:T(2,128)S(1)}, s32[2,40]{1,0:T(2,128)S(1)}, u32[]{:S(2)}, u32[]{:S(2)}) collective-permute-start(s32[2,40]{1,0:T(2,128)S(1)} %get-tuple-element.39), channel_id=1, source_target_pairs={{0,1},{2,3},{4,5},{6,7},{8,9},{10,11},{12,13},{14,15},{16,17},{18,... | collective-permute-start | bytes 968 | tf_op jit(solution)/shard_map/ppermute | solution.py:51
  1.4 4.2 %collective-permute-start.1 = (s32[2,40]{1,0:T(2,128)S(1)}, s32[2,40]{1,0:T(2,128)S(1)}, u32[]{:S(2)}, u32[]{:S(2)}) collective-permute-start(s32[2,40]{1,0:T(2,128)S(1)} %get-tuple-element.40), channel_id=1, source_target_pairs={{1,2},{3,4},{5,6},{7,8},{9,10},{11,12},{13,14},{17,18},{19,20},{21... | collective-permute-start | bytes 968 | tf_op jit(solution)/shard_map/ppermute | solution.py:51
  6.2 20.3 %collective-permute-start.2 = (bf16[32,8,8,128]{3,2,1,0:T(8,128)(2,1)S(1)}, bf16[32,8,8,128]{3,2,1,0:T(8,128)(2,1)S(1)}, u32[]{:S(2)}, u32[]{:S(2)}) collective-permute-start(bf16[32,8,8,128]{3,2,1,0:T(8,128)(2,1)S(1)} %get-tuple-element.41._), channel_id=1, source_target_pairs={{0,1},{2,3},{4,5},{6,7},{8,9},{10,11},{12,13},{14,15},{16,17},{18,... | collective-permute-start | bytes 1572872 | tf_op jit(solution)/shard_map/ppermute | solution.py:51
  6.7 19.9 %collective-permute-start.3 = (bf16[32,8,8,128]{3,2,1,0:T(8,128)(2,1)S(1)}, bf16[32,8,8,128]{3,2,1,0:T(8,128)(2,1)S(1)}, u32[]{:S(2)}, u32[]{:S(2)}) collective-permute-start(bf16[32,8,8,128]{3,2,1,0:T(8,128)(2,1)S(1)} %get-tuple-element.42), channel_id=1, source_target_pairs={{1,2},{3,4},{5,6},{7,8},{9,10},{11,12},{13,14},{17,18},{19,20},{21... | collective-permute-start | bytes 1572872 | tf_op jit(solution)/shard_map/ppermute | solution.py:51
  9.1 2.8 %collective-permute-start.4 = (bf16[3,16,8,128]{3,2,1,0:T(8,128)(2,1)S(1)}, bf16[3,16,8,128]{3,2,1,0:T(8,128)(2,1)S(1)}, u32[]{:S(2)}, u32[]{:S(2)}) collective-permute-start(bf16[3,16,8,128]{3,2,1,0:T(8,128)(2,1)S(1)} %get-tuple-element.43), channel_id=1, source_target_pairs={{0,1},{2,3},{4,5},{6,7},{8,9},{10,11},{12,13},{14,15},{16,17},{18,... | collective-permute-start | bytes 294920 | tf_op jit(solution)/shard_map/ppermute | solution.py:51
  9.1 13.8 %collective-permute-start.5 = (bf16[3,16,8,128]{3,2,1,0:T(8,128)(2,1)S(1)}, bf16[3,16,8,128]{3,2,1,0:T(8,128)(2,1)S(1)}, u32[]{:S(2)}, u32[]{:S(2)}) collective-permute-start(bf16[3,16,8,128]{3,2,1,0:T(8,128)(2,1)S(1)} %get-tuple-element.44), channel_id=1, source_target_pairs={{1,2},{3,4},{5,6},{7,8},{9,10},{11,12},{13,14},{17,18},{19,20},{21... | collective-permute-start | bytes 294920 | tf_op jit(solution)/shard_map/ppermute | solution.py:51
  27.4 8.1 %collective-permute-start.6 = (bf16[6,16,8,128]{3,2,1,0:T(8,128)(2,1)S(1)}, bf16[6,16,8,128]{3,2,1,0:T(8,128)(2,1)S(1)}, u32[]{:S(2)}, u32[]{:S(2)}) collective-permute-start(bf16[6,16,8,128]{3,2,1,0:T(8,128)(2,1)S(1)} %get-tuple-element.49), channel_id=1, source_target_pairs={{0,1},{2,3},{4,5},{6,7},{8,9},{10,11},{12,13},{14,15},{16,17},{18,... | collective-permute-start | bytes 589832 | tf_op jit(solution)/shard_map/ppermute | solution.py:51
  27.5 8.0 %collective-permute-start.7 = (bf16[6,16,8,128]{3,2,1,0:T(8,128)(2,1)S(1)}, bf16[6,16,8,128]{3,2,1,0:T(8,128)(2,1)S(1)}, u32[]{:S(2)}, u32[]{:S(2)}) collective-permute-start(bf16[6,16,8,128]{3,2,1,0:T(8,128)(2,1)S(1)} %get-tuple-element.50), channel_id=1, source_target_pairs={{1,2},{3,4},{5,6},{7,8},{9,10},{11,12},{13,14},{17,18},{19,20},{21... | collective-permute-start | bytes 589832 | tf_op jit(solution)/shard_map/ppermute | solution.py:51
  38.0 5.5 %collective-permute-start.8 = (bf16[32,8,8,128]{3,2,1,0:T(8,128)(2,1)S(1)}, bf16[32,8,8,128]{3,2,1,0:T(8,128)(2,1)S(1)}, u32[]{:S(2)}, u32[]{:S(2)}) collective-permute-start(bf16[32,8,8,128]{3,2,1,0:T(8,128)(2,1)S(1)} %get-tuple-element.60), channel_id=1, source_target_pairs={{0,1},{2,3},{4,5},{6,7},{8,9},{10,11},{12,13},{14,15},{16,17},{18,... | collective-permute-start | bytes 1572872 | tf_op jit(solution)/shard_map/ppermute | solution.py:51
  38.1 13.5 %collective-permute-start.9 = (bf16[32,8,8,128]{3,2,1,0:T(8,128)(2,1)S(1)}, bf16[32,8,8,128]{3,2,1,0:T(8,128)(2,1)S(1)}, u32[]{:S(2)}, u32[]{:S(2)}) collective-permute-start(bf16[32,8,8,128]{3,2,1,0:T(8,128)(2,1)S(1)} %get-tuple-element.61), channel_id=1, source_target_pairs={{1,2},{3,4},{5,6},{7,8},{9,10},{11,12},{13,14},{17,18},{19,20},{21... | collective-permute-start | bytes 1572872 | tf_op jit(solution)/shard_map/ppermute | solution.py:51
  52.4 8.3 %collective-permute-start.10 = (bf16[3,16,8,128]{3,2,1,0:T(8,128)(2,1)S(1)}, bf16[3,16,8,128]{3,2,1,0:T(8,128)(2,1)S(1)}, u32[]{:S(2)}, u32[]{:S(2)}) collective-permute-start(bf16[3,16,8,128]{3,2,1,0:T(8,128)(2,1)S(1)} %get-tuple-element.63), channel_id=1, source_target_pairs={{0,1},{2,3},{4,5},{6,7},{8,9},{10,11},{12,13},{14,15},{16,17},{18,... | collective-permute-start | bytes 294920 | tf_op jit(solution)/shard_map/ppermute | solution.py:51
  52.5 8.2 %collective-permute-start.11 = (bf16[3,16,8,128]{3,2,1,0:T(8,128)(2,1)S(1)}, bf16[3,16,8,128]{3,2,1,0:T(8,128)(2,1)S(1)}, u32[]{:S(2)}, u32[]{:S(2)}) collective-permute-start(bf16[3,16,8,128]{3,2,1,0:T(8,128)(2,1)S(1)} %get-tuple-element.64), channel_id=1, source_target_pairs={{1,2},{3,4},{5,6},{7,8},{9,10},{11,12},{13,14},{17,18},{19,20},{21... | collective-permute-start | bytes 294920 | tf_op jit(solution)/shard_map/ppermute | solution.py:51

commit v5 on v4

--- a/solution.py
+++ b/solution.py
@@ -211,8 +211,10 @@
     return [(a, b - a) for a, b in zip(bounds, bounds[1:])]
 
 
-def features_kernel(frame, feat_hbm, near_ref, far_ref, w_ref, out_ref, *refs):
+def features_kernel(frame, passed, feat_hbm, near_ref, far_ref, w_ref, *refs):
     feat_ref, x_ref, pad_ref, sem, edge_sem = refs[-5:]
+    outs = refs[min(frame, 2):-5]
+    out_ref, edges = outs[0], outs[1:1 + passed]
     rows, across, _, chans = feat_ref.shape
     cols = across * BLK
     even, has_above, has_below = borders()
@@ -224,9 +226,12 @@
         loads.append(pltpu.make_async_copy(feat_hbm.at[frame, part], feat_ref.at[part], sem.at[n]))
         loads[-1].start()
     starts = (jnp.where(even, rows - HALO, 0), jnp.where(even, 0, rows - HALO))
-    for n, edge in enumerate(refs[:-5]):
+    for n, edge in enumerate(edges):
         part = pl.ds(starts[n], HALO)
         loads.append(pltpu.make_async_copy(feat_hbm.at[frame + 1, part], edge, edge_sem.at[n]))
+        loads[-1].start()
+    if frame:
+        loads.append(pltpu.make_async_copy(refs[0], outs[-1].at[frame - 1], edge_sem.at[2]))
         loads[-1].start()
     for row in range(-HALO, rows + HALO):
         if row < 0:
@@ -286,12 +291,9 @@
         pool_ref[q * across:(q + 1) * across, r] = done
 
 
-def inner_kernel(frame, last, part_ref, warped_ref, w1_ref, w2_ref, w3_ref, *refs):
-    if frame:
-        refs = refs[1:]
-    out_ref = refs[0]
-    pool_ref = None if last else refs[1]
-    m_edge, d_edge, x_ref, m_ref, d_ref, pad_ref, state_ref, sem = refs[-8:]
+def inner_kernel(last, part_ref, warped_ref, w1_ref, w2_ref, w3_ref, state_ref, *refs):
+    pool_ref = None if last else refs[0]
+    m_edge, d_edge, x_ref, m_ref, d_ref, pad_ref = refs[-6:]
     spread = shifter(pad_ref)
     rows, across, _, chans = warped_ref.shape
     cols = across * BLK
@@ -318,23 +320,19 @@
         for n, half, one in split_rows(value, pairs, cols, chans):
             centre = m_ref[pair + n + 1, half, :, chans:2 * chans]
             finish(state_ref, pool_ref, centre, one, 2 * (pair + n) + half, across, chans)
-        pltpu.make_async_copy(
-            state_ref.at[pl.ds(2 * pair, 2 * pairs)],
-            out_ref.at[frame, pl.ds(2 * pair, 2 * pairs)],
-            sem,
-        ).start()
-    inner = pl.ds(4, rows - 8)
-    pltpu.make_async_copy(state_ref.at[inner], out_ref.at[frame, inner], sem).wait()
 
 
 def border_kernel(frame, last, part_ref, warped_ref, near_ref, far_ref, w1_ref, w2_ref, w3_ref,
                   m_edge, d_edge, *refs):
     if last:
-        _, out_ref, x_ref, m_ref, d_ref, pad_ref, state_ref, sem = refs
+        state_in, _, out_ref, x_ref, m_ref, d_ref, pad_ref, sem, state_ref = refs
         pool_ref = None
+        inner = pl.ds(4, warped_ref.shape[0] - 8)
+        copies = [pltpu.make_async_copy(state_in.at[inner], out_ref.at[frame, inner], sem.at[2])]
+        copies[0].start()
     else:
-        _, _, near_vmem, far_vmem, out_ref, pool_ref, near_out, far_out = refs[:8]
-        x_ref, m_ref, d_ref, pad_ref, state_ref, sem, near_list, far_list = refs[8:]
+        _, _, near_vmem, far_vmem, state_ref, pool_ref, near_out, far_out = refs[:8]
+        x_ref, m_ref, d_ref, pad_ref, sem, near_list, far_list = refs[8:]
         lists = [
             pltpu.make_async_copy(near_vmem, near_list, sem.at[2]),
             pltpu.make_async_copy(far_vmem, far_list, sem.at[3]),
@@ -385,22 +383,23 @@
         for n, half, one in split_rows(value, 2, cols, chans):
             one = masked(one, 2 * (first + n) + half - 1)
             spread(d_ref.at[side], n + side, half, one)
-    copies = []
     for side in range(2):
         first = side * (half_rows - 2)
         value = edge_dot(d_ref, side, w3_ref)
         for n, half, one in split_rows(value, 2, cols, chans):
             centre = m_ref[side, n + 1 - side, half, :, chans:2 * chans]
             finish(state_ref, pool_ref, centre, one, 2 * (first + n) + half, across, chans)
-        part = pl.ds(side * (rows - 4), 4)
-        copies.append(pltpu.make_async_copy(state_ref.at[part], out_ref.at[frame, part], sem.at[side]))
-        copies[-1].start()
-    if not last:
+        if last:
+            part = pl.ds(side * (rows - 4), 4)
+            copies.append(pltpu.make_async_copy(state_ref.at[part], out_ref.at[frame, part], sem.at[side]))
+            copies[-1].start()
+    if last:
+        for copy in copies:
+            copy.wait()
+    else:
         for copy in lists:
             copy.wait()
         pack(pool_ref, near_list, far_list, frame + 1, near_out, far_out)
-    for copy in copies:
-        copy.wait()
 
 
 def on_device(state_start, features, row_moves, col_moves, merging_weight, first_weight, second_weight):
@@ -471,31 +470,39 @@
     def wide(extra):
         return pltpu.VMEM((rows // 2 + extra, 2, cols, 3 * chans), BF16)
 
-    def features_part(frame, near_feat, far_feat):
+    out_shape = shape_of((frames, rows, across, BLK, chans))
+
+    def features_part(frame, near_feat, far_feat, before, out):
         passed = 0 if frame == frames - 1 else 2
+        done = ([resident(before)] if frame else []) + ([out] if frame > 1 else [])
         return pl.pallas_call(
-            functools.partial(features_kernel, frame),
-            out_shape=[on_chip((rows // 2 + 2, cols, 2 * chans), F32)] + [on_chip(edge_shape)] * passed,
-            in_specs=[ANY] + [VMEM] * 3,
-            out_specs=[VMEM] * (1 + passed),
+            functools.partial(features_kernel, frame, passed),
+            out_shape=[on_chip((rows // 2 + 2, cols, 2 * chans), F32)]
+            + [on_chip(edge_shape)] * passed
+            + [out_shape] * (frame > 0),
+            in_specs=[ANY] + [VMEM] * 3 + [VMEM] * (frame > 0) + [ANY] * (frame > 1),
+            out_specs=[VMEM] * (1 + passed) + [ANY] * (frame > 0),
+            input_output_aliases={5: 1 + passed} if frame > 1 else {},
             scratch_shapes=[
                 pltpu.VMEM((rows, across, BLK, chans), BF16),
                 wide(3),
                 pad_rows,
                 pltpu.SemaphoreType.DMA((4,)),
-                pltpu.SemaphoreType.DMA((2,)),
+                pltpu.SemaphoreType.DMA((3,)),
             ],
             compiler_params=room(16),
             name="features",
-        )(in_hbm(feats), resident(near_feat), resident(far_feat), resident(w_feat))
-
-    out = None
-    out_shape = shape_of((frames, rows, across, BLK, chans))
+        )(in_hbm(feats), resident(near_feat), resident(far_feat), resident(w_feat), *done)
+
+    out = state_now = None
+    state_shape = on_chip((rows, across, BLK, chans))
     edge_pairs = on_chip((2, 2, cols, 3 * chans))
     for frame in range(frames):
         last = frame == frames - 1
         near_got, far_got = swap_both(near_msg, far_msg)
-        part, *next_edges = features_part(frame, near_feat, far_feat)
+        part, *next_edges = features_part(frame, near_feat, far_feat, state_now, out)
+        if frame:
+            out = next_edges.pop()
         sent_edge = on_chip(((1 if last else 2) * HALO,) + edge_shape[1:])
         warped, near_edge, far_edge = pl.pallas_call(
             functools.partial(assemble_kernel, frame),
@@ -513,56 +520,50 @@
         near_halo, far_halo = swap_both(near_edge, far_edge)
         near_feat, far_feat = near_halo, far_halo
         args = tuple(map(resident, (part, warped, w_warp, w_first, w_second)))
-        results = pl.pallas_call(
-            functools.partial(inner_kernel, frame, last),
-            out_shape=[out_shape] + [pool_shape] * (not last) + [edge_pairs] * 2,
-            in_specs=[VMEM] * 5 + [ANY] * (frame > 0),
-            out_specs=[ANY] + [VMEM] * (2 + (not last)),
-            input_output_aliases={5: 0} if frame else {},
-            scratch_shapes=[
-                wide(3),
-                wide(2),
-                wide(1),
-            pad_rows,
-                pltpu.VMEM((rows, across, BLK, chans), BF16),
-                pltpu.SemaphoreType.DMA,
-            ],
+        state_now, *results = pl.pallas_call(
+            functools.partial(inner_kernel, last),
+            out_shape=[state_shape] + [pool_shape] * (not last) + [edge_pairs] * 2,
+            in_specs=[VMEM] * 5,
+            out_specs=[VMEM] * (3 + (not last)),
+            scratch_shapes=[wide(3), wide(2), wide(1), pad_rows],
             compiler_params=room(24),
             name="inner",
-        )(*args, *([out] if frame else []))
-        out = results[0]
+        )(*args)
         m_edge, d_edge = results[-2:]
         args = tuple(map(resident, (
             part, warped, near_halo, far_halo, w_warp, w_first, w_second, m_edge, d_edge
         )))
         scratch = [pltpu.VMEM((2, 3, 2, cols, 3 * chans), BF16) for _ in range(3)] + [
             pad_rows,
-            pltpu.VMEM((rows, across, BLK, chans), BF16),
             pltpu.SemaphoreType.DMA((4,)),
-        ] + [pltpu.SMEM((frames, list_len), jnp.int32)] * (0 if last else 2)
+        ]
+        if last:
+            scratch.append(pltpu.VMEM((rows, across, BLK, chans), BF16))
+        else:
+            scratch += [pltpu.SMEM((frames, list_len), jnp.int32)] * 2
         kernel = functools.partial(border_kernel, frame, last)
         if last:
             out = pl.pallas_call(
                 kernel,
                 out_shape=out_shape,
-                in_specs=[VMEM] * 9 + [ANY],
+                in_specs=[VMEM] * 10 + [ANY],
                 out_specs=ANY,
-                input_output_aliases={9: 0},
+                input_output_aliases={10: 0},
                 scratch_shapes=scratch,
                 compiler_params=room(12),
                 name="border",
-            )(*args, out)
+            )(*args, resident(state_now), out)
         else:
-            out, pool, near_msg, far_msg = pl.pallas_call(
+            state_now, pool, near_msg, far_msg = pl.pallas_call(
                 kernel,
-                out_shape=[out_shape, pool_shape, message, message],
-                in_specs=[VMEM] * 9 + [ANY] + [VMEM] * 3,
-                out_specs=[ANY] + [VMEM] * 3,
+                out_shape=[state_shape, pool_shape, message, message],
+                in_specs=[VMEM] * 13,
+                out_specs=[VMEM] * 4,
                 input_output_aliases={9: 0, 10: 1},
                 scratch_shapes=scratch,
                 compiler_params=room(12),
                 name="border",
-            )(*args, out, resident(results[1]), resident(near_list), resident(far_list))
+            )(*args, *map(resident, (state_now, results[0], near_list, far_list)))
     return out.reshape(frames, rows, cols, chans)
 
 

time: 63.6 us -> 60.8 us (0.956)
  Pallas kernels: 28.1 us -> 26.1 us
  waiting for transfers between devices: 20.7 us -> 19.3 us
  starting transfers between devices: 14.2 us -> 14.9 us
    pallas_call x6, Pallas kernels: 23.1 us -> 21.1 us  [the longest x2 9.29 us: on_device(): pl.pallas_call(functools.partial(inner_kernel, last), out_shape=[state_sh...]
    ppermute x12, waiting for transfers between devices: 20.7 us -> 19.3 us  [swap(): return lax.ppermute(x, ('clips', 'rows'), neighbours(first))]
    ppermute x12, starting transfers between devices: 14.2 us -> 14.9 us  [swap(): return lax.ppermute(x, ('clips', 'rows'), neighbours(first))]
  transfers between devices with their start and end apart: 12 -> 12, of which waited for: 3 -> 4; matrix products, arithmetic and copies ran while one was open for 0% -> 0% of each run, Pallas kernels for 31% -> 30%
where the time goes in v5:
time: 60.8 us; the launch traced here: 60.6 us
  Pallas kernels  26.1 us (43%)
  waiting for transfers between devices  19.3 us (32%)
  starting transfers between devices  14.9 us (25%)
    ppermute x12, waiting for transfers between devices, swap(): return lax.ppermute(x, ('clips', 'rows'), neighbours(first))  19.3 us
    ppermute x12, starting transfers between devices, swap(): return lax.ppermute(x, ('clips', 'rows'), neighbours(first))  14.9 us
    pallas_call x2, Pallas kernels, on_device(): pl.pallas_call(functools.partial(inner_kernel, last), out_shape=[state_sh...  9.29 us
    pallas_call x2, Pallas kernels, features_part(): pl.pallas_call(functools.partial(features_kernel, frame, passed), out_sha...  7.47 us
    pallas_call x1, Pallas kernels, on_device(): pl.pallas_call(kernel, out_shape=out_shape, in_specs=[VMEM] * 10 + [ANY],...  2.5 us
    pallas_call x1, Pallas kernels, on_device(): pl.pallas_call(kernel, out_shape=[state_shape, pool_shape, message, messa...  1.89 us
    pallas_call x2, Pallas kernels, on_device(): pl.pallas_call(functools.partial(assemble_kernel, frame), out_shape=[on_c...  1.59 us
    pallas_call x1, Pallas kernels, on_device(): pl.pallas_call(weights_kernel, out_shape=[pair_shape] * 4, in_specs=[ANY]...  1.5 us
  transfers between devices with their start and end apart: 12, of which 4 were waited for; matrix products, arithmetic and copies ran while one was open for 0% of the time, Pallas kernels for 30%

profile of v5, /device:TPU:1, one launch (start us, length us, event | category | flops | bytes accessed | tf_op | source)
XLA Modules:
  0.0 60.6 jit_solution(4709005228499084269)
XLA Ops:
  0.0 1.3 %tables.1 = (s32[2,64]{1,0:T(2,128)S(1)}, s32[2,40]{1,0:T(2,128)S(1)}, s32[2,40]{1,0:T(2,128)S(1)}, bf16[3,16,8,128]{3,2,1,0:T(8,128)(2,1)S(1)}, bf16[3,16,8,128...) custom-call(s32[2,64]{1,0:T(2,128)} %row_hbm.1, s32[2,64]{1,0:T(2,128)} %col_hbm.1, ...), custom_call_target="tpu_custom_call" | custom-call | tf_op jit(solution)/shard_map/tables/pallas_call | solution.py:420
  1.3 0.1 collective-permute-start
  1.4 2.7 %collective-permute-start.1 = (s32[2,40]{1,0:T(2,128)S(1)}, s32[2,40]{1,0:T(2,128)S(1)}, u32[]{:S(2)}, u32[]{:S(2)}) collective-permute-start(s32[2,40]{1,0:T(2,128)S(1)} %get-tuple-element.42), channel_id=1, source_target_pairs={{1,2},{3,4},{5,6},{7,8},{9,10},{11,12},{13,14},{17,18},{19,20},{21... | collective-permute-start | bytes 968 | tf_op jit(solution)/shard_map/ppermute | solution.py:51
  4.1 1.5 %collective-permute-done.1.far_list.refs_3_ = s32[2,40]{1,0:T(2,128)S(1)} collective-permute-done((s32[2,40]{1,0:T(2,128)S(1)}, s32[2,40]{1,0:T(2,128)S(1)}, u32[]{:S(2)}, u32[]{:S(2)}) %collective-permute-start.1) | collective-permute-done | bytes 352 | tf_op jit(solution)/shard_map/ppermute | solution.py:51
  5.6 0.6 %pack.1 = (bf16[32,8,8,128]{3,2,1,0:T(8,128)(2,1)S(1)}, bf16[32,8,8,128]{3,2,1,0:T(8,128)(2,1)S(1)}) custom-call(bf16[64,8,8,128]{3,2,1,0:T(8,128)(2,1)S(1)} %get-tuple-element.40.pool_ref, s32[2,40]{1,0:T(2,128)S(1)} %collective-permute-done.near_list.refs_2_, s32[2,40]{1,0:T(2,128)S(1)} %collective-permute-done.1.far_list.refs_3_), custom_call_target="tpu_custom_call" | custom-call | tf_op jit(solution)/shard_map/pack/pallas_call | solution.py:443
  6.2 1.5 %collective-permute-start.3 = (bf16[32,8,8,128]{3,2,1,0:T(8,128)(2,1)S(1)}, bf16[32,8,8,128]{3,2,1,0:T(8,128)(2,1)S(1)}, u32[]{:S(2)}, u32[]{:S(2)}) collective-permute-start(bf16[32,8,8,128]{3,2,1,0:T(8,128)(2,1)S(1)} %get-tuple-element.44), channel_id=1, source_target_pairs={{1,2},{3,4},{5,6},{7,8},{9,10},{11,12},{13,14},{17,18},{19,20},{21... | collective-permute-start | bytes 1572872 | tf_op jit(solution)/shard_map/ppermute | solution.py:51
  7.8 0.9 %collective-permute-start.2 = (bf16[32,8,8,128]{3,2,1,0:T(8,128)(2,1)S(1)}, bf16[32,8,8,128]{3,2,1,0:T(8,128)(2,1)S(1)}, u32[]{:S(2)}, u32[]{:S(2)}) collective-permute-start(bf16[32,8,8,128]{3,2,1,0:T(8,128)(2,1)S(1)} %get-tuple-element.43._), channel_id=1, source_target_pairs={{0,1},{2,3},{4,5},{6,7},{8,9},{10,11},{12,13},{14,15},{16,17},{18,... | collective-permute-start | bytes 1572872 | tf_op jit(solution)/shard_map/ppermute | solution.py:51
  8.7 1.6 %collective-permute-start.5 = (bf16[3,16,8,128]{3,2,1,0:T(8,128)(2,1)S(1)}, bf16[3,16,8,128]{3,2,1,0:T(8,128)(2,1)S(1)}, u32[]{:S(2)}, u32[]{:S(2)}) collective-permute-start(bf16[3,16,8,128]{3,2,1,0:T(8,128)(2,1)S(1)} %get-tuple-element.46), channel_id=1, source_target_pairs={{1,2},{3,4},{5,6},{7,8},{9,10},{11,12},{13,14},{17,18},{19,20},{21... | collective-permute-start | bytes 294920 | tf_op jit(solution)/shard_map/ppermute | solution.py:51
  10.3 1.5 %weights.1 = (bf16[1536,256]{1,0:T(8,128)(2,1)S(1)}, bf16[1536,256]{1,0:T(8,128)(2,1)S(1)}, bf16[1536,256]{1,0:T(8,128)(2,1)S(1)}, bf16[1536,256]{1,0:T(8,128)(2,1)S(1)}) custom-call(bf16[3,3,256,128]{3,2,1,0:T(8,128)(2,1)} %merging_hbm.1, bf16[3,3,128,128]{3,2,1,0:T(8,128)(2,1)} %first_hbm.1, bf16[3,3,128,128]{3,2,1,0:T(8,128)(2,1)} %second_hbm.1, ...), custom_call_target="tpu_custom_call" | custom-call | tf_op jit(solution)/shard_map/weights/pallas_call | solution.py:453
  11.8 9.8 %collective-permute-done.5.far_ref = bf16[3,16,8,128]{3,2,1,0:T(8,128)(2,1)S(1)} collective-permute-done((bf16[3,16,8,128]{3,2,1,0:T(8,128)(2,1)S(1)}, bf16[3,16,8,128]{3,2,1,0:T(8,128)(2,1)S(1)}, u32[]{:S(2)}, u32[]{:S(2)}) %collective-permute-start.5) | collective-permute-done | bytes 98336 | tf_op jit(solution)/shard_map/ppermute | solution.py:51
  21.6 3.6 %features.2 = (f32[18,128,256]{2,1,0:T(8,128)S(1)}, bf16[3,16,8,128]{3,2,1,0:T(8,128)(2,1)S(1)}, bf16[3,16,8,128]{3,2,1,0:T(8,128)(2,1)S(1)}) custom-call(bf16[2,32,16,8,128]{4,3,2,1,0:T(8,128)(2,1)} %bitcast.4, bf16[3,16,8,128]{3,2,1,0:T(8,128)(2,1)S(1)} %collective-permute-done.4.near_ref, bf16[3,16,8,128]{3,2,1,0:T(8,128)(2,1)S(1)} %collective-permute-done.5.far_ref, ...), custom_call_target="tpu_custom_call" | custom-call | tf_op jit(solution)/shard_map/features/pallas_call | solution.py:478
  25.3 0.8 %assemble.2 = (bf16[32,16,8,128]{3,2,1,0:T(8,128)(2,1)S(1)}, bf16[6,16,8,128]{3,2,1,0:T(8,128)(2,1)S(1)}, bf16[6,16,8,128]{3,2,1,0:T(8,128)(2,1)S(1)}) custom-call(s32[2,64]{1,0:T(2,128)S(1)} %get-tuple-element.39.table_vmem, bf16[64,8,8,128]{3,2,1,0:T(8,128)(2,1)S(1)} %get-tuple-element.40.pool_ref, ...), custom_call_target="tpu_custom_call" | custom-call | tf_op jit(solution)/shard_map/assemble/pallas_call | solution.py:507
  26.1 0.1 collective-permute-start.6
  26.1 2.5 %collective-permute-start.7 = (bf16[6,16,8,128]{3,2,1,0:T(8,128)(2,1)S(1)}, bf16[6,16,8,128]{3,2,1,0:T(8,128)(2,1)S(1)}, u32[]{:S(2)}, u32[]{:S(2)}) collective-permute-start(bf16[6,16,8,128]{3,2,1,0:T(8,128)(2,1)S(1)} %get-tuple-element.52), channel_id=1, source_target_pairs={{1,2},{3,4},{5,6},{7,8},{9,10},{11,12},{13,14},{17,18},{19,20},{21... | collective-permute-start | bytes 589832 | tf_op jit(solution)/shard_map/ppermute | solution.py:51
  28.7 4.7 %inner.2 = (bf16[32,16,8,128]{3,2,1,0:T(8,128)(2,1)S(1)}, bf16[64,8,8,128]{3,2,1,0:T(8,128)(2,1)S(1)}, bf16[2,2,128,384]{3,2,1,0:T(8,128)(2,1)S(1)}, bf16[2,2,128,384]{3,2,1,0:T(8,128)(2,1)S(1)}) custom-call(f32[18,128,256]{2,1,0:T(8,128)S(1)} %get-tuple-element.48._.part_ref, bf16[32,16,8,128]{3,2,1,0:T(8,128)(2,1)S(1)} %get-tuple-element.53.warped_ref, ...), custom_call_target="tpu_custom_call" | custom-call | tf_op jit(solution)/shard_map/inner/pallas_call | solution.py:523
  33.4 1.9 %border.2 = (bf16[32,16,8,128]{3,2,1,0:T(8,128)(2,1)S(1)}, bf16[64,8,8,128]{3,2,1,0:T(8,128)(2,1)S(1)}, bf16[32,8,8,128]{3,2,1,0:T(8,128)(2,1)S(1)}, bf16[32,8,8,128]{3,2,1,0:T(8,128)(2,1)S(1)}) custom-call(f32[18,128,256]{2,1,0:T(8,128)S(1)} %get-tuple-element.48._.part_ref, ...), custom_call_target="tpu_custom_call", output_to_operand_aliasing={{0}: (9, {}), {1}: (10, {})} | custom-call | tf_op jit(solution)/shard_map/border/pallas_call | solution.py:557
  35.3 0.1 collective-permute-start.8
  35.4 2.5 %collective-permute-start.9 = (bf16[32,8,8,128]{3,2,1,0:T(8,128)(2,1)S(1)}, bf16[32,8,8,128]{3,2,1,0:T(8,128)(2,1)S(1)}, u32[]{:S(2)}, u32[]{:S(2)}) collective-permute-start(bf16[32,8,8,128]{3,2,1,0:T(8,128)(2,1)S(1)} %get-tuple-element.65), channel_id=1, source_target_pairs={{1,2},{3,4},{5,6},{7,8},{9,10},{11,12},{13,14},{17,18},{19,20},{21... | collective-permute-start | bytes 1572872 | tf_op jit(solution)/shard_map/ppermute | solution.py:51
  37.9 3.9 %features.3 = (f32[18,128,256]{2,1,0:T(8,128)S(1)}, bf16[2,32,16,8,128]{4,3,2,1,0:T(8,128)(2,1)}) custom-call(bf16[2,32,16,8,128]{4,3,2,1,0:T(8,128)(2,1)} %bitcast.5, bf16[6,16,8,128]{3,2,1,0:T(8,128)(2,1)S(1)} %collective-permute-done.6.near_ref, bf16[6,16,8,128]{3,2,1,0:T(8,128)(2,1)S(1)} %collective-permute-done.7.far_ref, ...), custom_call_target="tpu_custom_call" | custom-call | tf_op jit(solution)/shard_map/features/pallas_call | solution.py:478
  41.8 7.9 %collective-permute-done.9.far_ref = bf16[32,8,8,128]{3,2,1,0:T(8,128)(2,1)S(1)} collective-permute-done((bf16[32,8,8,128]{3,2,1,0:T(8,128)(2,1)S(1)}, bf16[32,8,8,128]{3,2,1,0:T(8,128)(2,1)S(1)}, u32[]{:S(2)}, u32[]{:S(2)}) %collective-permute-start.9) | collective-permute-done | bytes 524320 | tf_op jit(solution)/shard_map/ppermute | solution.py:51
  49.7 0.8 %assemble.3 = (bf16[32,16,8,128]{3,2,1,0:T(8,128)(2,1)S(1)}, bf16[3,16,8,128]{3,2,1,0:T(8,128)(2,1)S(1)}, bf16[3,16,8,128]{3,2,1,0:T(8,128)(2,1)S(1)}) custom-call(s32[2,64]{1,0:T(2,128)S(1)} %get-tuple-element.39.table_vmem, bf16[64,8,8,128]{3,2,1,0:T(8,128)(2,1)S(1)} %get-tuple-element.63.pool_ref, ...), custom_call_target="tpu_custom_call" | custom-call | tf_op jit(solution)/shard_map/assemble/pallas_call | solution.py:507
  50.5 2.7 %collective-permute-start.11 = (bf16[3,16,8,128]{3,2,1,0:T(8,128)(2,1)S(1)}, bf16[3,16,8,128]{3,2,1,0:T(8,128)(2,1)S(1)}, u32[]{:S(2)}, u32[]{:S(2)}) collective-permute-start(bf16[3,16,8,128]{3,2,1,0:T(8,128)(2,1)S(1)} %get-tuple-element.68), channel_id=1, source_target_pairs={{1,2},{3,4},{5,6},{7,8},{9,10},{11,12},{13,14},{17,18},{19,20},{21... | collective-permute-start | bytes 294920 | tf_op jit(solution)/shard_map/ppermute | solution.py:51
  53.3 4.6 %inner.3 = (bf16[32,16,8,128]{3,2,1,0:T(8,128)(2,1)S(1)}, bf16[2,2,128,384]{3,2,1,0:T(8,128)(2,1)S(1)}, bf16[2,2,128,384]{3,2,1,0:T(8,128)(2,1)S(1)}) custom-call(f32[18,128,256]{2,1,0:T(8,128)S(1)} %get-tuple-element.62._.part_ref, bf16[32,16,8,128]{3,2,1,0:T(8,128)(2,1)S(1)} %get-tuple-element.66.warped_ref, ...), custom_call_target="tpu_custom_call" | custom-call | tf_op jit(solution)/shard_map/inner/pallas_call | solution.py:523
  57.9 2.5 %border.3 = bf16[2,32,16,8,128]{4,3,2,1,0:T(8,128)(2,1)} custom-call(f32[18,128,256]{2,1,0:T(8,128)S(1)} %get-tuple-element.62._.part_ref, bf16[32,16,8,128]{3,2,1,0:T(8,128)(2,1)S(1)} %get-tuple-element.66.warped_ref, bf16[3,16,8,128]{3,2,1,0:T(8,128)(2,1)S(1)} %collective-permute-done.10.near_ref, ...), custom_call_target="tpu_custom_call", output_to_operand_aliasing={{}: (10, {})} | custom-call | tf_op jit(solution)/shard_map/border/pallas_call | solution.py:546
  (11 shorter events, 0.1 us)
Async XLA Ops:
  1.3 2.8 %collective-permute-start = (s32[2,40]{1,0:T(2,128)S(1)}, s32[2,40]{1,0:T(2,128)S(1)}, u32[]{:S(2)}, u32[]{:S(2)}) collective-permute-start(s32[2,40]{1,0:T(2,128)S(1)} %get-tuple-element.41), channel_id=1, source_target_pairs={{0,1},{2,3},{4,5},{6,7},{8,9},{10,11},{12,13},{14,15},{16,17},{18,... | collective-permute-start | bytes 968 | tf_op jit(solution)/shard_map/ppermute | solution.py:51
  1.4 4.2 %collective-permute-start.1 = (s32[2,40]{1,0:T(2,128)S(1)}, s32[2,40]{1,0:T(2,128)S(1)}, u32[]{:S(2)}, u32[]{:S(2)}) collective-permute-start(s32[2,40]{1,0:T(2,128)S(1)} %get-tuple-element.42), channel_id=1, source_target_pairs={{1,2},{3,4},{5,6},{7,8},{9,10},{11,12},{13,14},{17,18},{19,20},{21... | collective-permute-start | bytes 968 | tf_op jit(solution)/shard_map/ppermute | solution.py:51
  6.2 19.0 %collective-permute-start.3 = (bf16[32,8,8,128]{3,2,1,0:T(8,128)(2,1)S(1)}, bf16[32,8,8,128]{3,2,1,0:T(8,128)(2,1)S(1)}, u32[]{:S(2)}, u32[]{:S(2)}) collective-permute-start(bf16[32,8,8,128]{3,2,1,0:T(8,128)(2,1)S(1)} %get-tuple-element.44), channel_id=1, source_target_pairs={{1,2},{3,4},{5,6},{7,8},{9,10},{11,12},{13,14},{17,18},{19,20},{21... | collective-permute-start | bytes 1572872 | tf_op jit(solution)/shard_map/ppermute | solution.py:51
  7.8 17.5 %collective-permute-start.2 = (bf16[32,8,8,128]{3,2,1,0:T(8,128)(2,1)S(1)}, bf16[32,8,8,128]{3,2,1,0:T(8,128)(2,1)S(1)}, u32[]{:S(2)}, u32[]{:S(2)}) collective-permute-start(bf16[32,8,8,128]{3,2,1,0:T(8,128)(2,1)S(1)} %get-tuple-element.43._), channel_id=1, source_target_pairs={{0,1},{2,3},{4,5},{6,7},{8,9},{10,11},{12,13},{14,15},{16,17},{18,... | collective-permute-start | bytes 1572872 | tf_op jit(solution)/shard_map/ppermute | solution.py:51
  8.7 3.1 %collective-permute-start.4 = (bf16[3,16,8,128]{3,2,1,0:T(8,128)(2,1)S(1)}, bf16[3,16,8,128]{3,2,1,0:T(8,128)(2,1)S(1)}, u32[]{:S(2)}, u32[]{:S(2)}) collective-permute-start(bf16[3,16,8,128]{3,2,1,0:T(8,128)(2,1)S(1)} %get-tuple-element.45), channel_id=1, source_target_pairs={{0,1},{2,3},{4,5},{6,7},{8,9},{10,11},{12,13},{14,15},{16,17},{18,... | collective-permute-start | bytes 294920 | tf_op jit(solution)/shard_map/ppermute | solution.py:51
  8.7 12.9 %collective-permute-start.5 = (bf16[3,16,8,128]{3,2,1,0:T(8,128)(2,1)S(1)}, bf16[3,16,8,128]{3,2,1,0:T(8,128)(2,1)S(1)}, u32[]{:S(2)}, u32[]{:S(2)}) collective-permute-start(bf16[3,16,8,128]{3,2,1,0:T(8,128)(2,1)S(1)} %get-tuple-element.46), channel_id=1, source_target_pairs={{1,2},{3,4},{5,6},{7,8},{9,10},{11,12},{13,14},{17,18},{19,20},{21... | collective-permute-start | bytes 294920 | tf_op jit(solution)/shard_map/ppermute | solution.py:51
  26.1 7.3 %collective-permute-start.6 = (bf16[6,16,8,128]{3,2,1,0:T(8,128)(2,1)S(1)}, bf16[6,16,8,128]{3,2,1,0:T(8,128)(2,1)S(1)}, u32[]{:S(2)}, u32[]{:S(2)}) collective-permute-start(bf16[6,16,8,128]{3,2,1,0:T(8,128)(2,1)S(1)} %get-tuple-element.51), channel_id=1, source_target_pairs={{0,1},{2,3},{4,5},{6,7},{8,9},{10,11},{12,13},{14,15},{16,17},{18,... | collective-permute-start | bytes 589832 | tf_op jit(solution)/shard_map/ppermute | solution.py:51
  26.1 7.3 %collective-permute-start.7 = (bf16[6,16,8,128]{3,2,1,0:T(8,128)(2,1)S(1)}, bf16[6,16,8,128]{3,2,1,0:T(8,128)(2,1)S(1)}, u32[]{:S(2)}, u32[]{:S(2)}) collective-permute-start(bf16[6,16,8,128]{3,2,1,0:T(8,128)(2,1)S(1)} %get-tuple-element.52), channel_id=1, source_target_pairs={{1,2},{3,4},{5,6},{7,8},{9,10},{11,12},{13,14},{17,18},{19,20},{21... | collective-permute-start | bytes 589832 | tf_op jit(solution)/shard_map/ppermute | solution.py:51
  35.3 6.5 %collective-permute-start.8 = (bf16[32,8,8,128]{3,2,1,0:T(8,128)(2,1)S(1)}, bf16[32,8,8,128]{3,2,1,0:T(8,128)(2,1)S(1)}, u32[]{:S(2)}, u32[]{:S(2)}) collective-permute-start(bf16[32,8,8,128]{3,2,1,0:T(8,128)(2,1)S(1)} %get-tuple-element.64), channel_id=1, source_target_pairs={{0,1},{2,3},{4,5},{6,7},{8,9},{10,11},{12,13},{14,15},{16,17},{18,... | collective-permute-start | bytes 1572872 | tf_op jit(solution)/shard_map/ppermute | solution.py:51
  35.4 14.3 %collective-permute-start.9 = (bf16[32,8,8,128]{3,2,1,0:T(8,128)(2,1)S(1)}, bf16[32,8,8,128]{3,2,1,0:T(8,128)(2,1)S(1)}, u32[]{:S(2)}, u32[]{:S(2)}) collective-permute-start(bf16[32,8,8,128]{3,2,1,0:T(8,128)(2,1)S(1)} %get-tuple-element.65), channel_id=1, source_target_pairs={{1,2},{3,4},{5,6},{7,8},{9,10},{11,12},{13,14},{17,18},{19,20},{21... | collective-permute-start | bytes 1572872 | tf_op jit(solution)/shard_map/ppermute | solution.py:51
  50.5 7.5 %collective-permute-start.10 = (bf16[3,16,8,128]{3,2,1,0:T(8,128)(2,1)S(1)}, bf16[3,16,8,128]{3,2,1,0:T(8,128)(2,1)S(1)}, u32[]{:S(2)}, u32[]{:S(2)}) collective-permute-start(bf16[3,16,8,128]{3,2,1,0:T(8,128)(2,1)S(1)} %get-tuple-element.67), channel_id=1, source_target_pairs={{0,1},{2,3},{4,5},{6,7},{8,9},{10,11},{12,13},{14,15},{16,17},{18,... | collective-permute-start | bytes 294920 | tf_op jit(solution)/shard_map/ppermute | solution.py:51
  50.5 7.4 %collective-permute-start.11 = (bf16[3,16,8,128]{3,2,1,0:T(8,128)(2,1)S(1)}, bf16[3,16,8,128]{3,2,1,0:T(8,128)(2,1)S(1)}, u32[]{:S(2)}, u32[]{:S(2)}) collective-permute-start(bf16[3,16,8,128]{3,2,1,0:T(8,128)(2,1)S(1)} %get-tuple-element.68), channel_id=1, source_target_pairs={{1,2},{3,4},{5,6},{7,8},{9,10},{11,12},{13,14},{17,18},{19,20},{21... | collective-permute-start | bytes 294920 | tf_op jit(solution)/shard_map/ppermute | solution.py:51

commit v6 on v5

--- a/solution.py
+++ b/solution.py
@@ -128,7 +128,8 @@
             out[frame:frame + 1] = got.astype(jnp.int32)
     for copy in edges:
         copy.wait()
-    pltpu.make_async_copy(pool_ref, pool_ref, sem.at[4]).wait()
+    own = pool_ref.at[pl.ds(0, blocks)]
+    pltpu.make_async_copy(own, own, sem.at[4]).wait()
 
 
 def weights_kernel(merging_hbm, first_hbm, second_hbm, _,
@@ -259,14 +260,13 @@
     table_copy = pltpu.make_async_copy(table_vmem, table_ref, table_sem)
     table_copy.start()
     rows, across = warped_out.shape[:2]
-    blocks = pool_ref.shape[0]
+    blocks = table_vmem.shape[1]
     slots = near_ref.shape[0]
     odd = lax.rem(lax.axis_index("rows"), 2)
     near_rows = pl.ds(jnp.where(odd == 0, rows - HALO, 0), HALO)
     far_rows = pl.ds(jnp.where(odd == 0, 0, rows - HALO), HALO)
     for edge, feat_edge in zip((near_edge, far_edge), refs[:-6]):
         edge[HALO:2 * HALO] = feat_edge[...]
-    all_ref[0:blocks] = pool_ref[...]
     all_ref[blocks:blocks + slots] = near_ref[...]
     all_ref[blocks + slots:blocks + 2 * slots] = far_ref[...]
     table_copy.wait()
@@ -414,7 +414,7 @@
     feats = features.reshape(frames, rows, across, BLK, chans)
     block_shape = (BLK, BLK, chans)
     edge_shape = (HALO, across, BLK, chans)
-    pool_shape = on_chip((blocks,) + block_shape)
+    pool_shape = on_chip((blocks + 2 * slots,) + block_shape)
     message = on_chip((slots,) + block_shape)
 
     table, near_list, far_list, near_feat, far_feat, pool = pl.pallas_call(
@@ -504,13 +504,13 @@
         if frame:
             out = next_edges.pop()
         sent_edge = on_chip(((1 if last else 2) * HALO,) + edge_shape[1:])
-        warped, near_edge, far_edge = pl.pallas_call(
+        warped, near_edge, far_edge, _ = pl.pallas_call(
             functools.partial(assemble_kernel, frame),
-            out_shape=[on_chip((rows, across, BLK, chans)), sent_edge, sent_edge],
+            out_shape=[on_chip((rows, across, BLK, chans)), sent_edge, sent_edge, pool_shape],
             in_specs=[VMEM] * 4 + [ANY] + [VMEM] * len(next_edges),
-            out_specs=[VMEM] * 3,
+            out_specs=[VMEM] * 4,
+            input_output_aliases={1: 3},
             scratch_shapes=[
-                pltpu.VMEM((blocks + 2 * slots,) + block_shape, BF16),
                 pltpu.SMEM((frames, blocks), jnp.int32),
                 pltpu.SemaphoreType.DMA,
             ],

time: 60.8 us -> 60.8 us (level)
  no operation moved by 1% of the time
where the time goes in v6:
time: 60.8 us; the launch traced here: 60.6 us
  Pallas kernels  26.3 us (43%)
  waiting for transfers between devices  19.3 us (32%)
  starting transfers between devices  14.7 us (24%)
    ppermute x12, waiting for transfers between devices, swap(): return lax.ppermute(x, ('clips', 'rows'), neighbours(first))  19.3 us
    ppermute x12, starting transfers between devices, swap(): return lax.ppermute(x, ('clips', 'rows'), neighbours(first))  14.7 us
    pallas_call x2, Pallas kernels, on_device(): pl.pallas_call(functools.partial(inner_kernel, last), out_shape=[state_sh...  9.46 us
    pallas_call x2, Pallas kernels, features_part(): pl.pallas_call(functools.partial(features_kernel, frame, passed), out_sha...  7.47 us
    pallas_call x1, Pallas kernels, on_device(): pl.pallas_call(kernel, out_shape=out_shape, in_specs=[VMEM] * 10 + [ANY],...  2.5 us
    pallas_call x1, Pallas kernels, on_device(): pl.pallas_call(kernel, out_shape=[state_shape, pool_shape, message, messa...  1.89 us
    pallas_call x2, Pallas kernels, on_device(): pl.pallas_call(functools.partial(assemble_kernel, frame), out_shape=[on_c...  1.59 us
    pallas_call x1, Pallas kernels, on_device(): pl.pallas_call(weights_kernel, out_shape=[pair_shape] * 4, in_specs=[ANY]...  1.5 us
  transfers between devices with their start and end apart: 12, of which 4 were waited for; matrix products, arithmetic and copies ran while one was open for 0% of the time, Pallas kernels for 30%

profile of v6, /device:TPU:1, one launch (start us, length us, event | category | flops | bytes accessed | tf_op | source)
XLA Modules:
  0.0 60.6 jit_solution(6137914049851458405)
XLA Ops:
  0.0 1.3 %tables.1 = (s32[2,64]{1,0:T(2,128)S(1)}, s32[2,40]{1,0:T(2,128)S(1)}, s32[2,40]{1,0:T(2,128)S(1)}, bf16[3,16,8,128]{3,2,1,0:T(8,128)(2,1)S(1)}, bf16[3,16,8,128...) custom-call(s32[2,64]{1,0:T(2,128)} %row_hbm.1, s32[2,64]{1,0:T(2,128)} %col_hbm.1, ...), custom_call_target="tpu_custom_call" | custom-call | tf_op jit(solution)/shard_map/tables/pallas_call | solution.py:420
  1.3 0.1 collective-permute-start
  1.4 2.7 %collective-permute-start.1 = (s32[2,40]{1,0:T(2,128)S(1)}, s32[2,40]{1,0:T(2,128)S(1)}, u32[]{:S(2)}, u32[]{:S(2)}) collective-permute-start(s32[2,40]{1,0:T(2,128)S(1)} %get-tuple-element.42), channel_id=1, source_target_pairs={{1,2},{3,4},{5,6},{7,8},{9,10},{11,12},{13,14},{17,18},{19,20},{21... | collective-permute-start | bytes 968 | tf_op jit(solution)/shard_map/ppermute | solution.py:51
  4.1 1.5 %collective-permute-done.1.far_list.refs_3_ = s32[2,40]{1,0:T(2,128)S(1)} collective-permute-done((s32[2,40]{1,0:T(2,128)S(1)}, s32[2,40]{1,0:T(2,128)S(1)}, u32[]{:S(2)}, u32[]{:S(2)}) %collective-permute-start.1) | collective-permute-done | bytes 352 | tf_op jit(solution)/shard_map/ppermute | solution.py:51
  5.6 0.6 %pack.1 = (bf16[32,8,8,128]{3,2,1,0:T(8,128)(2,1)S(1)}, bf16[32,8,8,128]{3,2,1,0:T(8,128)(2,1)S(1)}) custom-call(bf16[128,8,8,128]{3,2,1,0:T(8,128)(2,1)S(1)} %get-tuple-element.40.pool_ref, s32[2,40]{1,0:T(2,128)S(1)} %collective-permute-done.near_list.refs_2_, s32[2,40]{1,0:T(2,128)S(1)} %collective-permute-done.1.far_list.refs_3_), custom_call_target="tpu_custom_call" | custom-call | tf_op jit(solution)/shard_map/pack/pallas_call | solution.py:443
  6.2 1.5 %collective-permute-start.3 = (bf16[32,8,8,128]{3,2,1,0:T(8,128)(2,1)S(1)}, bf16[32,8,8,128]{3,2,1,0:T(8,128)(2,1)S(1)}, u32[]{:S(2)}, u32[]{:S(2)}) collective-permute-start(bf16[32,8,8,128]{3,2,1,0:T(8,128)(2,1)S(1)} %get-tuple-element.44), channel_id=1, source_target_pairs={{1,2},{3,4},{5,6},{7,8},{9,10},{11,12},{13,14},{17,18},{19,20},{21... | collective-permute-start | bytes 1572872 | tf_op jit(solution)/shard_map/ppermute | solution.py:51
  7.8 0.9 %collective-permute-start.2 = (bf16[32,8,8,128]{3,2,1,0:T(8,128)(2,1)S(1)}, bf16[32,8,8,128]{3,2,1,0:T(8,128)(2,1)S(1)}, u32[]{:S(2)}, u32[]{:S(2)}) collective-permute-start(bf16[32,8,8,128]{3,2,1,0:T(8,128)(2,1)S(1)} %get-tuple-element.43._), channel_id=1, source_target_pairs={{0,1},{2,3},{4,5},{6,7},{8,9},{10,11},{12,13},{14,15},{16,17},{18,... | collective-permute-start | bytes 1572872 | tf_op jit(solution)/shard_map/ppermute | solution.py:51
  8.7 1.6 %collective-permute-start.5 = (bf16[3,16,8,128]{3,2,1,0:T(8,128)(2,1)S(1)}, bf16[3,16,8,128]{3,2,1,0:T(8,128)(2,1)S(1)}, u32[]{:S(2)}, u32[]{:S(2)}) collective-permute-start(bf16[3,16,8,128]{3,2,1,0:T(8,128)(2,1)S(1)} %get-tuple-element.46), channel_id=1, source_target_pairs={{1,2},{3,4},{5,6},{7,8},{9,10},{11,12},{13,14},{17,18},{19,20},{21... | collective-permute-start | bytes 294920 | tf_op jit(solution)/shard_map/ppermute | solution.py:51
  10.3 1.5 %weights.1 = (bf16[1536,256]{1,0:T(8,128)(2,1)S(1)}, bf16[1536,256]{1,0:T(8,128)(2,1)S(1)}, bf16[1536,256]{1,0:T(8,128)(2,1)S(1)}, bf16[1536,256]{1,0:T(8,128)(2,1)S(1)}) custom-call(bf16[3,3,256,128]{3,2,1,0:T(8,128)(2,1)} %merging_hbm.1, bf16[3,3,128,128]{3,2,1,0:T(8,128)(2,1)} %first_hbm.1, bf16[3,3,128,128]{3,2,1,0:T(8,128)(2,1)} %second_hbm.1, ...), custom_call_target="tpu_custom_call" | custom-call | tf_op jit(solution)/shard_map/weights/pallas_call | solution.py:453
  11.8 9.8 %collective-permute-done.5.far_ref = bf16[3,16,8,128]{3,2,1,0:T(8,128)(2,1)S(1)} collective-permute-done((bf16[3,16,8,128]{3,2,1,0:T(8,128)(2,1)S(1)}, bf16[3,16,8,128]{3,2,1,0:T(8,128)(2,1)S(1)}, u32[]{:S(2)}, u32[]{:S(2)}) %collective-permute-start.5) | collective-permute-done | bytes 98336 | tf_op jit(solution)/shard_map/ppermute | solution.py:51
  21.6 3.6 %features.2 = (f32[18,128,256]{2,1,0:T(8,128)S(1)}, bf16[3,16,8,128]{3,2,1,0:T(8,128)(2,1)S(1)}, bf16[3,16,8,128]{3,2,1,0:T(8,128)(2,1)S(1)}) custom-call(bf16[2,32,16,8,128]{4,3,2,1,0:T(8,128)(2,1)} %bitcast.4, bf16[3,16,8,128]{3,2,1,0:T(8,128)(2,1)S(1)} %collective-permute-done.4.near_ref, bf16[3,16,8,128]{3,2,1,0:T(8,128)(2,1)S(1)} %collective-permute-done.5.far_ref, ...), custom_call_target="tpu_custom_call" | custom-call | tf_op jit(solution)/shard_map/features/pallas_call | solution.py:478
  25.3 0.8 %assemble.2 = (bf16[32,16,8,128]{3,2,1,0:T(8,128)(2,1)S(1)}, bf16[6,16,8,128]{3,2,1,0:T(8,128)(2,1)S(1)}, bf16[6,16,8,128]{3,2,1,0:T(8,128)(2,1)S(1)}, bf16[128,8,8,128]{3,2,1,0:T(8,128)(2,1)S(1)}) custom-call(s32[2,64]{1,0:T(2,128)S(1)} %get-tuple-element.39.table_vmem, ...), custom_call_target="tpu_custom_call", output_to_operand_aliasing={{3}: (1, {})} | custom-call | tf_op jit(solution)/shard_map/assemble/pallas_call | solution.py:507
  26.1 2.5 %collective-permute-start.7 = (bf16[6,16,8,128]{3,2,1,0:T(8,128)(2,1)S(1)}, bf16[6,16,8,128]{3,2,1,0:T(8,128)(2,1)S(1)}, u32[]{:S(2)}, u32[]{:S(2)}) collective-permute-start(bf16[6,16,8,128]{3,2,1,0:T(8,128)(2,1)S(1)} %get-tuple-element.52), channel_id=1, source_target_pairs={{1,2},{3,4},{5,6},{7,8},{9,10},{11,12},{13,14},{17,18},{19,20},{21... | collective-permute-start | bytes 589832 | tf_op jit(solution)/shard_map/ppermute | solution.py:51
  28.7 4.7 %inner.2 = (bf16[32,16,8,128]{3,2,1,0:T(8,128)(2,1)S(1)}, bf16[128,8,8,128]{3,2,1,0:T(8,128)(2,1)S(1)}, bf16[2,2,128,384]{3,2,1,0:T(8,128)(2,1)S(1)}, bf16[2,2,128,384]{3,2,1,0:T(8,128)(2,1)S(1)}) custom-call(f32[18,128,256]{2,1,0:T(8,128)S(1)} %get-tuple-element.48._.part_ref, bf16[32,16,8,128]{3,2,1,0:T(8,128)(2,1)S(1)} %get-tuple-element.53.warped_ref, ...), custom_call_target="tpu_custom_call" | custom-call | tf_op jit(solution)/shard_map/inner/pallas_call | solution.py:523
  33.4 1.9 %border.2 = (bf16[32,16,8,128]{3,2,1,0:T(8,128)(2,1)S(1)}, bf16[128,8,8,128]{3,2,1,0:T(8,128)(2,1)S(1)}, bf16[32,8,8,128]{3,2,1,0:T(8,128)(2,1)S(1)}, bf16[32,8,8,128]{3,2,1,0:T(8,128)(2,1)S(1)}) custom-call(f32[18,128,256]{2,1,0:T(8,128)S(1)} %get-tuple-element.48._.part_ref, ...), custom_call_target="tpu_custom_call", output_to_operand_aliasing={{0}: (9, {}), {1}: (10, {})} | custom-call | tf_op jit(solution)/shard_map/border/pallas_call | solution.py:557
  35.3 0.1 collective-permute-start.8
  35.4 2.5 %collective-permute-start.9 = (bf16[32,8,8,128]{3,2,1,0:T(8,128)(2,1)S(1)}, bf16[32,8,8,128]{3,2,1,0:T(8,128)(2,1)S(1)}, u32[]{:S(2)}, u32[]{:S(2)}) collective-permute-start(bf16[32,8,8,128]{3,2,1,0:T(8,128)(2,1)S(1)} %get-tuple-element.65), channel_id=1, source_target_pairs={{1,2},{3,4},{5,6},{7,8},{9,10},{11,12},{13,14},{17,18},{19,20},{21... | collective-permute-start | bytes 1572872 | tf_op jit(solution)/shard_map/ppermute | solution.py:51
  37.9 3.9 %features.3 = (f32[18,128,256]{2,1,0:T(8,128)S(1)}, bf16[2,32,16,8,128]{4,3,2,1,0:T(8,128)(2,1)}) custom-call(bf16[2,32,16,8,128]{4,3,2,1,0:T(8,128)(2,1)} %bitcast.5, bf16[6,16,8,128]{3,2,1,0:T(8,128)(2,1)S(1)} %collective-permute-done.6.near_ref, bf16[6,16,8,128]{3,2,1,0:T(8,128)(2,1)S(1)} %collective-permute-done.7.far_ref, ...), custom_call_target="tpu_custom_call" | custom-call | tf_op jit(solution)/shard_map/features/pallas_call | solution.py:478
  41.8 7.9 %collective-permute-done.9.far_ref = bf16[32,8,8,128]{3,2,1,0:T(8,128)(2,1)S(1)} collective-permute-done((bf16[32,8,8,128]{3,2,1,0:T(8,128)(2,1)S(1)}, bf16[32,8,8,128]{3,2,1,0:T(8,128)(2,1)S(1)}, u32[]{:S(2)}, u32[]{:S(2)}) %collective-permute-start.9) | collective-permute-done | bytes 524320 | tf_op jit(solution)/shard_map/ppermute | solution.py:51
  49.7 0.8 %assemble.3 = (bf16[32,16,8,128]{3,2,1,0:T(8,128)(2,1)S(1)}, bf16[3,16,8,128]{3,2,1,0:T(8,128)(2,1)S(1)}, bf16[3,16,8,128]{3,2,1,0:T(8,128)(2,1)S(1)}, bf16[128,8,8,128]{3,2,1,0:T(8,128)(2,1)S(1)}) custom-call(s32[2,64]{1,0:T(2,128)S(1)} %get-tuple-element.39.table_vmem, ...), custom_call_target="tpu_custom_call", output_to_operand_aliasing={{3}: (1, {})} | custom-call | tf_op jit(solution)/shard_map/assemble/pallas_call | solution.py:507
  50.5 0.1 collective-permute-start.10
  50.6 2.5 %collective-permute-start.11 = (bf16[3,16,8,128]{3,2,1,0:T(8,128)(2,1)S(1)}, bf16[3,16,8,128]{3,2,1,0:T(8,128)(2,1)S(1)}, u32[]{:S(2)}, u32[]{:S(2)}) collective-permute-start(bf16[3,16,8,128]{3,2,1,0:T(8,128)(2,1)S(1)} %get-tuple-element.68), channel_id=1, source_target_pairs={{1,2},{3,4},{5,6},{7,8},{9,10},{11,12},{13,14},{17,18},{19,20},{21... | collective-permute-start | bytes 294920 | tf_op jit(solution)/shard_map/ppermute | solution.py:51
  53.1 4.8 %inner.3 = (bf16[32,16,8,128]{3,2,1,0:T(8,128)(2,1)S(1)}, bf16[2,2,128,384]{3,2,1,0:T(8,128)(2,1)S(1)}, bf16[2,2,128,384]{3,2,1,0:T(8,128)(2,1)S(1)}) custom-call(f32[18,128,256]{2,1,0:T(8,128)S(1)} %get-tuple-element.62._.part_ref, bf16[32,16,8,128]{3,2,1,0:T(8,128)(2,1)S(1)} %get-tuple-element.66.warped_ref, ...), custom_call_target="tpu_custom_call" | custom-call | tf_op jit(solution)/shard_map/inner/pallas_call | solution.py:523
  57.9 2.5 %border.3 = bf16[2,32,16,8,128]{4,3,2,1,0:T(8,128)(2,1)} custom-call(f32[18,128,256]{2,1,0:T(8,128)S(1)} %get-tuple-element.62._.part_ref, bf16[32,16,8,128]{3,2,1,0:T(8,128)(2,1)S(1)} %get-tuple-element.66.warped_ref, bf16[3,16,8,128]{3,2,1,0:T(8,128)(2,1)S(1)} %collective-permute-done.10.near_ref, ...), custom_call_target="tpu_custom_call", output_to_operand_aliasing={{}: (10, {})} | custom-call | tf_op jit(solution)/shard_map/border/pallas_call | solution.py:546
  (11 shorter events, 0.1 us)
Async XLA Ops:
  1.3 2.8 %collective-permute-start = (s32[2,40]{1,0:T(2,128)S(1)}, s32[2,40]{1,0:T(2,128)S(1)}, u32[]{:S(2)}, u32[]{:S(2)}) collective-permute-start(s32[2,40]{1,0:T(2,128)S(1)} %get-tuple-element.41), channel_id=1, source_target_pairs={{0,1},{2,3},{4,5},{6,7},{8,9},{10,11},{12,13},{14,15},{16,17},{18,... | collective-permute-start | bytes 968 | tf_op jit(solution)/shard_map/ppermute | solution.py:51
  1.4 4.2 %collective-permute-start.1 = (s32[2,40]{1,0:T(2,128)S(1)}, s32[2,40]{1,0:T(2,128)S(1)}, u32[]{:S(2)}, u32[]{:S(2)}) collective-permute-start(s32[2,40]{1,0:T(2,128)S(1)} %get-tuple-element.42), channel_id=1, source_target_pairs={{1,2},{3,4},{5,6},{7,8},{9,10},{11,12},{13,14},{17,18},{19,20},{21... | collective-permute-start | bytes 968 | tf_op jit(solution)/shard_map/ppermute | solution.py:51
  6.2 19.0 %collective-permute-start.3 = (bf16[32,8,8,128]{3,2,1,0:T(8,128)(2,1)S(1)}, bf16[32,8,8,128]{3,2,1,0:T(8,128)(2,1)S(1)}, u32[]{:S(2)}, u32[]{:S(2)}) collective-permute-start(bf16[32,8,8,128]{3,2,1,0:T(8,128)(2,1)S(1)} %get-tuple-element.44), channel_id=1, source_target_pairs={{1,2},{3,4},{5,6},{7,8},{9,10},{11,12},{13,14},{17,18},{19,20},{21... | collective-permute-start | bytes 1572872 | tf_op jit(solution)/shard_map/ppermute | solution.py:51
  7.8 17.5 %collective-permute-start.2 = (bf16[32,8,8,128]{3,2,1,0:T(8,128)(2,1)S(1)}, bf16[32,8,8,128]{3,2,1,0:T(8,128)(2,1)S(1)}, u32[]{:S(2)}, u32[]{:S(2)}) collective-permute-start(bf16[32,8,8,128]{3,2,1,0:T(8,128)(2,1)S(1)} %get-tuple-element.43._), channel_id=1, source_target_pairs={{0,1},{2,3},{4,5},{6,7},{8,9},{10,11},{12,13},{14,15},{16,17},{18,... | collective-permute-start | bytes 1572872 | tf_op jit(solution)/shard_map/ppermute | solution.py:51
  8.7 3.1 %collective-permute-start.4 = (bf16[3,16,8,128]{3,2,1,0:T(8,128)(2,1)S(1)}, bf16[3,16,8,128]{3,2,1,0:T(8,128)(2,1)S(1)}, u32[]{:S(2)}, u32[]{:S(2)}) collective-permute-start(bf16[3,16,8,128]{3,2,1,0:T(8,128)(2,1)S(1)} %get-tuple-element.45), channel_id=1, source_target_pairs={{0,1},{2,3},{4,5},{6,7},{8,9},{10,11},{12,13},{14,15},{16,17},{18,... | collective-permute-start | bytes 294920 | tf_op jit(solution)/shard_map/ppermute | solution.py:51
  8.7 12.9 %collective-permute-start.5 = (bf16[3,16,8,128]{3,2,1,0:T(8,128)(2,1)S(1)}, bf16[3,16,8,128]{3,2,1,0:T(8,128)(2,1)S(1)}, u32[]{:S(2)}, u32[]{:S(2)}) collective-permute-start(bf16[3,16,8,128]{3,2,1,0:T(8,128)(2,1)S(1)} %get-tuple-element.46), channel_id=1, source_target_pairs={{1,2},{3,4},{5,6},{7,8},{9,10},{11,12},{13,14},{17,18},{19,20},{21... | collective-permute-start | bytes 294920 | tf_op jit(solution)/shard_map/ppermute | solution.py:51
  26.1 7.3 %collective-permute-start.6 = (bf16[6,16,8,128]{3,2,1,0:T(8,128)(2,1)S(1)}, bf16[6,16,8,128]{3,2,1,0:T(8,128)(2,1)S(1)}, u32[]{:S(2)}, u32[]{:S(2)}) collective-permute-start(bf16[6,16,8,128]{3,2,1,0:T(8,128)(2,1)S(1)} %get-tuple-element.51), channel_id=1, source_target_pairs={{0,1},{2,3},{4,5},{6,7},{8,9},{10,11},{12,13},{14,15},{16,17},{18,... | collective-permute-start | bytes 589832 | tf_op jit(solution)/shard_map/ppermute | solution.py:51
  26.1 7.3 %collective-permute-start.7 = (bf16[6,16,8,128]{3,2,1,0:T(8,128)(2,1)S(1)}, bf16[6,16,8,128]{3,2,1,0:T(8,128)(2,1)S(1)}, u32[]{:S(2)}, u32[]{:S(2)}) collective-permute-start(bf16[6,16,8,128]{3,2,1,0:T(8,128)(2,1)S(1)} %get-tuple-element.52), channel_id=1, source_target_pairs={{1,2},{3,4},{5,6},{7,8},{9,10},{11,12},{13,14},{17,18},{19,20},{21... | collective-permute-start | bytes 589832 | tf_op jit(solution)/shard_map/ppermute | solution.py:51
  35.3 6.5 %collective-permute-start.8 = (bf16[32,8,8,128]{3,2,1,0:T(8,128)(2,1)S(1)}, bf16[32,8,8,128]{3,2,1,0:T(8,128)(2,1)S(1)}, u32[]{:S(2)}, u32[]{:S(2)}) collective-permute-start(bf16[32,8,8,128]{3,2,1,0:T(8,128)(2,1)S(1)} %get-tuple-element.64), channel_id=1, source_target_pairs={{0,1},{2,3},{4,5},{6,7},{8,9},{10,11},{12,13},{14,15},{16,17},{18,... | collective-permute-start | bytes 1572872 | tf_op jit(solution)/shard_map/ppermute | solution.py:51
  35.4 14.3 %collective-permute-start.9 = (bf16[32,8,8,128]{3,2,1,0:T(8,128)(2,1)S(1)}, bf16[32,8,8,128]{3,2,1,0:T(8,128)(2,1)S(1)}, u32[]{:S(2)}, u32[]{:S(2)}) collective-permute-start(bf16[32,8,8,128]{3,2,1,0:T(8,128)(2,1)S(1)} %get-tuple-element.65), channel_id=1, source_target_pairs={{1,2},{3,4},{5,6},{7,8},{9,10},{11,12},{13,14},{17,18},{19,20},{21... | collective-permute-start | bytes 1572872 | tf_op jit(solution)/shard_map/ppermute | solution.py:51
  50.5 7.5 %collective-permute-start.10 = (bf16[3,16,8,128]{3,2,1,0:T(8,128)(2,1)S(1)}, bf16[3,16,8,128]{3,2,1,0:T(8,128)(2,1)S(1)}, u32[]{:S(2)}, u32[]{:S(2)}) collective-permute-start(bf16[3,16,8,128]{3,2,1,0:T(8,128)(2,1)S(1)} %get-tuple-element.67), channel_id=1, source_target_pairs={{0,1},{2,3},{4,5},{6,7},{8,9},{10,11},{12,13},{14,15},{16,17},{18,... | collective-permute-start | bytes 294920 | tf_op jit(solution)/shard_map/ppermute | solution.py:51
  50.6 7.4 %collective-permute-start.11 = (bf16[3,16,8,128]{3,2,1,0:T(8,128)(2,1)S(1)}, bf16[3,16,8,128]{3,2,1,0:T(8,128)(2,1)S(1)}, u32[]{:S(2)}, u32[]{:S(2)}) collective-permute-start(bf16[3,16,8,128]{3,2,1,0:T(8,128)(2,1)S(1)} %get-tuple-element.68), channel_id=1, source_target_pairs={{1,2},{3,4},{5,6},{7,8},{9,10},{11,12},{13,14},{17,18},{19,20},{21... | collective-permute-start | bytes 294920 | tf_op jit(solution)/shard_map/ppermute | solution.py:51
